TPU v7x, 256 devices: a whole 4x4x8 slice. The times are simulated.
256 devices in a mesh: user: 16 (over y_hi, x, core), item: 16 (over y_lo, z).
Axes of the slice: x: 4, y: 4 (y_hi: 2, y_lo: 2; y = y_hi * 2 + y_lo), z: 8, core: 2. Of those that a mesh axis runs over, the one named last changes fastest.
Arguments:
- user_pred: bfloat16 [16384, 128], P('user'), may hold values from -1.75 to 1.75
- user_imp: bfloat16 [16384, 128], P('user'), may hold values from -1.75 to 1.75
- item_pred: bfloat16 [4096, 128], P('item'), may hold values from -1.75 to 1.75
- item_imp: bfloat16 [4096, 128], P('item'), may hold values from -1.75 to 1.75
- uno_user: int32 [16, 16, 64], P('user', 'item'), may hold values from 0 to 7
- uno_item: int32 [16, 16, 64], P('user', 'item'), may hold values from 0 to 1
- obs_user: int32 [16, 16, 16], P('user', 'item'), may hold values from 0 to 7
- obs_item: int32 [16, 16, 16], P('user', 'item'), may hold values from 0 to 1
- obs_count: int32 [16, 16, 16], P('user', 'item'), may hold values from 0 to 1
- obs_label: int32 [16, 16, 16, 128, 128], P('user', 'item'), may hold values from 0 to 2
- obs_prop: bfloat16 [16, 16, 16, 128, 128], P('user', 'item'), may hold values from 0.099609375 to 1
Outputs:
- user_pred_grad: float32 [16384, 128], P(('user', 'item'))
- user_imp_grad: float32 [16384, 128], P(('user', 'item'))
- item_pred_grad: float32 [4096, 128], P(('item', 'user'))
- item_imp_grad: float32 [4096, 128], P(('item', 'user'))
Inputs may be any that keep to these rules, and one draw needn't show every extreme that they name: `uno_item`: each device's unobserved slots come in equal groups, one group for each item shard in order. Each device's observed slots come in equal groups of 16 / number of item indices, one group for each item shard in order; only the first obs_count slots of a group hold tiles.
All inputs are finite; a program needn't handle non-finite values.
Results may differ from a plain program's by a relative error of at most 0.0027.
Values may be sent and summed in bfloat16 or wider, within the bound.
A program may use at most 64 MiB of HBM per device.

v0:
```python
import jax
import jax.numpy as jnp
from jax import lax
from jax.sharding import PartitionSpec as P

loss_weight = 0.015625


def shifted(x, axis, by):
    length = lax.axis_size(axis)
    return lax.ppermute(x, axis, [(i, (i + by) % length) for i in range(length)])


def product(form, first, second):
    return jnp.einsum(form, first, second, preferred_element_type=jnp.float32)


def segments(form, onehot, values):
    return jnp.einsum(form, onehot, values, precision=lax.Precision.HIGHEST)


def shards(
    user_pred,
    user_imp,
    item_pred,
    item_imp,
    uno_user,
    uno_item,
    obs_user,
    obs_item,
    obs_count,
    obs_label,
    obs_prop,
):
    item_ways = lax.axis_size("item")
    position = lax.axis_index("item")
    tile_size = obs_label.shape[-1]
    rank_size = user_pred.shape[1]
    user_rows = user_pred.shape[0]
    shard_rows = item_pred.shape[0]
    user_blocks = user_rows // tile_size
    item_blocks = shard_rows // tile_size
    own_pred = user_pred.reshape(user_blocks, tile_size, rank_size)
    own_imp = user_imp.reshape(user_blocks, tile_size, rank_size)
    uno_users = uno_user.reshape(item_ways, -1)
    uno_items = uno_item.reshape(item_ways, -1)
    obs_users = obs_user.reshape(item_ways, -1)
    obs_items = obs_item.reshape(item_ways, -1)
    counts = obs_count.reshape(item_ways)
    labels = obs_label.reshape(item_ways, -1, tile_size, tile_size)
    propens = obs_prop.reshape(item_ways, -1, tile_size, tile_size)
    obs_slots = obs_users.shape[1]
    user_range = jnp.arange(user_blocks, dtype=jnp.int32)[:, None]
    item_range = jnp.arange(item_blocks, dtype=jnp.int32)[:, None]

    def select_row(table, shard):
        return lax.dynamic_index_in_dim(table, shard, 0, keepdims=False)

    def shard_terms(piece, shard):
        blocks = piece.reshape(2, item_blocks, tile_size, rank_size)
        user_ids = select_row(uno_users, shard)
        item_ids = select_row(uno_items, shard)
        user_tiles = own_pred[user_ids]
        item_tiles = blocks[0][item_ids]
        logits = product("tar,tbr->tab", user_tiles, item_tiles)
        imputed = product("tar,tbr->tab", own_imp[user_ids], blocks[1][item_ids])
        grads = ((jax.nn.sigmoid(logits) - jax.nn.sigmoid(imputed)) * loss_weight).astype(
            jnp.bfloat16
        )
        user_delta = product("tab,tbr->tar", grads, item_tiles)
        item_delta = product("tab,tar->tbr", grads, user_tiles)
        ouser_ids = select_row(obs_users, shard)
        oitem_ids = select_row(obs_items, shard)
        ou_tiles = own_pred[ouser_ids]
        ox_tiles = own_imp[ouser_ids]
        ov_tiles = blocks[0][oitem_ids]
        oy_tiles = blocks[1][oitem_ids]
        ologits = product("tar,tbr->tab", ou_tiles, ov_tiles)
        oimputed = product("tar,tbr->tab", ox_tiles, oy_tiles)
        predicted = jax.nn.sigmoid(ologits)
        imputes = jax.nn.sigmoid(oimputed)
        valid = (jnp.arange(obs_slots, dtype=jnp.int32) < select_row(counts, shard)).astype(
            jnp.float32
        )[:, None, None]
        state_tile = select_row(labels, shard)
        seen = (state_tile > 0).astype(jnp.float32)
        clicks = (state_tile == 2).astype(jnp.float32)
        weight = valid * seen / select_row(propens, shard).astype(jnp.float32)
        ograds = (
            (valid * (predicted - imputes) + weight * (imputes - clicks)) * loss_weight
        ).astype(jnp.bfloat16)
        ohgrads = (
            2.0
            * weight
            * (imputes - clicks)
            * ologits
            * ologits
            * imputes
            * (1.0 - imputes)
            * loss_weight
        ).astype(jnp.bfloat16)
        user_onehot = (user_ids[None, :] == user_range).astype(jnp.float32)
        ouser_onehot = (ouser_ids[None, :] == user_range).astype(jnp.float32)
        item_onehot = (item_ids[None, :] == item_range).astype(jnp.float32)
        oitem_onehot = (oitem_ids[None, :] == item_range).astype(jnp.float32)
        user_pred_term = segments("kt,tar->kar", user_onehot, user_delta) + segments(
            "kt,tar->kar", ouser_onehot, product("tab,tbr->tar", ograds, ov_tiles)
        )
        user_imp_term = segments(
            "kt,tar->kar", ouser_onehot, product("tab,tbr->tar", ohgrads, oy_tiles)
        )
        item_pred_term = segments("kt,tbr->kbr", item_onehot, item_delta) + segments(
            "kt,tbr->kbr", oitem_onehot, product("tab,tar->tbr", ograds, ou_tiles)
        )
        item_imp_term = segments(
            "kt,tbr->kbr", oitem_onehot, product("tab,tar->tbr", ohgrads, ox_tiles)
        )
        user_term = jnp.stack([user_pred_term, user_imp_term]).reshape(2, user_rows, rank_size)
        item_term = jnp.stack([item_pred_term, item_imp_term]).reshape(2, shard_rows, rank_size)
        return (user_term, item_term)

    def add_items(item_acc, item_term, shard):
        begin = shard * shard_rows
        current = lax.dynamic_slice_in_dim(item_acc, begin, shard_rows, 1)
        return lax.dynamic_update_slice_in_dim(item_acc, current + item_term, begin, 1)

    def advance(cycle_step, carried_state):
        piece, user_acc, item_acc = carried_state
        shard = (position - cycle_step) % item_ways
        user_term, item_term = shard_terms(piece, shard)
        item_acc = add_items(item_acc, item_term, shard)
        piece = shifted(piece, "item", 1)
        return (piece, user_acc + user_term, item_acc)

    start_piece = jnp.stack([item_pred, item_imp])
    user_zeros = jnp.zeros((2, user_rows, rank_size), jnp.float32)
    item_zeros = jnp.zeros((2, shard_rows * item_ways, rank_size), jnp.float32)
    final_state = lax.fori_loop(0, item_ways - 1, advance, (start_piece, user_zeros, item_zeros))
    piece, user_acc, item_acc = final_state
    shard = (position - (item_ways - 1)) % item_ways
    user_term, item_term = shard_terms(piece, shard)
    item_acc = add_items(item_acc, item_term, shard)
    user_acc, item_acc = (user_acc + user_term, item_acc)
    user_share = lax.psum_scatter(user_acc, "item", scatter_dimension=1, tiled=True)
    item_acc = lax.psum_scatter(item_acc, "item", scatter_dimension=1, tiled=True)
    item_share = lax.psum_scatter(item_acc, "user", scatter_dimension=1, tiled=True)
    return (user_share[0], user_share[1], item_share[0], item_share[1])


def solution(mesh):
    in_specs = (
        P("user", None),
        P("user", None),
        P("item", None),
        P("item", None),
        P("user", "item", None),
        P("user", "item", None),
        P("user", "item", None),
        P("user", "item", None),
        P("user", "item", None),
        P("user", "item", None, None, None),
        P("user", "item", None, None, None),
    )
    out_specs = (
        P(("user", "item"), None),
        P(("user", "item"), None),
        P(("item", "user"), None),
        P(("item", "user"), None),
    )
    return jax.shard_map(shards, mesh=mesh, in_specs=in_specs, out_specs=out_specs, check_vma=False)
```

profile of v0, /device:TPU:1, one launch (start us, length us, event | category | flops | bytes accessed | tf_op | source)
XLA Modules:
  0.0 533.7 jit_solution(15174572185034874242)
XLA Ops:
  7.8 1.3 reduce.6
  9.2 1.3 reduce.7
  10.6 1.3 constant_dynamic-slice_fusion.4
  14.5 1.3 fusion.128
  15.8 1.5 gather_fusion.4
  17.4 1.5 gather_fusion.6
  19.8 2.2 broadcast_in_dim.63
  22.1 269.1 %while.29 = (s32[]{:T(128)}, bf16[2,256,128]{2,1,0:T(8,128)(2,1)S(1)}, f32[2,1024,128]{2,1,0:T(8,128)S(1)}, f32[2,4096,128]{2,1,0:T(8,128)}, s32[]{:T(128)}, /*i...) while((s32[]{:T(128)}, ...), condition=%wide.region_1.2_spmd.clone.clone, body=%wide.region_0.1_spmd.clone.clone.sunk | while | flops 102697064 | bytes 14265322 | solution.py:138
  22.1 2.5 collective-permute-start
  32.7 1.1 fusion.218
  33.8 0.9 fusion.219
  39.5 1.7 fusion.230
  41.2 1.7 collective-permute-start
  51.0 1.1 fusion.218
  52.1 0.9 fusion.219
  57.8 1.7 fusion.230
  59.5 1.7 collective-permute-start
  69.3 1.1 fusion.218
  70.4 0.9 fusion.219
  76.1 1.7 fusion.230
  77.8 2.9 collective-permute-start
  88.9 1.1 fusion.218
  89.9 0.9 fusion.219
  95.6 1.7 fusion.230
  106.3 1.1 fusion.218
  107.3 0.9 fusion.219
  113.1 1.7 fusion.230
  123.7 1.1 fusion.218
  124.8 0.9 fusion.219
  130.5 1.7 fusion.230
  141.1 1.1 fusion.218
  142.2 0.9 fusion.219
  147.9 1.7 fusion.230
  157.8 1.1 fusion.218
  158.9 0.9 fusion.219
  164.6 1.7 fusion.230
  174.5 1.1 fusion.218
  175.6 0.9 fusion.219
  181.3 1.7 fusion.230
  183.1 1.4 collective-permute-start
  192.5 1.1 fusion.218
  193.6 0.9 fusion.219
  199.3 1.7 fusion.230
  201.0 1.7 collective-permute-start
  210.9 1.1 fusion.218
  211.9 0.9 fusion.219
  217.6 1.7 fusion.230
  219.4 2.9 collective-permute-start
  230.4 1.1 fusion.218
  237.2 1.7 fusion.230
  247.8 1.1 fusion.218
  254.6 1.7 fusion.230
  265.2 1.1 fusion.218
  272.0 1.7 fusion.230
  282.6 1.1 fusion.218
  289.4 1.7 fusion.230
  294.4 1.1 fusion.86
  298.9 1.7 fusion.77
  302.8 1.1 maximum_add_fusion.2
  303.9 70.2 %reduce-scatter.6.cloned.1.call-done = f32[2,256,128]{2,1,0:T(8,128)} async-done(((f32[2,4096,128]{2,1,0:T(8,128)}), f32[2,256,128]{2,1,0:T(8,128)}) %reduce-scatter.6.cloned.1.call-update) | async-done | bytes 262160 | tf_op jit(solution)/shard_map/reduce_scatter | solution.py:145
  374.1 69.4 %reduce-scatter.4.cloned.1.call-done = f32[2,64,128]{2,1,0:T(8,128)} async-done(((f32[2,1024,128]{2,1,0:T(8,128)}), f32[2,64,128]{2,1,0:T(8,128)}) %reduce-scatter.4.cloned.1.call-update) | async-done | bytes 65552 | tf_op jit(solution)/shard_map/reduce_scatter | solution.py:144
  443.6 1.4 slice_bitcast_fusion
  445.0 80.9 %reduce-scatter.8.cloned.1.call-done = f32[2,16,128]{2,1,0:T(8,128)} async-done(((f32[2,256,128]{2,1,0:T(8,128)}), f32[2,16,128]{2,1,0:T(8,128)}) %reduce-scatter.8.cloned.1.call-update) | async-done | bytes 16400 | tf_op jit(solution)/shard_map/reduce_scatter | solution.py:146
  525.8 1.3 slice_bitcast_fusion.2
  (556 shorter events, 143.1 us)
Async XLA Ops:
  7.2 14.9 %copy-start.2 = (s32[1,1,16]{2,1,0:T(1,128)S(1)}, s32[1,1,16]{2,1,0:T(1,128)}, u32[]{:S(2)}) copy-start(s32[1,1,16]{2,1,0:T(1,128)} %param.19) | copy-start | bytes 196
  7.2 14.9 %copy-start.3 = (s32[1,1,16]{2,1,0:T(1,128)S(1)}, s32[1,1,16]{2,1,0:T(1,128)}, u32[]{:S(2)}) copy-start(s32[1,1,16]{2,1,0:T(1,128)} %param.20) | copy-start | bytes 196
  7.2 14.9 %copy-start.4 = (s32[1,1,16]{2,1,0:T(1,128)S(1)}, s32[1,1,16]{2,1,0:T(1,128)}, u32[]{:S(2)}) copy-start(s32[1,1,16]{2,1,0:T(1,128)} %param.21) | copy-start | bytes 196
  7.2 14.8 %copy-start = (bf16[1024,128]{1,0:T(8,128)(2,1)S(1)}, bf16[1024,128]{1,0:T(8,128)(2,1)}, u32[]{:S(2)}) copy-start(bf16[1024,128]{1,0:T(8,128)(2,1)} %param.13) | copy-start | bytes 786436
  7.2 14.8 %copy-start.1 = (bf16[1024,128]{1,0:T(8,128)(2,1)S(1)}, bf16[1024,128]{1,0:T(8,128)(2,1)}, u32[]{:S(2)}) copy-start(bf16[1024,128]{1,0:T(8,128)(2,1)} %param.14) | copy-start | bytes 786436
  7.2 366.9 %reduce-scatter.6.cloned.1.call-start = ((), (), s32[]{:S(2)}) async-start(), calls=%async_computation.4 | async-start | bytes 4456448 | tf_op jit(solution)/shard_map/reduce_scatter | solution.py:145
  22.1 19.1 %collective-permute-start = (bf16[2,256,128]{2,1,0:T(8,128)(2,1)S(1)}, bf16[2,256,128]{2,1,0:T(8,128)(2,1)S(1)}, u32[]{:S(2)}, u32[]{:S(2)}) collective-permute-start(bf16[2,256,128]{2,1,0:T(8,128)(2,1)S(1)} %copy.53), channel_id=1, source_target_pairs={{0,1},{1,2},{2,3},{3,4},{4,5},{5,6},{6,7},{7,8},{8,9},{9,10},{10,1... | collective-permute-start | bytes 393224 | tf_op jit(solution)/shard_map/while/body/eval_jaxpr/ppermute | solution.py:11
  41.2 18.3 %collective-permute-start = (bf16[2,256,128]{2,1,0:T(8,128)(2,1)S(1)}, bf16[2,256,128]{2,1,0:T(8,128)(2,1)S(1)}, u32[]{:S(2)}, u32[]{:S(2)}) collective-permute-start(bf16[2,256,128]{2,1,0:T(8,128)(2,1)S(1)} %copy.53), channel_id=1, source_target_pairs={{0,1},{1,2},{2,3},{3,4},{4,5},{5,6},{6,7},{7,8},{8,9},{9,10},{10,1... | collective-permute-start | bytes 393224 | tf_op jit(solution)/shard_map/while/body/eval_jaxpr/ppermute | solution.py:11
  59.5 18.3 %collective-permute-start = (bf16[2,256,128]{2,1,0:T(8,128)(2,1)S(1)}, bf16[2,256,128]{2,1,0:T(8,128)(2,1)S(1)}, u32[]{:S(2)}, u32[]{:S(2)}) collective-permute-start(bf16[2,256,128]{2,1,0:T(8,128)(2,1)S(1)} %copy.53), channel_id=1, source_target_pairs={{0,1},{1,2},{2,3},{3,4},{4,5},{5,6},{6,7},{7,8},{8,9},{9,10},{10,1... | collective-permute-start | bytes 393224 | tf_op jit(solution)/shard_map/while/body/eval_jaxpr/ppermute | solution.py:11
  77.8 19.5 %collective-permute-start = (bf16[2,256,128]{2,1,0:T(8,128)(2,1)S(1)}, bf16[2,256,128]{2,1,0:T(8,128)(2,1)S(1)}, u32[]{:S(2)}, u32[]{:S(2)}) collective-permute-start(bf16[2,256,128]{2,1,0:T(8,128)(2,1)S(1)} %copy.53), channel_id=1, source_target_pairs={{0,1},{1,2},{2,3},{3,4},{4,5},{5,6},{6,7},{7,8},{8,9},{9,10},{10,1... | collective-permute-start | bytes 393224 | tf_op jit(solution)/shard_map/while/body/eval_jaxpr/ppermute | solution.py:11
  97.4 17.4 %collective-permute-start = (bf16[2,256,128]{2,1,0:T(8,128)(2,1)S(1)}, bf16[2,256,128]{2,1,0:T(8,128)(2,1)S(1)}, u32[]{:S(2)}, u32[]{:S(2)}) collective-permute-start(bf16[2,256,128]{2,1,0:T(8,128)(2,1)S(1)} %copy.53), channel_id=1, source_target_pairs={{0,1},{1,2},{2,3},{3,4},{4,5},{5,6},{6,7},{7,8},{8,9},{9,10},{10,1... | collective-permute-start | bytes 393224 | tf_op jit(solution)/shard_map/while/body/eval_jaxpr/ppermute | solution.py:11
  114.8 17.4 %collective-permute-start = (bf16[2,256,128]{2,1,0:T(8,128)(2,1)S(1)}, bf16[2,256,128]{2,1,0:T(8,128)(2,1)S(1)}, u32[]{:S(2)}, u32[]{:S(2)}) collective-permute-start(bf16[2,256,128]{2,1,0:T(8,128)(2,1)S(1)} %copy.53), channel_id=1, source_target_pairs={{0,1},{1,2},{2,3},{3,4},{4,5},{5,6},{6,7},{7,8},{8,9},{9,10},{10,1... | collective-permute-start | bytes 393224 | tf_op jit(solution)/shard_map/while/body/eval_jaxpr/ppermute | solution.py:11
  132.2 17.4 %collective-permute-start = (bf16[2,256,128]{2,1,0:T(8,128)(2,1)S(1)}, bf16[2,256,128]{2,1,0:T(8,128)(2,1)S(1)}, u32[]{:S(2)}, u32[]{:S(2)}) collective-permute-start(bf16[2,256,128]{2,1,0:T(8,128)(2,1)S(1)} %copy.53), channel_id=1, source_target_pairs={{0,1},{1,2},{2,3},{3,4},{4,5},{5,6},{6,7},{7,8},{8,9},{9,10},{10,1... | collective-permute-start | bytes 393224 | tf_op jit(solution)/shard_map/while/body/eval_jaxpr/ppermute | solution.py:11
  149.6 16.7 %collective-permute-start = (bf16[2,256,128]{2,1,0:T(8,128)(2,1)S(1)}, bf16[2,256,128]{2,1,0:T(8,128)(2,1)S(1)}, u32[]{:S(2)}, u32[]{:S(2)}) collective-permute-start(bf16[2,256,128]{2,1,0:T(8,128)(2,1)S(1)} %copy.53), channel_id=1, source_target_pairs={{0,1},{1,2},{2,3},{3,4},{4,5},{5,6},{6,7},{7,8},{8,9},{9,10},{10,1... | collective-permute-start | bytes 393224 | tf_op jit(solution)/shard_map/while/body/eval_jaxpr/ppermute | solution.py:11
  166.4 16.7 %collective-permute-start = (bf16[2,256,128]{2,1,0:T(8,128)(2,1)S(1)}, bf16[2,256,128]{2,1,0:T(8,128)(2,1)S(1)}, u32[]{:S(2)}, u32[]{:S(2)}) collective-permute-start(bf16[2,256,128]{2,1,0:T(8,128)(2,1)S(1)} %copy.53), channel_id=1, source_target_pairs={{0,1},{1,2},{2,3},{3,4},{4,5},{5,6},{6,7},{7,8},{8,9},{9,10},{10,1... | collective-permute-start | bytes 393224 | tf_op jit(solution)/shard_map/while/body/eval_jaxpr/ppermute | solution.py:11
  183.1 18.0 %collective-permute-start = (bf16[2,256,128]{2,1,0:T(8,128)(2,1)S(1)}, bf16[2,256,128]{2,1,0:T(8,128)(2,1)S(1)}, u32[]{:S(2)}, u32[]{:S(2)}) collective-permute-start(bf16[2,256,128]{2,1,0:T(8,128)(2,1)S(1)} %copy.53), channel_id=1, source_target_pairs={{0,1},{1,2},{2,3},{3,4},{4,5},{5,6},{6,7},{7,8},{8,9},{9,10},{10,1... | collective-permute-start | bytes 393224 | tf_op jit(solution)/shard_map/while/body/eval_jaxpr/ppermute | solution.py:11
  201.0 18.3 %collective-permute-start = (bf16[2,256,128]{2,1,0:T(8,128)(2,1)S(1)}, bf16[2,256,128]{2,1,0:T(8,128)(2,1)S(1)}, u32[]{:S(2)}, u32[]{:S(2)}) collective-permute-start(bf16[2,256,128]{2,1,0:T(8,128)(2,1)S(1)} %copy.53), channel_id=1, source_target_pairs={{0,1},{1,2},{2,3},{3,4},{4,5},{5,6},{6,7},{7,8},{8,9},{9,10},{10,1... | collective-permute-start | bytes 393224 | tf_op jit(solution)/shard_map/while/body/eval_jaxpr/ppermute | solution.py:11
  219.4 19.5 %collective-permute-start = (bf16[2,256,128]{2,1,0:T(8,128)(2,1)S(1)}, bf16[2,256,128]{2,1,0:T(8,128)(2,1)S(1)}, u32[]{:S(2)}, u32[]{:S(2)}) collective-permute-start(bf16[2,256,128]{2,1,0:T(8,128)(2,1)S(1)} %copy.53), channel_id=1, source_target_pairs={{0,1},{1,2},{2,3},{3,4},{4,5},{5,6},{6,7},{7,8},{8,9},{9,10},{10,1... | collective-permute-start | bytes 393224 | tf_op jit(solution)/shard_map/while/body/eval_jaxpr/ppermute | solution.py:11
  238.9 17.4 %collective-permute-start = (bf16[2,256,128]{2,1,0:T(8,128)(2,1)S(1)}, bf16[2,256,128]{2,1,0:T(8,128)(2,1)S(1)}, u32[]{:S(2)}, u32[]{:S(2)}) collective-permute-start(bf16[2,256,128]{2,1,0:T(8,128)(2,1)S(1)} %copy.53), channel_id=1, source_target_pairs={{0,1},{1,2},{2,3},{3,4},{4,5},{5,6},{6,7},{7,8},{8,9},{9,10},{10,1... | collective-permute-start | bytes 393224 | tf_op jit(solution)/shard_map/while/body/eval_jaxpr/ppermute | solution.py:11
  256.3 17.4 %collective-permute-start = (bf16[2,256,128]{2,1,0:T(8,128)(2,1)S(1)}, bf16[2,256,128]{2,1,0:T(8,128)(2,1)S(1)}, u32[]{:S(2)}, u32[]{:S(2)}) collective-permute-start(bf16[2,256,128]{2,1,0:T(8,128)(2,1)S(1)} %copy.53), channel_id=1, source_target_pairs={{0,1},{1,2},{2,3},{3,4},{4,5},{5,6},{6,7},{7,8},{8,9},{9,10},{10,1... | collective-permute-start | bytes 393224 | tf_op jit(solution)/shard_map/while/body/eval_jaxpr/ppermute | solution.py:11
  273.8 17.4 %collective-permute-start = (bf16[2,256,128]{2,1,0:T(8,128)(2,1)S(1)}, bf16[2,256,128]{2,1,0:T(8,128)(2,1)S(1)}, u32[]{:S(2)}, u32[]{:S(2)}) collective-permute-start(bf16[2,256,128]{2,1,0:T(8,128)(2,1)S(1)} %copy.53), channel_id=1, source_target_pairs={{0,1},{1,2},{2,3},{3,4},{4,5},{5,6},{6,7},{7,8},{8,9},{9,10},{10,1... | collective-permute-start | bytes 393224 | tf_op jit(solution)/shard_map/while/body/eval_jaxpr/ppermute | solution.py:11
  300.6 142.9 %reduce-scatter.4.cloned.1.call-start = ((), (), s32[]{:S(2)}) async-start(), calls=%async_computation.3 | async-start | bytes 1114112 | tf_op jit(solution)/shard_map/reduce_scatter | solution.py:144
  303.9 222.0 %reduce-scatter.8.cloned.1.call-start = ((), (), s32[]{:S(2)}) async-start(), calls=%async_computation.5 | async-start | bytes 278528 | tf_op jit(solution)/shard_map/reduce_scatter | solution.py:146
Sparse Core Ops, SparseCore 0:
  300.7 73.3 reduce-scatter.5
  376.6 66.8 reduce-scatter.3
  448.1 77.6 reduce-scatter.7
where the time goes:
time: 538 us; the launch traced here: 534 us
  waiting for transfers between devices  221 us (41%)
  other arithmetic  76.2 us (14%)
  local copies, waits for them, and re-layouts  68.4 us (13%)
  loops' own time  67.7 us (13%)
  matrix products  62.2 us (12%)
  starting transfers between devices  20.1 us (4%)
  between operations  18.6 us (3%)
    reduce_scatter x1, waiting for transfers between devices, shards(): lax.psum_scatter(item_acc, 'user', scatter_dimension=1, tiled=True)  80.9 us
    reduce_scatter x1, waiting for transfers between devices, shards(): lax.psum_scatter(item_acc, 'item', scatter_dimension=1, tiled=True)  70.2 us
    reduce_scatter x1, waiting for transfers between devices, shards(): lax.psum_scatter(user_acc, 'item', scatter_dimension=1, tiled=True)  69.4 us
    another operation x1, loops' own time, shards(): lax.fori_loop(0, item_ways - 1, advance, (start_piece, user_zeros, item_z...  67.7 us
    dot_general x160, matrix products, product(): return jnp.einsum(form, first, second, preferred_element_type=jnp.float32)  43.9 us
    dynamic_update_slice x16, other arithmetic, add_items(): lax.dynamic_update_slice_in_dim(item_acc, current + item_term, begin, 1)  27.3 us
    ppermute x15, starting transfers between devices, shifted(): lax.ppermute(x, axis, [(i, (i + by) % length) for i in range(length)])  20 us
    dynamic_slice x31, local copies, waits for them, and re-layouts, select_row(): return lax.dynamic_index_in_dim(table, shard, 0, keepdims=False)  20 us
  transfers between devices with their start and end apart: 18, of which 3 were waited for; matrix products, arithmetic and copies ran while one was open for 35% of the time, Pallas kernels for 0%

commit v1 on v0

v1 whole, which is shorter than its diff:
```python
import jax
import jax.numpy as jnp
from jax import lax
from jax.sharding import PartitionSpec as P

loss_weight = 0.015625
META_ROWS = 8


def product(form, first, second):
    return jnp.einsum(form, first, second, preferred_element_type=jnp.float32)


def split_product(form, wide, narrow):
    hi = wide.astype(jnp.bfloat16)
    lo = (wide - hi.astype(jnp.float32)).astype(jnp.bfloat16)
    return product(form, hi, narrow) + product(form, lo, narrow)


def shards(
    user_pred,
    user_imp,
    item_pred,
    item_imp,
    uno_user,
    uno_item,
    obs_user,
    obs_item,
    obs_count,
    obs_label,
    obs_prop,
):
    item_ways = lax.axis_size("item")
    user_ways = lax.axis_size("user")
    tile = obs_label.shape[-1]
    rank = user_pred.shape[1]
    user_rows = user_pred.shape[0]
    shard_rows = item_pred.shape[0]
    user_blocks = user_rows // tile
    item_blocks = shard_rows // tile
    n_blocks = user_blocks * item_blocks
    obs_slots = obs_user.shape[-1] // item_ways

    uno_pos = (uno_user * item_blocks + uno_item).reshape(item_ways, -1)
    uno_counts = jnp.sum(
        (uno_pos[:, :, None] == jnp.arange(n_blocks, dtype=jnp.int32)).astype(jnp.float32), axis=1
    )
    obs_pos = (obs_user * item_blocks + obs_item).reshape(item_ways, obs_slots)
    place = jnp.arange(obs_slots, dtype=jnp.int32)
    valid = (place[None, :] < obs_count.reshape(item_ways, 1)).astype(jnp.float32)
    meta = jnp.zeros((item_ways, META_ROWS, tile), jnp.float32)
    meta = meta.at[:, 0, :n_blocks].set(uno_counts)
    meta = meta.at[:, 1, :obs_slots].set(obs_pos.astype(jnp.float32))
    meta = meta.at[:, 2, :obs_slots].set(valid)
    labels = obs_label.reshape(item_ways, obs_slots * tile, tile).astype(jnp.bfloat16)
    propens = obs_prop.reshape(item_ways, obs_slots * tile, tile)
    package = jnp.concatenate([labels, propens, meta.astype(jnp.bfloat16)], axis=1)
    got = lax.all_to_all(package, "item", 0, 0, tiled=True)
    got_labels = got[:, : obs_slots * tile].reshape(item_ways * obs_slots, tile, tile)
    got_props = got[:, obs_slots * tile : 2 * obs_slots * tile].reshape(item_ways * obs_slots, tile, tile)
    got_meta = got[:, 2 * obs_slots * tile :].astype(jnp.float32)
    counts = jnp.sum(got_meta[:, 0, :n_blocks], axis=0)
    tile_pos = got_meta[:, 1, :obs_slots].reshape(-1).astype(jnp.int32)
    tile_valid = got_meta[:, 2, :obs_slots].reshape(-1)

    logits = product("ar,br->ab", user_pred, item_pred)
    imputed = product("ar,br->ab", user_imp, item_imp)

    def blocked(x):
        return x.reshape(user_blocks, tile, item_blocks, tile).transpose(0, 2, 1, 3).reshape(n_blocks, tile, tile)

    def unblocked(x):
        return x.reshape(user_blocks, item_blocks, tile, tile).transpose(0, 2, 1, 3).reshape(user_rows, shard_rows)

    logit_blocks = blocked(logits)
    imputed_blocks = blocked(imputed)
    uno_grads = ((jax.nn.sigmoid(logit_blocks) - jax.nn.sigmoid(imputed_blocks)) * loss_weight).astype(jnp.bfloat16)

    ologits = logit_blocks[tile_pos]
    predicted = jax.nn.sigmoid(ologits)
    imputes = jax.nn.sigmoid(imputed_blocks[tile_pos])
    tvalid = tile_valid[:, None, None]
    seen = (got_labels > 0).astype(jnp.float32)
    clicks = (got_labels == 2).astype(jnp.float32)
    weight = tvalid * seen / got_props.astype(jnp.float32)
    ograds = ((tvalid * (predicted - imputes) + weight * (imputes - clicks)) * loss_weight).astype(jnp.bfloat16)
    ohgrads = (
        2.0 * weight * (imputes - clicks) * ologits * ologits * imputes * (1.0 - imputes) * loss_weight
    ).astype(jnp.bfloat16)
    onehot = (tile_pos[:, None] == jnp.arange(n_blocks, dtype=jnp.int32)[None, :]).astype(jnp.bfloat16)
    grad_blocks = counts[:, None, None] * uno_grads.astype(jnp.float32) + product("tk,tab->kab", onehot, ograds)
    hgrad_blocks = product("tk,tab->kab", onehot, ohgrads)
    grad_full = unblocked(grad_blocks)
    hgrad_full = unblocked(hgrad_blocks)

    user_part = jnp.stack(
        [split_product("ab,br->ar", grad_full, item_pred), split_product("ab,br->ar", hgrad_full, item_imp)]
    )
    item_part = jnp.stack(
        [split_product("ab,ar->br", grad_full, user_pred), split_product("ab,ar->br", hgrad_full, user_imp)]
    )

    user_chunks = user_part.reshape(2, item_ways, user_rows // item_ways, rank).transpose(1, 0, 2, 3)
    user_got = lax.all_to_all(user_chunks, "item", 0, 0, tiled=True)
    user_share = jnp.sum(user_got, axis=0)
    item_chunks = item_part.reshape(2, user_ways, shard_rows // user_ways, rank).transpose(1, 0, 2, 3)
    item_got = lax.all_to_all(item_chunks, "user", 0, 0, tiled=True)
    item_share = jnp.sum(item_got, axis=0)
    return (user_share[0], user_share[1], item_share[0], item_share[1])


def solution(mesh):
    in_specs = (
        P("user", None),
        P("user", None),
        P("item", None),
        P("item", None),
        P("user", "item", None),
        P("user", "item", None),
        P("user", "item", None),
        P("user", "item", None),
        P("user", "item", None),
        P("user", "item", None, None, None),
        P("user", "item", None, None, None),
    )
    out_specs = (
        P(("user", "item"), None),
        P(("user", "item"), None),
        P(("item", "user"), None),
        P(("item", "user"), None),
    )
    return jax.shard_map(shards, mesh=mesh, in_specs=in_specs, out_specs=out_specs, check_vma=False)
```

time: 538 us -> 107 us (0.20)
  waiting for transfers between devices: 221 us -> 50 us
  other arithmetic: 76.2 us -> 7.85 us
  loops' own time: 67.7 us -> 0 us
  local copies, waits for them, and re-layouts: 68.4 us -> 13.7 us
  matrix products: 62.2 us -> 10.5 us
  between operations: 18.6 us -> 0.97 us
    reduce_scatter x3 -> x0, waiting for transfers between devices: 221 us -> none  [the longest x1 80.9 us: shards(): lax.psum_scatter(item_acc, 'user', scatter_dimension=1, tiled=True)]
    another operation x1 -> x0, loops' own time: 67.7 us -> none  [shards(): lax.fori_loop(0, item_ways - 1, advance, (start_piece, user_zeros, item_z...]
    all_to_all x0 -> x3, waiting for transfers between devices: none -> 50 us  [the longest x1 24.1 us: shards(): user_got = lax.all_to_all(user_chunks, 'item', 0, 0, tiled=True)]
    gather x64 -> x2, local copies, waits for them, and re-layouts: 38.5 us -> 2.2 us  [the longest x1 1.59 us: shards(): ologits = logit_blocks[tile_pos]]
    dot_general x160 -> x12, matrix products: 43.9 us -> 10.5 us  [product(): return jnp.einsum(form, first, second, preferred_element_type=jnp.float32)]
    dynamic_update_slice x16 -> x0, other arithmetic: 27.3 us -> none  [add_items(): lax.dynamic_update_slice_in_dim(item_acc, current + item_term, begin, 1)]
    all_to_all x0 -> x3, starting transfers between devices: none -> 23 us  [the longest x1 10.3 us: shards(): got = lax.all_to_all(package, 'item', 0, 0, tiled=True)]
    another operation x33 -> x0, other arithmetic: 20.7 us -> none
  transfers between devices with their start and end apart: 18 -> 3, of which waited for: 3 -> 3; matrix products, arithmetic and copies ran while one was open for 35% -> 8% of each run, Pallas kernels for 0% -> 0%
where the time goes in v1:
time: 107 us; the launch traced here: 106 us
  waiting for transfers between devices  50 us (47%)
  starting transfers between devices  23 us (21%)
  local copies, waits for them, and re-layouts  13.7 us (13%)
  matrix products  10.5 us (10%)
  other arithmetic  7.85 us (7%)
    all_to_all x1, waiting for transfers between devices, shards(): user_got = lax.all_to_all(user_chunks, 'item', 0, 0, tiled=True)  24.1 us
    all_to_all x1, waiting for transfers between devices, shards(): got = lax.all_to_all(package, 'item', 0, 0, tiled=True)  19 us
    dot_general x12, matrix products, product(): return jnp.einsum(form, first, second, preferred_element_type=jnp.float32)  10.5 us
    all_to_all x1, starting transfers between devices, shards(): got = lax.all_to_all(package, 'item', 0, 0, tiled=True)  10.3 us
    all_to_all x1, starting transfers between devices, shards(): item_got = lax.all_to_all(item_chunks, 'user', 0, 0, tiled=True)  9.04 us
    all_to_all x1, waiting for transfers between devices, shards(): item_got = lax.all_to_all(item_chunks, 'user', 0, 0, tiled=True)  6.98 us
    all_to_all x1, starting transfers between devices, shards(): user_got = lax.all_to_all(user_chunks, 'item', 0, 0, tiled=True)  3.65 us
    unnamed x28, local copies, waits for them, and re-layouts  3.4 us
  transfers between devices with their start and end apart: 3, of which 3 were waited for; matrix products, arithmetic and copies ran while one was open for 8% of the time, Pallas kernels for 0%

profile of v1, /device:TPU:1, one launch (start us, length us, event | category | flops | bytes accessed | tf_op | source)
XLA Modules:
  0.0 106.0 jit_solution(16804017538367890530)
XLA Ops:
  0.6 0.0 copy-start
  0.6 0.0 copy-start.12
  0.7 0.7 fusion.27
  1.4 0.1 copy.55
  1.5 0.7 convert_bitcast_fusion.1
  2.2 0.1 copy.54
  2.3 0.7 add_reduce_fusion
  3.0 0.1 eq.34
  3.0 0.1 copy.53
  3.1 0.1 convert_reduce_fusion
  3.4 1.3 %convert_bitcast_fusion = bf16[16,128,128]{2,1,0:T(8,128)(2,1)S(1)} fusion(s32[1,1,16,128,128]{4,3,2,1,0:T(8,128)} %param.26), kind=kLoop, calls=%fused_computation.28 | loop fusion | flops 262144 | bytes 1572864 | tf_op jit(solution)/shard_map/convert_element_type | solution.py:55
  4.7 0.0 copy-done.12
  4.7 1.1 pad_maximum_fusion
  5.8 10.3 %all-to-all-start = ((bf16[16,264,128]{2,1,0:T(8,128)(2,1)}), bf16[16,264,128]{2,1,0:T(8,128)(2,1)S(1)}, u32[]{:S(2)}, u32[]{:S(2)}) async-start(bf16[16,264,128]{2,1,0:T(8,128)(2,1)} %pad_maximum_fusion), calls=%async_computation | async-start | bytes 2162688 | tf_op jit(solution)/shard_map/all_to_all | solution.py:58
  16.0 0.0 copy-done
  16.0 0.0 copy-done.9
  16.1 0.3 fusion.39
  16.3 0.5 reshape.218
  16.9 0.4 copy.57
  17.3 0.0 copy-start.6
  17.3 0.0 copy-start.10
  17.3 1.0 copy-done.1
  18.3 0.3 copy.59
  18.6 0.0 copy-done.6
  18.6 0.0 copy-done.10
  18.6 1.3 %fusion.40 = f32[1024,256]{1,0:T(8,128)} fusion(bf16[1024,128]{1,0:T(8,128)(2,1)S(1)} %copy-done.6, bf16[256,128]{1,0:T(8,128)(2,1)S(1)} %copy-done.10), kind=kOutput, calls=%fused_computation.69 | convolution fusion | flops 67108864 | bytes 1376256 | tf_op jit(solution)/shard_map/ar,br->ab/dot_general | solution.py:11
  19.9 1.7 %reshape.220 = f32[8,128,2,128]{3,2,1,0:T(2,128)S(1)} reshape(f32[1024,256]{1,0:T(8,128)} %fusion.40) | data formatting | bytes 2097152 | tf_op jit(solution)/shard_map/reshape | solution.py:70
  21.7 0.4 copy.58
  22.0 1.0 copy-done.3
  23.0 0.3 copy.61
  23.4 19.0 %all-to-all-done = bf16[16,264,128]{2,1,0:T(8,128)(2,1)S(1)} async-done(((bf16[16,264,128]{2,1,0:T(8,128)(2,1)}), bf16[16,264,128]{2,1,0:T(8,128)(2,1)S(1)}, u32[]{:S(2)}, u32[]{:S(2)}) %all-to-all-start) | async-done | bytes 1081376 | tf_op jit(solution)/shard_map/all_to_all | solution.py:58
  42.3 0.4 fusion.21
  42.7 0.2 slice_reduce_fusion
  43.0 1.6 %gather_fusion = f32[16,128,128]{2,1,0:T(8,128)} fusion(f32[16,128,128]{2,1,0:T(8,128)S(1)} %copy.59, s32[1024]{0:T(1024)S(1)} %pad_clamp_fusion), kind=kCustom, calls=%fused_computation | custom fusion | bytes 2097216 | tf_op jit(solution)/shard_map/gather | solution.py:79
  44.6 0.6 gather_fusion.1
  45.2 0.1 fusion.38
  45.3 1.1 %copy-done.5 = f32[16,128,128]{2,1,0:T(8,128)S(1)} copy-done((f32[16,128,128]{2,1,0:T(8,128)S(1)}, f32[16,128,128]{2,1,0:T(8,128)}, u32[]{:S(2)}) %copy-start.5) | copy-done | bytes 1048600
  46.4 3.1 %fusion.9 = f32[16,128,128]{2,0,1:T(8,128)} fusion(f32[16,128,128]{2,1,0:T(8,128)S(1)} %copy-done.5, f32[16,128,128]{2,1,0:T(8,128)S(1)} %gather_fusion.1, bf16[16,128,128]{2,1,0:T(8,128)(2,1)S(1)} %get-tuple-element.41, s32[16]{0:T(128)S(1)} %fusion.21, bf16[16,128,128]{2,1,0:T(8,128)(2,1)S(1)} %get-tuple-element.40, f32[16]{0:T(128)S(1)} %slice_reduce_fusion), kind=kOutput, calls=%fused_computation.29 | convolution fusion | flops 14156032 | bytes 4194432 | tf_op jit(solution)/shard_map/tk,tab->kab/dot_general | solution.py:11
  49.5 2.5 %convolution_add_fusion = f32[16,128,128]{2,0,1:T(8,128)S(1)} fusion(f32[16]{0:T(128)S(1)} %slice_reduce_fusion.1, f32[16,128,128]{2,0,1:T(8,128)S(1)} %bitcast.101, f32[16,128,128]{2,0,1:T(8,128)S(1)} %bitcast.99, f32[16,128,128]{2,1,0:T(8,128)S(1)} %copy-done.5, f32[16]{0:T(128)S(1)} %slice_reduce_fusion, f32[16,128,128]{2,1,0:T(8,128)S(1)} %gather_fusion.1, ...), kind=kOutput, calls=%fused_computation.3 | convolution fusion | flops 17301760 | bytes 6291648 | tf_op jit(solution)/shard_map/tk,tab->kab/dot_general | solution.py:11
  52.0 0.7 copy.65
  52.7 1.0 fusion.11
  53.7 0.4 fusion.12
  54.0 0.0 copy-start.7
  54.1 0.0 copy-start.11
  54.1 1.7 %copy.68 = f32[8,2,128,128]{2,0,3,1:T(8,128)S(1)} copy(f32[8,2,128,128]{3,1,0,2:T(2,128)} %bitcast.106) | data formatting | bytes 2097152 | tf_op jit(solution)/shard_map/reshape | solution.py:73
  55.8 0.3 fusion.13
  56.2 0.0 copy-start.8
  56.2 0.4 fusion.14
  56.5 0.2 copy-done.13
  56.7 0.3 convolution_add_fusion.4
  57.0 0.1 copy-done.8
  57.1 0.3 convolution_add_fusion.3
  57.4 0.7 maximum_bitcast_fusion.1
  58.2 9.0 %all-to-all-start.2 = ((f32[16,2,16,128]{3,2,1,0:T(8,128)}), f32[16,2,16,128]{3,2,1,0:T(8,128)}, u32[]{:S(2)}, u32[]{:S(2)}) async-start(f32[16,2,16,128]{3,2,1,0:T(8,128)} %maximum_bitcast_fusion.1), calls=%async_computation.2 | async-start | bytes 524288 | tf_op jit(solution)/shard_map/all_to_all | solution.py:107
  67.2 0.4 convolution_add_fusion.2
  67.6 0.4 convolution_add_fusion.1
  67.9 1.1 %maximum_bitcast_fusion = f32[16,2,64,128]{3,2,1,0:T(8,128)} fusion(f32[1,16,64,128]{3,2,0,1:T(8,128)S(1)} %bitcast.105, f32[1,16,64,128]{3,2,0,1:T(8,128)S(1)} %bitcast.104), kind=kLoop, calls=%fused_computation.19 | loop fusion | flops 262144 | bytes 2097152 | tf_op jit(solution)/shard_map/transpose | solution.py:103
  69.0 7.0 %all-to-all-done.2 = f32[16,2,16,128]{3,2,1,0:T(8,128)} async-done(((f32[16,2,16,128]{3,2,1,0:T(8,128)}), f32[16,2,16,128]{3,2,1,0:T(8,128)}, u32[]{:S(2)}, u32[]{:S(2)}) %all-to-all-start.2) | async-done | bytes 262176 | tf_op jit(solution)/shard_map/all_to_all | solution.py:107
  76.0 3.7 %all-to-all-start.1 = ((f32[16,2,64,128]{3,2,1,0:T(8,128)}), f32[16,2,64,128]{3,2,1,0:T(8,128)S(1)}, u32[]{:S(2)}, u32[]{:S(2)}) async-start(f32[16,2,64,128]{3,2,1,0:T(8,128)} %maximum_bitcast_fusion), calls=%async_computation.1 | async-start | bytes 2097152 | tf_op jit(solution)/shard_map/all_to_all | solution.py:104
  79.7 1.0 reduce_sum.39
  80.6 0.6 slice_bitcast_fusion.2
  81.2 24.1 %all-to-all-done.1 = f32[16,2,64,128]{3,2,1,0:T(8,128)S(1)} async-done(((f32[16,2,64,128]{3,2,1,0:T(8,128)}), f32[16,2,64,128]{3,2,1,0:T(8,128)S(1)}, u32[]{:S(2)}, u32[]{:S(2)}) %all-to-all-start.1) | async-done | bytes 1048608 | tf_op jit(solution)/shard_map/all_to_all | solution.py:104
  105.3 0.1 reduce_sum.38
  105.4 0.6 slice_bitcast_fusion
  (19 shorter events, 0.2 us)
Async XLA Ops:
  0.6 15.4 %copy-start = (bf16[1024,128]{1,0:T(8,128)(2,1)S(1)}, bf16[1024,128]{1,0:T(8,128)(2,1)}, u32[]{:S(2)}) copy-start(bf16[1024,128]{1,0:T(8,128)(2,1)} %param.17) | copy-start | bytes 786436
  0.6 4.0 %copy-start.12 = (bf16[1,1,16,128,128]{4,3,2,1,0:T(8,128)(2,1)S(1)}, bf16[1,1,16,128,128]{4,3,2,1,0:T(8,128)(2,1)}, u32[]{:S(2)}) copy-start(bf16[1,1,16,128,128]{4,3,2,1,0:T(8,128)(2,1)} %param.27) | copy-start | bytes 1572868
  5.8 10.3 %copy-start.9 = (bf16[256,128]{1,0:T(8,128)(2,1)S(1)}, bf16[256,128]{1,0:T(8,128)(2,1)}, u32[]{:S(2)}) copy-start(bf16[256,128]{1,0:T(8,128)(2,1)} %param.19) | copy-start | bytes 196612
  5.8 36.6 %all-to-all-start = ((bf16[16,264,128]{2,1,0:T(8,128)(2,1)}), bf16[16,264,128]{2,1,0:T(8,128)(2,1)S(1)}, u32[]{:S(2)}, u32[]{:S(2)}) async-start(bf16[16,264,128]{2,1,0:T(8,128)(2,1)} %pad_maximum_fusion), calls=%async_computation | async-start | bytes 2162688 | tf_op jit(solution)/shard_map/all_to_all | solution.py:58
  17.3 1.0 copy-start.1
  17.3 1.3 %copy-start.6 = (bf16[1024,128]{1,0:T(8,128)(2,1)S(1)}, bf16[1024,128]{1,0:T(8,128)(2,1)}, u32[]{:S(2)}) copy-start(bf16[1024,128]{1,0:T(8,128)(2,1)} %param.18) | copy-start | bytes 786436
  17.3 1.3 %copy-start.10 = (bf16[256,128]{1,0:T(8,128)(2,1)S(1)}, bf16[256,128]{1,0:T(8,128)(2,1)}, u32[]{:S(2)}) copy-start(bf16[256,128]{1,0:T(8,128)(2,1)} %param.20) | copy-start | bytes 196612
  22.0 1.0 copy-start.3
  45.2 1.2 %copy-start.5 = (f32[16,128,128]{2,1,0:T(8,128)S(1)}, f32[16,128,128]{2,1,0:T(8,128)}, u32[]{:S(2)}) copy-start(f32[16,128,128]{2,1,0:T(8,128)} %gather_fusion) | copy-start | bytes 3145732
  46.4 3.1 %copy-start.2 = (f32[8,2,128,128]{3,1,0,2:T(2,128)S(1)}, f32[8,2,128,128]{3,1,0,2:T(2,128)}, u32[]{:S(2)}) copy-start(f32[8,2,128,128]{3,1,0,2:T(2,128)} %copy-done.1) | copy-start | bytes 3145732
  46.4 3.1 %copy-start.4 = (f32[8,2,128,128]{3,1,0,2:T(2,128)S(1)}, f32[8,2,128,128]{3,1,0,2:T(2,128)}, u32[]{:S(2)}) copy-start(f32[8,2,128,128]{3,1,0,2:T(2,128)} %copy-done.3) | copy-start | bytes 3145732
  54.0 1.8 %copy-start.7 = (bf16[1024,128]{1,0:T(8,128)(2,1)S(1)}, bf16[1024,128]{1,0:T(8,128)(2,1)}, u32[]{:S(2)}) copy-start(bf16[1024,128]{1,0:T(8,128)(2,1)} %param.18) | copy-start | bytes 786436
  54.1 2.1 %copy-start.11 = (bf16[256,128]{1,0:T(8,128)(2,1)S(1)}, bf16[256,128]{1,0:T(8,128)(2,1)}, u32[]{:S(2)}) copy-start(bf16[256,128]{1,0:T(8,128)(2,1)} %param.20) | copy-start | bytes 196612
  55.8 0.9 copy-start.13
  56.2 1.0 copy-start.8
  58.2 17.8 %all-to-all-start.2 = ((f32[16,2,16,128]{3,2,1,0:T(8,128)}), f32[16,2,16,128]{3,2,1,0:T(8,128)}, u32[]{:S(2)}, u32[]{:S(2)}) async-start(f32[16,2,16,128]{3,2,1,0:T(8,128)} %maximum_bitcast_fusion.1), calls=%async_computation.2 | async-start | bytes 524288 | tf_op jit(solution)/shard_map/all_to_all | solution.py:107
  76.0 29.3 %all-to-all-start.1 = ((f32[16,2,64,128]{3,2,1,0:T(8,128)}), f32[16,2,64,128]{3,2,1,0:T(8,128)S(1)}, u32[]{:S(2)}, u32[]{:S(2)}) async-start(f32[16,2,64,128]{3,2,1,0:T(8,128)} %maximum_bitcast_fusion), calls=%async_computation.1 | async-start | bytes 2097152 | tf_op jit(solution)/shard_map/all_to_all | solution.py:104

commit v2 on v1

--- a/solution.py
+++ b/solution.py
@@ -1,7 +1,13 @@
+import functools
+
 import jax
 import jax.numpy as jnp
 from jax import lax
+from jax.experimental import pallas as pl
+from jax.experimental.pallas import tpu as pltpu
 from jax.sharding import PartitionSpec as P
+
+MESH = pl.DeviceIdType.MESH
 
 loss_weight = 0.015625
 META_ROWS = 8
@@ -9,6 +15,48 @@
 
 def product(form, first, second):
     return jnp.einsum(form, first, second, preferred_element_type=jnp.float32)
+
+
+def exchange_kernel(axis, n, x_ref, y_ref, send_sem, recv_sem, local_sem):
+    me = lax.axis_index(axis)
+    barrier = pltpu.get_barrier_semaphore()
+    for k in range(1, n):
+        pl.semaphore_signal(barrier, inc=1, device_id={axis: lax.rem(me + k, n)}, device_id_type=MESH)
+    pl.semaphore_wait(barrier, n - 1)
+    local = pltpu.make_async_copy(x_ref.at[me], y_ref.at[me], local_sem)
+    local.start()
+    copies = []
+    for k in range(1, n):
+        peer = lax.rem(me + k, n)
+        copy = pltpu.make_async_remote_copy(
+            src_ref=x_ref.at[peer],
+            dst_ref=y_ref.at[me],
+            send_sem=send_sem.at[k],
+            recv_sem=recv_sem.at[k],
+            device_id={axis: peer},
+            device_id_type=MESH,
+        )
+        copy.start()
+        copies.append(copy)
+    for copy in copies:
+        copy.wait()
+    local.wait()
+
+
+def exchange(x, axis, collective):
+    n = lax.axis_size(axis)
+    return pl.pallas_call(
+        functools.partial(exchange_kernel, axis, n),
+        out_shape=jax.ShapeDtypeStruct(x.shape, x.dtype),
+        in_specs=[pl.BlockSpec(memory_space=pl.ANY)],
+        out_specs=pl.BlockSpec(memory_space=pl.ANY),
+        scratch_shapes=[
+            pltpu.SemaphoreType.DMA((n,)),
+            pltpu.SemaphoreType.DMA((n,)),
+            pltpu.SemaphoreType.DMA(()),
+        ],
+        compiler_params=pltpu.CompilerParams(collective_id=collective, has_side_effects=True),
+    )(x)
 
 
 def split_product(form, wide, narrow):
@@ -55,7 +103,7 @@
     labels = obs_label.reshape(item_ways, obs_slots * tile, tile).astype(jnp.bfloat16)
     propens = obs_prop.reshape(item_ways, obs_slots * tile, tile)
     package = jnp.concatenate([labels, propens, meta.astype(jnp.bfloat16)], axis=1)
-    got = lax.all_to_all(package, "item", 0, 0, tiled=True)
+    got = exchange(package, "item", 0)
     got_labels = got[:, : obs_slots * tile].reshape(item_ways * obs_slots, tile, tile)
     got_props = got[:, obs_slots * tile : 2 * obs_slots * tile].reshape(item_ways * obs_slots, tile, tile)
     got_meta = got[:, 2 * obs_slots * tile :].astype(jnp.float32)
@@ -101,10 +149,10 @@
     )
 
     user_chunks = user_part.reshape(2, item_ways, user_rows // item_ways, rank).transpose(1, 0, 2, 3)
-    user_got = lax.all_to_all(user_chunks, "item", 0, 0, tiled=True)
+    user_got = exchange(user_chunks, "item", 1)
     user_share = jnp.sum(user_got, axis=0)
     item_chunks = item_part.reshape(2, user_ways, shard_rows // user_ways, rank).transpose(1, 0, 2, 3)
-    item_got = lax.all_to_all(item_chunks, "user", 0, 0, tiled=True)
+    item_got = exchange(item_chunks, "user", 2)
     item_share = jnp.sum(item_got, axis=0)
     return (user_share[0], user_share[1], item_share[0], item_share[1])
 

time: 107 us -> 103 us (0.963)
  Pallas kernels: 0 us -> 74.1 us
  waiting for transfers between devices: 50 us -> 0 us
  starting transfers between devices: 23 us -> 0 us
  other arithmetic: 7.85 us -> 14.1 us
  local copies, waits for them, and re-layouts: 13.7 us -> 8.24 us
  matrix products: 10.5 us -> 5.68 us
    pallas_call x0 -> x3, Pallas kernels: none -> 74.1 us  [exchange(): pl.pallas_call(functools.partial(exchange_kernel, axis, n), out_shape=jax...]
    all_to_all x3 -> x0, waiting for transfers between devices: 50 us -> none  [the longest x1 24.1 us: shards(): user_got = lax.all_to_all(user_chunks, 'item', 0, 0, tiled=True)]
    all_to_all x3 -> x0, starting transfers between devices: 23 us -> none  [the longest x1 10.3 us: shards(): got = lax.all_to_all(package, 'item', 0, 0, tiled=True)]
    dot_general x12, matrix products: 10.5 us -> 5.68 us  [product(): return jnp.einsum(form, first, second, preferred_element_type=jnp.float32)]
    convert_element_type x0 -> x1, other arithmetic: none -> 3.44 us  [shards(): ((tvalid * (predicted - imputes) + weight * (imputes - clicks)) * loss_we...]
    unnamed x28 -> x20, local copies, waits for them, and re-layouts: 3.4 us -> 0.52 us
    reshape x4, local copies, waits for them, and re-layouts: 2.96 us -> 1.29 us  [blocked(): x.reshape(user_blocks, tile, item_blocks, tile).transpose(0, 2, 1, 3)]
    reshape x2, local copies, waits for them, and re-layouts: 2.43 us -> 1.07 us  [unblocked(): x.reshape(user_blocks, item_blocks, tile, tile).transpose(0, 2, 1, 3)]
  transfers between devices with their start and end apart: 3 -> 0, of which waited for: 3 -> 0; matrix products, arithmetic and copies ran while one was open for 8% -> 0% of each run, Pallas kernels for 0% -> 0%
where the time goes in v2:
time: 103 us
  Pallas kernels  74.1 us (72%)
  other arithmetic  14.1 us (14%)
  local copies, waits for them, and re-layouts  8.24 us (8%)
  matrix products  5.68 us (6%)
    pallas_call x3, Pallas kernels, exchange(): pl.pallas_call(functools.partial(exchange_kernel, axis, n), out_shape=jax...  74.1 us
    dot_general x12, matrix products, product(): return jnp.einsum(form, first, second, preferred_element_type=jnp.float32)  5.68 us
    convert_element_type x1, other arithmetic, shards(): ((tvalid * (predicted - imputes) + weight * (imputes - clicks)) * loss_we...  3.44 us

profile of v2, /device:TPU:1, one launch (start us, length us, event | category | flops | bytes accessed | tf_op | source)
XLA Modules:
  0.0 103.0 jit_solution(15531087150551429417)
XLA Ops:
  0.6 0.0 copy-start
  0.6 0.0 copy-start.9
  0.7 0.8 add_reduce_fusion
  1.4 0.7 convert_bitcast_fusion.1
  2.1 0.7 fusion.24
  2.8 0.1 copy.33
  2.9 0.1 copy.32
  3.0 0.1 eq.34
  3.0 0.1 copy.31
  3.1 0.1 convert_reduce_fusion
  3.2 0.1 scatter.11
  3.4 0.1 scatter.14
  3.5 1.3 %convert_bitcast_fusion = bf16[16,128,128]{2,1,0:T(8,128)(2,1)S(1)} fusion(s32[1,1,16,128,128]{4,3,2,1,0:T(8,128)} %param.26), kind=kLoop, calls=%fused_computation.29 | loop fusion | flops 262144 | bytes 1572864 | tf_op jit(solution)/shard_map/convert_element_type | solution.py:103
  4.9 0.0 copy-done.9
  4.9 1.1 %pad_maximum_fusion.x_ref = bf16[16,264,128]{2,1,0:T(8,128)(2,1)} fusion(bf16[16,8,128]{2,1,0:T(8,128)(2,1)S(1)} %scatter.14, bf16[16,128,128]{2,1,0:T(8,128)(2,1)S(1)} %bitcast.102, bf16[16,128,128]{2,1,0:T(8,128)(2,1)S(1)} %convert_bitcast_fusion), kind=kLoop, calls=%fused_computation.7 | loop fusion | flops 3244032 | bytes 2162688 | tf_op jit(solution)/shard_map/concatenate | solution.py:105
  6.0 34.0 %shard_map.138 = bf16[16,264,128]{2,1,0:T(8,128)(2,1)} custom-call(bf16[16,264,128]{2,1,0:T(8,128)(2,1)} %pad_maximum_fusion.x_ref), custom_call_target="tpu_custom_call" | custom-call | tf_op jit(solution)/shard_map/pallas_call | solution.py:48
  40.0 0.8 slice_convert_fusion
  40.8 0.4 fusion.18
  41.2 0.2 slice_reduce_fusion
  41.4 0.0 copy-done
  41.4 0.0 copy-done.6
  41.4 0.3 fusion.26
  41.7 0.5 reshape.218
  42.3 0.1 copy.34
  42.4 0.0 copy-start.3
  42.4 0.0 copy-start.5
  42.4 1.6 %gather_fusion = f32[16,128,128]{2,1,0:T(8,128)} fusion(f32[16,128,128]{2,1,0:T(8,128)S(1)} %bitcast.94, s32[1024]{0:T(1024)S(1)} %pad_clamp_fusion), kind=kCustom, calls=%fused_computation | custom fusion | bytes 2097216 | tf_op jit(solution)/shard_map/gather | solution.py:127
  44.0 0.0 copy-done.3
  44.0 0.0 copy-done.5
  44.1 0.3 fusion.27
  44.4 0.5 reshape.220
  44.9 0.1 copy.35
  45.0 0.0 copy-start.1
  45.0 1.6 %gather_fusion.1 = f32[16,128,128]{2,1,0:T(8,128)} fusion(f32[16,128,128]{2,1,0:T(8,128)S(1)} %bitcast.95, s32[1024]{0:T(1024)S(1)} %pad_clamp_fusion), kind=kCustom, calls=%fused_computation.1 | custom fusion | bytes 2097216 | tf_op jit(solution)/shard_map/gather | solution.py:129
  46.6 0.0 copy-done.1
  46.6 3.4 %multiply_convert_fusion = (bf16[16,128,128]{2,1,0:T(8,128)(2,1)S(1)}, bf16[16,128,128]{2,1,0:T(8,128)(2,1)}) fusion(f32[16,128,128]{2,1,0:T(8,128)} %gather_fusion, f32[16]{0:T(128)S(1)} %slice_reduce_fusion, f32[16,128,128]{2,1,0:T(8,128)} %gather_fusion.1, bf16[16,264,128]{2,1,0:T(8,128)(2,1)S(1)} %copy-done.1), kind=kLoop, calls=%fused_computation.20 | loop fusion | flops 7340032 | bytes 4194368 | tf_op jit(solution)/shard_map/convert_element_type | solution.py:134
  50.1 0.4 fusion.8
  50.5 0.7 copy_add_fusion
  51.2 0.4 copy.38
  51.6 0.0 copy-start.2
  51.6 0.3 fusion.10
  51.9 1.0 convolution_add_fusion.3
  52.9 0.0 copy-done.2
  52.9 0.4 fusion.6
  53.3 0.7 copy.40
  54.0 0.0 copy-start.4
  54.0 0.0 copy-start.8
  54.0 1.3 %fusion.12 = f32[256,128]{1,0:T(8,128)S(1)} fusion(bf16[1024,128]{1,0:T(8,128)(2,1)} %param.18, f32[32,8,8,128]{3,2,1,0:T(8,128)S(1)} %bitcast.90), kind=kOutput, calls=%fused_computation.33 | convolution fusion | flops 67108864 | bytes 1441792 | tf_op jit(solution)/shard_map/ab,ar->br/dot_general | solution.py:17
  55.3 0.3 convolution_add_fusion.2
  55.6 0.0 copy-done.8
  55.6 0.7 maximum_bitcast_fusion.1.x_ref
  56.4 11.4 %shard_map.140 = f32[16,2,16,128]{3,2,1,0:T(8,128)} custom-call(f32[16,2,16,128]{3,2,1,0:T(8,128)} %maximum_bitcast_fusion.1.x_ref), custom_call_target="tpu_custom_call" | custom-call | tf_op jit(solution)/shard_map/pallas_call | solution.py:48
  67.7 1.0 reduce_sum.39
  68.7 0.6 slice_bitcast_fusion.2
  69.3 0.3 fusion.13
  69.7 0.0 copy-start.7
  69.7 0.4 convolution_add_fusion
  70.0 0.5 copy-done.7
  70.5 0.4 fusion.11
  70.9 0.4 convolution_add_fusion.1
  71.2 1.1 %maximum_bitcast_fusion.x_ref = f32[16,2,64,128]{3,2,1,0:T(8,128)} fusion(f32[1,16,64,128]{3,2,0,1:T(8,128)S(1)} %bitcast.98, f32[1,16,64,128]{3,2,0,1:T(8,128)S(1)} %bitcast.99), kind=kLoop, calls=%fused_computation.18 | loop fusion | flops 262144 | bytes 2097152 | tf_op jit(solution)/shard_map/transpose | solution.py:151
  72.3 28.7 %shard_map.139 = f32[16,2,64,128]{3,2,1,0:T(8,128)} custom-call(f32[16,2,64,128]{3,2,1,0:T(8,128)} %maximum_bitcast_fusion.x_ref), custom_call_target="tpu_custom_call" | custom-call | tf_op jit(solution)/shard_map/pallas_call | solution.py:48
  101.1 1.3 %reduce_sum.38 = f32[2,64,128]{2,1,0:T(8,128)S(1)} reduce(f32[16,2,64,128]{3,2,1,0:T(8,128)} %shard_map.139, f32[]{:T(128)} %constant.104.clone.1), dimensions={0}, to_apply=%region_2.0 | reduce | flops 245760 | bytes 1114116 | tf_op jit(solution)/shard_map/reduce_sum | solution.py:153
  102.4 0.6 slice_bitcast_fusion
  (6 shorter events, 0.1 us)
Async XLA Ops:
  0.6 40.8 %copy-start = (bf16[1024,128]{1,0:T(8,128)(2,1)S(1)}, bf16[1024,128]{1,0:T(8,128)(2,1)}, u32[]{:S(2)}) copy-start(bf16[1024,128]{1,0:T(8,128)(2,1)} %param.17) | copy-start | bytes 786436
  0.6 4.2 %copy-start.9 = (bf16[1,1,16,128,128]{4,3,2,1,0:T(8,128)(2,1)S(1)}, bf16[1,1,16,128,128]{4,3,2,1,0:T(8,128)(2,1)}, u32[]{:S(2)}) copy-start(bf16[1,1,16,128,128]{4,3,2,1,0:T(8,128)(2,1)} %param.27) | copy-start | bytes 1572868
  6.0 35.4 %copy-start.6 = (bf16[256,128]{1,0:T(8,128)(2,1)S(1)}, bf16[256,128]{1,0:T(8,128)(2,1)}, u32[]{:S(2)}) copy-start(bf16[256,128]{1,0:T(8,128)(2,1)} %param.19) | copy-start | bytes 196612
  42.4 1.7 %copy-start.3 = (bf16[1024,128]{1,0:T(8,128)(2,1)S(1)}, bf16[1024,128]{1,0:T(8,128)(2,1)}, u32[]{:S(2)}) copy-start(bf16[1024,128]{1,0:T(8,128)(2,1)} %param.18) | copy-start | bytes 786436
  42.4 1.7 %copy-start.5 = (bf16[256,128]{1,0:T(8,128)(2,1)S(1)}, bf16[256,128]{1,0:T(8,128)(2,1)}, u32[]{:S(2)}) copy-start(bf16[256,128]{1,0:T(8,128)(2,1)} %param.20) | copy-start | bytes 196612
  45.0 1.6 %copy-start.1 = (bf16[16,264,128]{2,1,0:T(8,128)(2,1)S(1)}, bf16[16,264,128]{2,1,0:T(8,128)(2,1)}, u32[]{:S(2)}) copy-start(bf16[16,264,128]{2,1,0:T(8,128)(2,1)} %shard_map.138) | copy-start | bytes 3244036
  51.6 1.3 %copy-start.2 = (bf16[16,128,128]{2,1,0:T(8,128)(2,1)S(1)}, bf16[16,128,128]{2,1,0:T(8,128)(2,1)}, u32[]{:S(2)}) copy-start(bf16[16,128,128]{2,1,0:T(8,128)(2,1)} %get-tuple-element.41) | copy-start | bytes 1572868
  54.0 1.3 %copy-start.4 = (bf16[1024,128]{1,0:T(8,128)(2,1)S(1)}, bf16[1024,128]{1,0:T(8,128)(2,1)}, u32[]{:S(2)}) copy-start(bf16[1024,128]{1,0:T(8,128)(2,1)} %param.18) | copy-start | bytes 786436
  54.0 1.6 %copy-start.8 = (f32[256,128]{1,0:T(8,128)S(1)}, f32[256,128]{1,0:T(8,128)}, u32[]{:S(2)}) copy-start(f32[256,128]{1,0:T(8,128)} %convolution_add_fusion.3) | copy-start | bytes 393220
  69.7 0.8 copy-start.7

commit v3 on v1

--- a/solution.py
+++ b/solution.py
@@ -1,7 +1,13 @@
+import functools
+
 import jax
 import jax.numpy as jnp
 from jax import lax
+from jax.experimental import pallas as pl
+from jax.experimental.pallas import tpu as pltpu
 from jax.sharding import PartitionSpec as P
+
+MESH = pl.DeviceIdType.MESH
 
 loss_weight = 0.015625
 META_ROWS = 8
@@ -9,6 +15,61 @@
 
 def product(form, first, second):
     return jnp.einsum(form, first, second, preferred_element_type=jnp.float32)
+
+
+def exchange_kernel(axes, *refs):
+    count = len(axes)
+    x_refs, y_refs = refs[:count], refs[count : 2 * count]
+    send_sem, recv_sem, local_sem = refs[2 * count :]
+    barrier = pltpu.get_barrier_semaphore()
+    for axis in axes:
+        n = lax.axis_size(axis)
+        me = lax.axis_index(axis)
+        for k in range(1, n):
+            pl.semaphore_signal(barrier, inc=1, device_id={axis: lax.rem(me + k, n)}, device_id_type=MESH)
+    pl.semaphore_wait(barrier, sum(lax.axis_size(axis) - 1 for axis in axes))
+    copies = []
+    slot = 0
+    for which, axis in enumerate(axes):
+        n = lax.axis_size(axis)
+        me = lax.axis_index(axis)
+        x_ref, y_ref = x_refs[which], y_refs[which]
+        local = pltpu.make_async_copy(x_ref.at[me], y_ref.at[me], local_sem.at[which])
+        local.start()
+        copies.append(local)
+        for k in range(1, n):
+            peer = lax.rem(me + k, n)
+            copy = pltpu.make_async_remote_copy(
+                src_ref=x_ref.at[peer],
+                dst_ref=y_ref.at[me],
+                send_sem=send_sem.at[slot],
+                recv_sem=recv_sem.at[slot],
+                device_id={axis: peer},
+                device_id_type=MESH,
+            )
+            copy.start()
+            copies.append(copy)
+            slot += 1
+    for copy in copies:
+        copy.wait()
+
+
+def exchange(pairs, collective):
+    axes = tuple(axis for _, axis in pairs)
+    arrays = [x for x, _ in pairs]
+    slots = sum(lax.axis_size(axis) - 1 for axis in axes)
+    return pl.pallas_call(
+        functools.partial(exchange_kernel, axes),
+        out_shape=[jax.ShapeDtypeStruct(x.shape, x.dtype) for x in arrays],
+        in_specs=[pl.BlockSpec(memory_space=pl.ANY)] * len(arrays),
+        out_specs=[pl.BlockSpec(memory_space=pl.ANY)] * len(arrays),
+        scratch_shapes=[
+            pltpu.SemaphoreType.DMA((slots,)),
+            pltpu.SemaphoreType.DMA((slots,)),
+            pltpu.SemaphoreType.DMA((len(arrays),)),
+        ],
+        compiler_params=pltpu.CompilerParams(collective_id=collective, has_side_effects=True),
+    )(*arrays)
 
 
 def split_product(form, wide, narrow):
@@ -55,7 +116,7 @@
     labels = obs_label.reshape(item_ways, obs_slots * tile, tile).astype(jnp.bfloat16)
     propens = obs_prop.reshape(item_ways, obs_slots * tile, tile)
     package = jnp.concatenate([labels, propens, meta.astype(jnp.bfloat16)], axis=1)
-    got = lax.all_to_all(package, "item", 0, 0, tiled=True)
+    (got,) = exchange([(package, "item")], 0)
     got_labels = got[:, : obs_slots * tile].reshape(item_ways * obs_slots, tile, tile)
     got_props = got[:, obs_slots * tile : 2 * obs_slots * tile].reshape(item_ways * obs_slots, tile, tile)
     got_meta = got[:, 2 * obs_slots * tile :].astype(jnp.float32)
@@ -101,10 +162,9 @@
     )
 
     user_chunks = user_part.reshape(2, item_ways, user_rows // item_ways, rank).transpose(1, 0, 2, 3)
-    user_got = lax.all_to_all(user_chunks, "item", 0, 0, tiled=True)
+    item_chunks = item_part.reshape(2, user_ways, shard_rows // user_ways, rank).transpose(1, 0, 2, 3)
+    user_got, item_got = exchange([(user_chunks, "item"), (item_chunks, "user")], 1)
     user_share = jnp.sum(user_got, axis=0)
-    item_chunks = item_part.reshape(2, user_ways, shard_rows // user_ways, rank).transpose(1, 0, 2, 3)
-    item_got = lax.all_to_all(item_chunks, "user", 0, 0, tiled=True)
     item_share = jnp.sum(item_got, axis=0)
     return (user_share[0], user_share[1], item_share[0], item_share[1])
 

time: 107 us -> 95 us (0.89)
  Pallas kernels: 0 us -> 66.6 us
  waiting for transfers between devices: 50 us -> 0 us
  starting transfers between devices: 23 us -> 0 us
  local copies, waits for them, and re-layouts: 13.7 us -> 8.24 us
  other arithmetic: 7.85 us -> 13.2 us
  matrix products: 10.5 us -> 5.66 us
    pallas_call x0 -> x2, Pallas kernels: none -> 66.6 us  [exchange(): pl.pallas_call(functools.partial(exchange_kernel, axes), out_shape=[jax.S...]
    all_to_all x3 -> x0, waiting for transfers between devices: 50 us -> none  [the longest x1 24.1 us: shards(): user_got = lax.all_to_all(user_chunks, 'item', 0, 0, tiled=True)]
    all_to_all x3 -> x0, starting transfers between devices: 23 us -> none  [the longest x1 10.3 us: shards(): got = lax.all_to_all(package, 'item', 0, 0, tiled=True)]
    dot_general x12, matrix products: 10.5 us -> 5.66 us  [product(): return jnp.einsum(form, first, second, preferred_element_type=jnp.float32)]
    convert_element_type x0 -> x1, other arithmetic: none -> 3.44 us  [shards(): ((tvalid * (predicted - imputes) + weight * (imputes - clicks)) * loss_we...]
    unnamed x28 -> x22, local copies, waits for them, and re-layouts: 3.4 us -> 0.53 us
    reshape x4, local copies, waits for them, and re-layouts: 2.96 us -> 1.29 us  [blocked(): x.reshape(user_blocks, tile, item_blocks, tile).transpose(0, 2, 1, 3)]
    reshape x2, local copies, waits for them, and re-layouts: 2.43 us -> 1.07 us  [unblocked(): x.reshape(user_blocks, item_blocks, tile, tile).transpose(0, 2, 1, 3)]
  transfers between devices with their start and end apart: 3 -> 0, of which waited for: 3 -> 0; matrix products, arithmetic and copies ran while one was open for 8% -> 0% of each run, Pallas kernels for 0% -> 0%
where the time goes in v3:
time: 95 us; the launch traced here: 94.6 us
  Pallas kernels  66.6 us (70%)
  other arithmetic  13.2 us (14%)
  local copies, waits for them, and re-layouts  8.24 us (9%)
  matrix products  5.66 us (6%)
    pallas_call x2, Pallas kernels, exchange(): pl.pallas_call(functools.partial(exchange_kernel, axes), out_shape=[jax.S...  66.6 us
    dot_general x12, matrix products, product(): return jnp.einsum(form, first, second, preferred_element_type=jnp.float32)  5.66 us
    convert_element_type x1, other arithmetic, shards(): ((tvalid * (predicted - imputes) + weight * (imputes - clicks)) * loss_we...  3.44 us

profile of v3, /device:TPU:1, one launch (start us, length us, event | category | flops | bytes accessed | tf_op | source)
XLA Modules:
  0.0 94.6 jit_solution(11403638714664762148)
XLA Ops:
  0.6 0.0 copy-start
  0.6 0.0 copy-start.9
  0.7 0.8 add_reduce_fusion
  1.4 0.7 convert_bitcast_fusion.1
  2.1 0.7 fusion.24
  2.8 0.1 copy.33
  2.9 0.1 copy.32
  3.0 0.1 eq.34
  3.0 0.1 copy.31
  3.1 0.1 convert_reduce_fusion
  3.2 0.1 scatter.11
  3.4 0.1 scatter.14
  3.5 1.3 %convert_bitcast_fusion = bf16[16,128,128]{2,1,0:T(8,128)(2,1)S(1)} fusion(s32[1,1,16,128,128]{4,3,2,1,0:T(8,128)} %param.26), kind=kLoop, calls=%fused_computation.29 | loop fusion | flops 262144 | bytes 1572864 | tf_op jit(solution)/shard_map/convert_element_type | solution.py:116
  4.9 0.0 copy-done.9
  4.9 1.1 %pad_maximum_fusion.refs_0_ = bf16[16,264,128]{2,1,0:T(8,128)(2,1)} fusion(bf16[16,8,128]{2,1,0:T(8,128)(2,1)S(1)} %scatter.14, bf16[16,128,128]{2,1,0:T(8,128)(2,1)S(1)} %bitcast.102, bf16[16,128,128]{2,1,0:T(8,128)(2,1)S(1)} %convert_bitcast_fusion), kind=kLoop, calls=%fused_computation.7 | loop fusion | flops 3244032 | bytes 2162688 | tf_op jit(solution)/shard_map/concatenate | solution.py:118
  6.0 34.0 %shard_map.138 = bf16[16,264,128]{2,1,0:T(8,128)(2,1)} custom-call(bf16[16,264,128]{2,1,0:T(8,128)(2,1)} %pad_maximum_fusion.refs_0_), custom_call_target="tpu_custom_call" | custom-call | tf_op jit(solution)/shard_map/pallas_call | solution.py:61
  40.0 0.8 slice_convert_fusion
  40.7 0.4 fusion.18
  41.1 0.2 slice_reduce_fusion
  41.4 0.0 copy-done
  41.4 0.0 copy-done.6
  41.4 0.3 fusion.26
  41.7 0.5 reshape.218
  42.2 0.1 copy.34
  42.4 0.0 copy-start.3
  42.4 0.0 copy-start.5
  42.4 1.6 %gather_fusion = f32[16,128,128]{2,1,0:T(8,128)} fusion(f32[16,128,128]{2,1,0:T(8,128)S(1)} %bitcast.94, s32[1024]{0:T(1024)S(1)} %pad_clamp_fusion), kind=kCustom, calls=%fused_computation | custom fusion | bytes 2097216 | tf_op jit(solution)/shard_map/gather | solution.py:140
  44.0 0.0 copy-done.3
  44.0 0.0 copy-done.5
  44.0 0.3 fusion.27
  44.3 0.5 reshape.220
  44.9 0.1 copy.35
  45.0 0.0 copy-start.1
  45.0 1.6 %gather_fusion.1 = f32[16,128,128]{2,1,0:T(8,128)} fusion(f32[16,128,128]{2,1,0:T(8,128)S(1)} %bitcast.95, s32[1024]{0:T(1024)S(1)} %pad_clamp_fusion), kind=kCustom, calls=%fused_computation.1 | custom fusion | bytes 2097216 | tf_op jit(solution)/shard_map/gather | solution.py:142
  46.6 0.0 copy-done.1
  46.6 3.4 %multiply_convert_fusion = (bf16[16,128,128]{2,1,0:T(8,128)(2,1)S(1)}, bf16[16,128,128]{2,1,0:T(8,128)(2,1)}) fusion(f32[16,128,128]{2,1,0:T(8,128)} %gather_fusion, f32[16]{0:T(128)S(1)} %slice_reduce_fusion, f32[16,128,128]{2,1,0:T(8,128)} %gather_fusion.1, bf16[16,264,128]{2,1,0:T(8,128)(2,1)S(1)} %copy-done.1), kind=kLoop, calls=%fused_computation.20 | loop fusion | flops 7340032 | bytes 4194368 | tf_op jit(solution)/shard_map/convert_element_type | solution.py:147
  50.0 0.4 fusion.8
  50.4 0.7 copy_add_fusion
  51.2 0.4 copy.38
  51.6 0.0 copy-start.2
  51.6 0.3 fusion.10
  51.9 1.0 %convolution_add_fusion.3 = f32[256,128]{1,0:T(8,128)} fusion(f32[256,128]{1,0:T(8,128)S(1)} %fusion.10, bf16[1024,128]{1,0:T(8,128)(2,1)S(1)} %copy-done, f32[32,8,8,128]{3,2,1,0:T(8,128)S(1)} %bitcast.87), kind=kOutput, calls=%fused_computation.6 | convolution fusion | flops 68190208 | bytes 1572864 | tf_op jit(solution)/shard_map/ab,ar->br/dot_general | solution.py:17
  52.9 0.0 copy-done.2
  52.9 0.4 fusion.6
  53.3 0.7 copy.40
  54.0 0.0 copy-start.4
  54.0 0.0 copy-start.8
  54.0 1.3 %fusion.12 = f32[256,128]{1,0:T(8,128)S(1)} fusion(bf16[1024,128]{1,0:T(8,128)(2,1)} %param.18, f32[32,8,8,128]{3,2,1,0:T(8,128)S(1)} %bitcast.90), kind=kOutput, calls=%fused_computation.33 | convolution fusion | flops 67108864 | bytes 1441792 | tf_op jit(solution)/shard_map/ab,ar->br/dot_general | solution.py:17
  55.3 0.0 copy-done.4
  55.3 0.3 convolution_add_fusion.2
  55.6 0.0 copy-done.8
  55.6 0.7 maximum_bitcast_fusion.1.refs_1_
  56.4 0.4 fusion.13
  56.7 0.0 copy-start.7
  56.7 0.4 convolution_add_fusion
  57.1 0.5 copy-done.7
  57.6 0.4 fusion.11
  57.9 0.4 convolution_add_fusion.1
  58.3 1.1 %maximum_bitcast_fusion.refs_0_ = f32[16,2,64,128]{3,2,1,0:T(8,128)} fusion(f32[1,16,64,128]{3,2,0,1:T(8,128)S(1)} %bitcast.98, f32[1,16,64,128]{3,2,0,1:T(8,128)S(1)} %bitcast.99), kind=kLoop, calls=%fused_computation.18 | loop fusion | flops 262144 | bytes 2097152 | tf_op jit(solution)/shard_map/transpose | solution.py:164
  59.4 32.6 %shard_map.139 = (f32[16,2,64,128]{3,2,1,0:T(8,128)}, f32[16,2,16,128]{3,2,1,0:T(8,128)}) custom-call(f32[16,2,64,128]{3,2,1,0:T(8,128)} %maximum_bitcast_fusion.refs_0_, f32[16,2,16,128]{3,2,1,0:T(8,128)} %maximum_bitcast_fusion.1.refs_1_), custom_call_target="tpu_custom_call" | custom-call | tf_op jit(solution)/shard_map/pallas_call | solution.py:61
  92.0 0.0 copy-start.10
  92.0 1.3 %reduce_sum.38 = f32[2,64,128]{2,1,0:T(8,128)S(1)} reduce(f32[16,2,64,128]{3,2,1,0:T(8,128)} %get-tuple-element.42, f32[]{:T(128)} %constant.104.clone.1), dimensions={0}, to_apply=%region_2.0 | reduce | flops 245760 | bytes 1114116 | tf_op jit(solution)/shard_map/reduce_sum | solution.py:167
  93.4 0.6 slice_bitcast_fusion.2
  94.0 0.6 slice_bitcast_fusion
  (7 shorter events, 0.1 us)
Async XLA Ops:
  0.6 40.8 %copy-start = (bf16[1024,128]{1,0:T(8,128)(2,1)S(1)}, bf16[1024,128]{1,0:T(8,128)(2,1)}, u32[]{:S(2)}) copy-start(bf16[1024,128]{1,0:T(8,128)(2,1)} %param.17) | copy-start | bytes 786436
  0.6 4.2 %copy-start.9 = (bf16[1,1,16,128,128]{4,3,2,1,0:T(8,128)(2,1)S(1)}, bf16[1,1,16,128,128]{4,3,2,1,0:T(8,128)(2,1)}, u32[]{:S(2)}) copy-start(bf16[1,1,16,128,128]{4,3,2,1,0:T(8,128)(2,1)} %param.27) | copy-start | bytes 1572868
  6.0 35.4 %copy-start.6 = (bf16[256,128]{1,0:T(8,128)(2,1)S(1)}, bf16[256,128]{1,0:T(8,128)(2,1)}, u32[]{:S(2)}) copy-start(bf16[256,128]{1,0:T(8,128)(2,1)} %param.19) | copy-start | bytes 196612
  42.4 1.7 %copy-start.3 = (bf16[1024,128]{1,0:T(8,128)(2,1)S(1)}, bf16[1024,128]{1,0:T(8,128)(2,1)}, u32[]{:S(2)}) copy-start(bf16[1024,128]{1,0:T(8,128)(2,1)} %param.18) | copy-start | bytes 786436
  42.4 1.7 %copy-start.5 = (bf16[256,128]{1,0:T(8,128)(2,1)S(1)}, bf16[256,128]{1,0:T(8,128)(2,1)}, u32[]{:S(2)}) copy-start(bf16[256,128]{1,0:T(8,128)(2,1)} %param.20) | copy-start | bytes 196612
  45.0 1.6 %copy-start.1 = (bf16[16,264,128]{2,1,0:T(8,128)(2,1)S(1)}, bf16[16,264,128]{2,1,0:T(8,128)(2,1)}, u32[]{:S(2)}) copy-start(bf16[16,264,128]{2,1,0:T(8,128)(2,1)} %shard_map.138) | copy-start | bytes 3244036
  51.6 1.3 %copy-start.2 = (bf16[16,128,128]{2,1,0:T(8,128)(2,1)S(1)}, bf16[16,128,128]{2,1,0:T(8,128)(2,1)}, u32[]{:S(2)}) copy-start(bf16[16,128,128]{2,1,0:T(8,128)(2,1)} %get-tuple-element.45) | copy-start | bytes 1572868
  54.0 1.3 %copy-start.4 = (bf16[1024,128]{1,0:T(8,128)(2,1)S(1)}, bf16[1024,128]{1,0:T(8,128)(2,1)}, u32[]{:S(2)}) copy-start(bf16[1024,128]{1,0:T(8,128)(2,1)} %param.18) | copy-start | bytes 786436
  54.0 1.6 %copy-start.8 = (f32[256,128]{1,0:T(8,128)S(1)}, f32[256,128]{1,0:T(8,128)}, u32[]{:S(2)}) copy-start(f32[256,128]{1,0:T(8,128)} %convolution_add_fusion.3) | copy-start | bytes 393220
  56.7 0.8 copy-start.7
  92.0 1.3 %copy-start.10 = (f32[16,2,16,128]{3,2,1,0:T(8,128)S(1)}, f32[16,2,16,128]{3,2,1,0:T(8,128)}, u32[]{:S(2)}) copy-start(f32[16,2,16,128]{3,2,1,0:T(8,128)} %get-tuple-element.43) | copy-start | bytes 786436

commit v4 on v3

--- a/solution.py
+++ b/solution.py
@@ -17,10 +17,25 @@
     return jnp.einsum(form, first, second, preferred_element_type=jnp.float32)
 
 
-def exchange_kernel(axes, *refs):
-    count = len(axes)
-    x_refs, y_refs = refs[:count], refs[count : 2 * count]
-    send_sem, recv_sem, local_sem = refs[2 * count :]
+def dense_blocks(tile, item_blocks, up_ref, ui_ref, vp_ref, vi_ref, s_ref, m_ref, d_ref):
+    def block(k, carry):
+        users = pl.ds(pl.multiple_of((k // item_blocks) * tile, tile), tile)
+        items = pl.ds(pl.multiple_of((k % item_blocks) * tile, tile), tile)
+        dims = (((1,), (1,)), ((), ()))
+        logits = lax.dot_general(up_ref[users, :], vp_ref[items, :], dims, preferred_element_type=jnp.float32)
+        imputed = lax.dot_general(ui_ref[users, :], vi_ref[items, :], dims, preferred_element_type=jnp.float32)
+        s_ref[k] = logits
+        m_ref[k] = imputed
+        d_ref[k] = ((jax.nn.sigmoid(logits) - jax.nn.sigmoid(imputed)) * loss_weight).astype(d_ref.dtype)
+        return carry
+
+    lax.fori_loop(0, s_ref.shape[0], block, 0)
+
+
+def exchange_kernel(axes, count, work_in, work, *refs):
+    x_refs, y_refs = refs[:count], refs[count + work_in : 2 * count + work_in]
+    send_sem, recv_sem, local_sem = refs[-3:]
+    work_refs = refs[count : count + work_in] + refs[2 * count + work_in : -3]
     barrier = pltpu.get_barrier_semaphore()
     for axis in axes:
         n = lax.axis_size(axis)
@@ -50,26 +65,29 @@
             copy.start()
             copies.append(copy)
             slot += 1
+    if work is not None:
+        work(*work_refs)
     for copy in copies:
         copy.wait()
 
 
-def exchange(pairs, collective):
+def exchange(pairs, collective, work=None, work_inputs=(), work_outputs=()):
     axes = tuple(axis for _, axis in pairs)
     arrays = [x for x, _ in pairs]
     slots = sum(lax.axis_size(axis) - 1 for axis in axes)
+    vmem = pl.BlockSpec(memory_space=pltpu.VMEM)
     return pl.pallas_call(
-        functools.partial(exchange_kernel, axes),
-        out_shape=[jax.ShapeDtypeStruct(x.shape, x.dtype) for x in arrays],
-        in_specs=[pl.BlockSpec(memory_space=pl.ANY)] * len(arrays),
-        out_specs=[pl.BlockSpec(memory_space=pl.ANY)] * len(arrays),
+        functools.partial(exchange_kernel, axes, len(arrays), len(work_inputs), work),
+        out_shape=[jax.ShapeDtypeStruct(x.shape, x.dtype) for x in arrays] + list(work_outputs),
+        in_specs=[pl.BlockSpec(memory_space=pl.ANY)] * len(arrays) + [vmem] * len(work_inputs),
+        out_specs=[pl.BlockSpec(memory_space=pl.ANY)] * len(arrays) + [vmem] * len(work_outputs),
         scratch_shapes=[
             pltpu.SemaphoreType.DMA((slots,)),
             pltpu.SemaphoreType.DMA((slots,)),
             pltpu.SemaphoreType.DMA((len(arrays),)),
         ],
         compiler_params=pltpu.CompilerParams(collective_id=collective, has_side_effects=True),
-    )(*arrays)
+    )(*arrays, *work_inputs)
 
 
 def split_product(form, wide, narrow):
@@ -116,7 +134,18 @@
     labels = obs_label.reshape(item_ways, obs_slots * tile, tile).astype(jnp.bfloat16)
     propens = obs_prop.reshape(item_ways, obs_slots * tile, tile)
     package = jnp.concatenate([labels, propens, meta.astype(jnp.bfloat16)], axis=1)
-    (got,) = exchange([(package, "item")], 0)
+    block_shape = (n_blocks, tile, tile)
+    got, logit_blocks, imputed_blocks, uno_grads = exchange(
+        [(package, "item")],
+        0,
+        functools.partial(dense_blocks, tile, item_blocks),
+        (user_pred, user_imp, item_pred, item_imp),
+        (
+            jax.ShapeDtypeStruct(block_shape, jnp.float32),
+            jax.ShapeDtypeStruct(block_shape, jnp.float32),
+            jax.ShapeDtypeStruct(block_shape, jnp.bfloat16),
+        ),
+    )
     got_labels = got[:, : obs_slots * tile].reshape(item_ways * obs_slots, tile, tile)
     got_props = got[:, obs_slots * tile : 2 * obs_slots * tile].reshape(item_ways * obs_slots, tile, tile)
     got_meta = got[:, 2 * obs_slots * tile :].astype(jnp.float32)
@@ -124,18 +153,8 @@
     tile_pos = got_meta[:, 1, :obs_slots].reshape(-1).astype(jnp.int32)
     tile_valid = got_meta[:, 2, :obs_slots].reshape(-1)
 
-    logits = product("ar,br->ab", user_pred, item_pred)
-    imputed = product("ar,br->ab", user_imp, item_imp)
-
-    def blocked(x):
-        return x.reshape(user_blocks, tile, item_blocks, tile).transpose(0, 2, 1, 3).reshape(n_blocks, tile, tile)
-
     def unblocked(x):
         return x.reshape(user_blocks, item_blocks, tile, tile).transpose(0, 2, 1, 3).reshape(user_rows, shard_rows)
-
-    logit_blocks = blocked(logits)
-    imputed_blocks = blocked(imputed)
-    uno_grads = ((jax.nn.sigmoid(logit_blocks) - jax.nn.sigmoid(imputed_blocks)) * loss_weight).astype(jnp.bfloat16)
 
     ologits = logit_blocks[tile_pos]
     predicted = jax.nn.sigmoid(ologits)

time: 95 us -> 94.5 us (level)
  Pallas kernels: 66.6 us -> 69.1 us
  matrix products: 5.66 us -> 3.42 us
  other arithmetic: 13.2 us -> 11.2 us
  local copies, waits for them, and re-layouts: 8.24 us -> 9.31 us
    pallas_call x2, Pallas kernels: 66.6 us -> 69.1 us  [exchange(): pl.pallas_call(functools.partial(exchange_kernel, axes, len(arrays), len(...]
    dot_general x12 -> x10, matrix products: 5.66 us -> 3.42 us  [product(): return jnp.einsum(form, first, second, preferred_element_type=jnp.float32)]
    unnamed x22 -> x18, local copies, waits for them, and re-layouts: 0.53 us -> 2.36 us
    convert_element_type x1, other arithmetic: 3.44 us -> 1.9 us  [shards(): ((tvalid * (predicted - imputes) + weight * (imputes - clicks)) * loss_we...]
    reshape x4 -> x0, local copies, waits for them, and re-layouts: 1.29 us -> none  [blocked(): x.reshape(user_blocks, tile, item_blocks, tile).transpose(0, 2, 1, 3)]
where the time goes in v4:
time: 94.5 us; the launch traced here: 93.9 us
  Pallas kernels  69.1 us (73%)
  other arithmetic  11.2 us (12%)
  local copies, waits for them, and re-layouts  9.31 us (10%)
  matrix products  3.42 us (4%)
    pallas_call x2, Pallas kernels, exchange(): pl.pallas_call(functools.partial(exchange_kernel, axes, len(arrays), len(...  69.1 us
    dot_general x10, matrix products, product(): return jnp.einsum(form, first, second, preferred_element_type=jnp.float32)  3.42 us
    unnamed x18, local copies, waits for them, and re-layouts  2.36 us
    gather x1, local copies, waits for them, and re-layouts, shards(): ologits = logit_blocks[tile_pos]  1.93 us
    convert_element_type x1, other arithmetic, shards(): ((tvalid * (predicted - imputes) + weight * (imputes - clicks)) * loss_we...  1.9 us

profile of v4, /device:TPU:1, one launch (start us, length us, event | category | flops | bytes accessed | tf_op | source)
XLA Modules:
  0.0 93.9 jit_solution(17969727336978743811)
XLA Ops:
  0.6 0.0 copy-start.6
  0.6 0.7 add_reduce_fusion
  1.4 0.7 convert_bitcast_fusion.1
  2.1 0.7 fusion.24
  2.7 0.1 copy.29
  2.8 0.1 copy.28
  2.9 0.1 eq.34
  3.0 0.1 copy.27
  3.1 0.1 convert_reduce_fusion
  3.2 0.1 scatter.11
  3.4 0.1 scatter.14
  3.5 1.3 %convert_bitcast_fusion = bf16[16,128,128]{2,1,0:T(8,128)(2,1)S(1)} fusion(s32[1,1,16,128,128]{4,3,2,1,0:T(8,128)} %param.26), kind=kLoop, calls=%fused_computation.28 | loop fusion | flops 262144 | bytes 1572864 | tf_op jit(solution)/shard_map/convert_element_type | solution.py:134
  4.8 0.0 copy-done.6
  4.9 1.1 %pad_maximum_fusion.refs_0_ = bf16[16,264,128]{2,1,0:T(8,128)(2,1)} fusion(bf16[16,8,128]{2,1,0:T(8,128)(2,1)S(1)} %scatter.14, bf16[16,128,128]{2,1,0:T(8,128)(2,1)S(1)} %bitcast.88, bf16[16,128,128]{2,1,0:T(8,128)(2,1)S(1)} %convert_bitcast_fusion), kind=kLoop, calls=%fused_computation.7 | loop fusion | flops 3244032 | bytes 2162688 | tf_op jit(solution)/shard_map/concatenate | solution.py:136
  5.9 36.5 %shard_map.138 = (bf16[16,264,128]{2,1,0:T(8,128)(2,1)}, f32[16,128,128]{2,1,0:T(8,128)}, f32[16,128,128]{2,1,0:T(8,128)}, bf16[16,128,128]{2,1,0:T(8,128)(2,1)}) custom-call(bf16[16,264,128]{2,1,0:T(8,128)(2,1)} %pad_maximum_fusion.refs_0_, bf16[1024,128]{1,0:T(8,128)(2,1)} %refs_1_.1, bf16[1024,128]{1,0:T(8,128)(2,1)} %refs_2_.1, ...), custom_call_target="tpu_custom_call" | custom-call | tf_op jit(solution)/shard_map/pallas_call | solution.py:79
  42.4 0.8 slice_convert_fusion
  43.2 0.4 fusion.18
  43.6 0.2 slice_reduce_fusion
  43.8 1.8 %gather_fusion.1 = f32[16,128,128]{2,1,0:T(8,128)S(1)} fusion(f32[16,128,128]{2,1,0:T(8,128)} %get-tuple-element.49, s32[1024]{0:T(1024)S(1)} %pad_clamp_fusion), kind=kCustom, calls=%fused_computation.1 | custom fusion | bytes 2097216 | tf_op jit(solution)/shard_map/gather | solution.py:161
  45.7 0.0 copy-start.1
  45.7 1.9 %gather_fusion = f32[16,128,128]{2,1,0:T(8,128)S(1)} fusion(f32[16,128,128]{2,1,0:T(8,128)} %get-tuple-element.48, s32[1024]{0:T(1024)S(1)} %pad_clamp_fusion), kind=kCustom, calls=%fused_computation | custom fusion | bytes 2097216 | tf_op jit(solution)/shard_map/gather | solution.py:159
  47.6 0.0 copy-done.1
  47.6 1.9 %multiply_convert_fusion = (bf16[16,128,128]{2,1,0:T(8,128)(2,1)S(1)}, bf16[16,128,128]{2,1,0:T(8,128)(2,1)}) fusion(f32[16,128,128]{2,1,0:T(8,128)S(1)} %gather_fusion, f32[16]{0:T(128)S(1)} %slice_reduce_fusion, f32[16,128,128]{2,1,0:T(8,128)S(1)} %gather_fusion.1, bf16[16,264,128]{2,1,0:T(8,128)(2,1)S(1)} %copy-done.1), kind=kLoop, calls=%fused_computation.20 | loop fusion | flops 7340032 | bytes 4194368 | tf_op jit(solution)/shard_map/convert_element_type | solution.py:166
  49.5 0.0 copy-start.7
  49.5 0.4 fusion.8
  49.9 0.6 copy-done.7
  50.6 0.4 copy_add_fusion
  51.0 0.0 copy-start.2
  51.0 0.4 copy.32
  51.4 0.5 copy-done.2
  51.9 0.0 copy-start
  51.9 0.3 fusion.10
  52.2 0.3 convolution_add_fusion.3
  52.5 0.4 copy-done
  53.0 0.4 fusion.6
  53.4 0.0 copy-start.3
  53.4 0.7 copy.34
  54.0 0.3 copy-done.3
  54.3 0.3 fusion.12
  54.6 0.0 copy-start.4
  54.6 0.3 convolution_add_fusion.2
  54.9 0.7 maximum_bitcast_fusion.1.refs_1_
  55.7 0.0 copy-done.4
  55.7 0.4 fusion.13
  56.0 0.0 copy-start.5
  56.1 0.4 convolution_add_fusion
  56.4 0.5 copy-done.5
  56.9 0.4 fusion.11
  57.2 0.4 convolution_add_fusion.1
  57.6 1.1 %maximum_bitcast_fusion.refs_0_ = f32[16,2,64,128]{3,2,1,0:T(8,128)} fusion(f32[1,16,64,128]{3,2,0,1:T(8,128)S(1)} %bitcast.84, f32[1,16,64,128]{3,2,0,1:T(8,128)S(1)} %bitcast.85), kind=kLoop, calls=%fused_computation.18 | loop fusion | flops 262144 | bytes 2097152 | tf_op jit(solution)/shard_map/transpose | solution.py:183
  58.7 32.6 %shard_map.139 = (f32[16,2,64,128]{3,2,1,0:T(8,128)}, f32[16,2,16,128]{3,2,1,0:T(8,128)}) custom-call(f32[16,2,64,128]{3,2,1,0:T(8,128)} %maximum_bitcast_fusion.refs_0_, f32[16,2,16,128]{3,2,1,0:T(8,128)} %maximum_bitcast_fusion.1.refs_1_), custom_call_target="tpu_custom_call" | custom-call | tf_op jit(solution)/shard_map/pallas_call | solution.py:79
  91.3 0.0 copy-start.8
  91.3 1.3 %reduce_sum.38 = f32[2,64,128]{2,1,0:T(8,128)S(1)} reduce(f32[16,2,64,128]{3,2,1,0:T(8,128)} %get-tuple-element.50, f32[]{:T(128)} %constant.104.clone.1), dimensions={0}, to_apply=%region_2.0 | reduce | flops 245760 | bytes 1114116 | tf_op jit(solution)/shard_map/reduce_sum | solution.py:186
  92.6 0.0 copy-done.8
  92.7 0.6 slice_bitcast_fusion.2
  93.3 0.6 slice_bitcast_fusion
  (5 shorter events, 0.1 us)
Async XLA Ops:
  0.6 4.2 %copy-start.6 = (bf16[1,1,16,128,128]{4,3,2,1,0:T(8,128)(2,1)S(1)}, bf16[1,1,16,128,128]{4,3,2,1,0:T(8,128)(2,1)}, u32[]{:S(2)}) copy-start(bf16[1,1,16,128,128]{4,3,2,1,0:T(8,128)(2,1)} %param.27) | copy-start | bytes 1572868
  45.7 1.9 %copy-start.1 = (bf16[16,264,128]{2,1,0:T(8,128)(2,1)S(1)}, bf16[16,264,128]{2,1,0:T(8,128)(2,1)}, u32[]{:S(2)}) copy-start(bf16[16,264,128]{2,1,0:T(8,128)(2,1)} %get-tuple-element.46) | copy-start | bytes 3244036
  49.5 1.0 %copy-start.7 = (bf16[16,128,128]{2,1,0:T(8,128)(2,1)S(1)}, bf16[16,128,128]{2,1,0:T(8,128)(2,1)}, u32[]{:S(2)}) copy-start(bf16[16,128,128]{2,1,0:T(8,128)(2,1)} %get-tuple-element.47) | copy-start | bytes 1572868
  51.0 1.0 %copy-start.2 = (bf16[1024,128]{1,0:T(8,128)(2,1)S(1)}, bf16[1024,128]{1,0:T(8,128)(2,1)}, u32[]{:S(2)}) copy-start(bf16[1024,128]{1,0:T(8,128)(2,1)} %refs_1_.1) | copy-start | bytes 786436
  51.9 1.0 %copy-start = (bf16[16,128,128]{2,1,0:T(8,128)(2,1)S(1)}, bf16[16,128,128]{2,1,0:T(8,128)(2,1)}, u32[]{:S(2)}) copy-start(bf16[16,128,128]{2,1,0:T(8,128)(2,1)} %get-tuple-element.53) | copy-start | bytes 1572868
  53.4 1.0 %copy-start.3 = (bf16[1024,128]{1,0:T(8,128)(2,1)S(1)}, bf16[1024,128]{1,0:T(8,128)(2,1)}, u32[]{:S(2)}) copy-start(bf16[1024,128]{1,0:T(8,128)(2,1)} %refs_2_.1) | copy-start | bytes 786436
  54.6 1.1 %copy-start.4 = (bf16[256,128]{1,0:T(8,128)(2,1)S(1)}, bf16[256,128]{1,0:T(8,128)(2,1)}, u32[]{:S(2)}) copy-start(bf16[256,128]{1,0:T(8,128)(2,1)} %refs_4_.1) | copy-start | bytes 196612
  56.0 0.8 copy-start.5
  91.3 1.3 %copy-start.8 = (f32[16,2,16,128]{3,2,1,0:T(8,128)S(1)}, f32[16,2,16,128]{3,2,1,0:T(8,128)}, u32[]{:S(2)}) copy-start(f32[16,2,16,128]{3,2,1,0:T(8,128)} %get-tuple-element.51) | copy-start | bytes 786436

commit v5 on v4

--- a/solution.py
+++ b/solution.py
@@ -90,10 +90,68 @@
     )(*arrays, *work_inputs)
 
 
-def split_product(form, wide, narrow):
-    hi = wide.astype(jnp.bfloat16)
-    lo = (wide - hi.astype(jnp.float32)).astype(jnp.bfloat16)
-    return product(form, hi, narrow) + product(form, lo, narrow)
+def tile_kernel(
+    tile, user_blocks, item_blocks, n_tiles, obs_slots,
+    pos_ref, count_ref, valid_ref,
+    s_ref, m_ref, d_ref, got_ref, up_ref, ui_ref, vp_ref, vi_ref,
+    user_out, item_out,
+    g_acc, h_acc, user_acc, item_acc,
+):
+    n_blocks = user_blocks * item_blocks
+    for k in range(n_blocks):
+        g_acc[k] = count_ref[k] * d_ref[k].astype(jnp.float32)
+        h_acc[k] = jnp.zeros((tile, tile), jnp.float32)
+
+    def observed(t, carry):
+        pos = pos_ref[t]
+        valid = valid_ref[t]
+        ologits = s_ref[pos]
+        predicted = jax.nn.sigmoid(ologits)
+        imputes = jax.nn.sigmoid(m_ref[pos])
+        origin = t // obs_slots
+        slot = t % obs_slots
+        labels = got_ref[origin, pl.ds(slot * tile, tile), :].astype(jnp.float32)
+        propens = got_ref[origin, pl.ds((obs_slots + slot) * tile, tile), :].astype(jnp.float32)
+        seen = (labels > 0).astype(jnp.float32)
+        clicks = (labels == 2).astype(jnp.float32)
+        weight = valid * seen / propens
+        ograds = ((valid * (predicted - imputes) + weight * (imputes - clicks)) * loss_weight).astype(jnp.bfloat16)
+        ohgrads = (
+            2.0 * weight * (imputes - clicks) * ologits * ologits * imputes * (1.0 - imputes) * loss_weight
+        ).astype(jnp.bfloat16)
+        g_acc[pos] += ograds.astype(jnp.float32)
+        h_acc[pos] += ohgrads.astype(jnp.float32)
+        return carry
+
+    lax.fori_loop(0, n_tiles, observed, 0)
+
+    user_acc[...] = jnp.zeros(user_acc.shape, jnp.float32)
+    item_acc[...] = jnp.zeros(item_acc.shape, jnp.float32)
+    forward = (((1,), (0,)), ((), ()))
+    backward = (((0,), (0,)), ((), ()))
+    for ub in range(user_blocks):
+        users = pl.ds(ub * tile, tile)
+        for ib in range(item_blocks):
+            items = pl.ds(ib * tile, tile)
+            k = ub * item_blocks + ib
+            for model, acc, u_ref, v_ref in ((0, g_acc, up_ref, vp_ref), (1, h_acc, ui_ref, vi_ref)):
+                wide = acc[k]
+                hi = wide.astype(jnp.bfloat16)
+                lo = (wide - hi.astype(jnp.float32)).astype(jnp.bfloat16)
+                v = v_ref[items, :]
+                u = u_ref[users, :]
+                user_acc[model, users, :] += lax.dot_general(
+                    hi, v, forward, preferred_element_type=jnp.float32
+                ) + lax.dot_general(lo, v, forward, preferred_element_type=jnp.float32)
+                item_acc[model, items, :] += lax.dot_general(
+                    hi, u, backward, preferred_element_type=jnp.float32
+                ) + lax.dot_general(lo, u, backward, preferred_element_type=jnp.float32)
+    user_rows = user_out.shape[2]
+    for dest in range(user_out.shape[0]):
+        user_out[dest] = user_acc[:, pl.ds(dest * user_rows, user_rows), :]
+    item_rows = item_out.shape[2]
+    for dest in range(item_out.shape[0]):
+        item_out[dest] = item_acc[:, pl.ds(dest * item_rows, item_rows), :]
 
 
 def shards(
@@ -146,42 +204,31 @@
             jax.ShapeDtypeStruct(block_shape, jnp.bfloat16),
         ),
     )
-    got_labels = got[:, : obs_slots * tile].reshape(item_ways * obs_slots, tile, tile)
-    got_props = got[:, obs_slots * tile : 2 * obs_slots * tile].reshape(item_ways * obs_slots, tile, tile)
     got_meta = got[:, 2 * obs_slots * tile :].astype(jnp.float32)
     counts = jnp.sum(got_meta[:, 0, :n_blocks], axis=0)
     tile_pos = got_meta[:, 1, :obs_slots].reshape(-1).astype(jnp.int32)
     tile_valid = got_meta[:, 2, :obs_slots].reshape(-1)
 
-    def unblocked(x):
-        return x.reshape(user_blocks, item_blocks, tile, tile).transpose(0, 2, 1, 3).reshape(user_rows, shard_rows)
-
-    ologits = logit_blocks[tile_pos]
-    predicted = jax.nn.sigmoid(ologits)
-    imputes = jax.nn.sigmoid(imputed_blocks[tile_pos])
-    tvalid = tile_valid[:, None, None]
-    seen = (got_labels > 0).astype(jnp.float32)
-    clicks = (got_labels == 2).astype(jnp.float32)
-    weight = tvalid * seen / got_props.astype(jnp.float32)
-    ograds = ((tvalid * (predicted - imputes) + weight * (imputes - clicks)) * loss_weight).astype(jnp.bfloat16)
-    ohgrads = (
-        2.0 * weight * (imputes - clicks) * ologits * ologits * imputes * (1.0 - imputes) * loss_weight
-    ).astype(jnp.bfloat16)
-    onehot = (tile_pos[:, None] == jnp.arange(n_blocks, dtype=jnp.int32)[None, :]).astype(jnp.bfloat16)
-    grad_blocks = counts[:, None, None] * uno_grads.astype(jnp.float32) + product("tk,tab->kab", onehot, ograds)
-    hgrad_blocks = product("tk,tab->kab", onehot, ohgrads)
-    grad_full = unblocked(grad_blocks)
-    hgrad_full = unblocked(hgrad_blocks)
-
-    user_part = jnp.stack(
-        [split_product("ab,br->ar", grad_full, item_pred), split_product("ab,br->ar", hgrad_full, item_imp)]
-    )
-    item_part = jnp.stack(
-        [split_product("ab,ar->br", grad_full, user_pred), split_product("ab,ar->br", hgrad_full, user_imp)]
-    )
-
-    user_chunks = user_part.reshape(2, item_ways, user_rows // item_ways, rank).transpose(1, 0, 2, 3)
-    item_chunks = item_part.reshape(2, user_ways, shard_rows // user_ways, rank).transpose(1, 0, 2, 3)
+    vmem = pl.BlockSpec(memory_space=pltpu.VMEM)
+    smem = pl.BlockSpec(memory_space=pltpu.SMEM)
+    user_chunks, item_chunks = pl.pallas_call(
+        functools.partial(tile_kernel, tile, user_blocks, item_blocks, item_ways * obs_slots, obs_slots),
+        out_shape=[
+            jax.ShapeDtypeStruct((item_ways, 2, user_rows // item_ways, rank), jnp.float32),
+            jax.ShapeDtypeStruct((user_ways, 2, shard_rows // user_ways, rank), jnp.float32),
+        ],
+        in_specs=[smem] * 3 + [vmem] * 8,
+        out_specs=[vmem, vmem],
+        scratch_shapes=[
+            pltpu.VMEM((n_blocks, tile, tile), jnp.float32),
+            pltpu.VMEM((n_blocks, tile, tile), jnp.float32),
+            pltpu.VMEM((2, user_rows, rank), jnp.float32),
+            pltpu.VMEM((2, shard_rows, rank), jnp.float32),
+        ],
+    )(
+        tile_pos, counts, tile_valid,
+        logit_blocks, imputed_blocks, uno_grads, got, user_pred, user_imp, item_pred, item_imp,
+    )
     user_got, item_got = exchange([(user_chunks, "item"), (item_chunks, "user")], 1)
     user_share = jnp.sum(user_got, axis=0)
     item_share = jnp.sum(item_got, axis=0)

time: 94.5 us -> 86.7 us (0.917)
  local copies, waits for them, and re-layouts: 9.31 us -> 2.63 us
  Pallas kernels: 69.1 us -> 75 us
  matrix products: 3.42 us -> 0 us
  other arithmetic: 11.2 us -> 8.12 us
    pallas_call x0 -> x1, Pallas kernels: none -> 5.85 us  [shards(): pl.pallas_call(functools.partial(tile_kernel, tile, user_blocks, item_blo...]
    gather x2 -> x0, local copies, waits for them, and re-layouts: 3.77 us -> none  [the longest x1 1.93 us: shards(): ologits = logit_blocks[tile_pos]]
    dot_general x10 -> x0, matrix products: 3.42 us -> none  [product(): return jnp.einsum(form, first, second, preferred_element_type=jnp.float32)]
    unnamed x18 -> x4, local copies, waits for them, and re-layouts: 2.36 us -> 0.01 us
    convert_element_type x1 -> x0, other arithmetic: 1.9 us -> none  [shards(): ((tvalid * (predicted - imputes) + weight * (imputes - clicks)) * loss_we...]
    transpose x2 -> x0, other arithmetic: 1.85 us -> none  [the longest x1 1.1 us: shards(): user_part.reshape(2, item_ways, user_rows // item_ways, rank)]
    reshape x2 -> x0, local copies, waits for them, and re-layouts: 1.07 us -> none  [unblocked(): x.reshape(user_blocks, item_blocks, tile, tile).transpose(0, 2, 1, 3)]
where the time goes in v5:
time: 86.7 us; the launch traced here: 86.4 us
  Pallas kernels  75 us (87%)
  other arithmetic  8.12 us (9%)
  local copies, waits for them, and re-layouts  2.63 us (3%)
    pallas_call x2, Pallas kernels, exchange(): pl.pallas_call(functools.partial(exchange_kernel, axes, len(arrays), len(...  69.1 us
    pallas_call x1, Pallas kernels, shards(): pl.pallas_call(functools.partial(tile_kernel, tile, user_blocks, item_blo...  5.85 us

profile of v5, /device:TPU:1, one launch (start us, length us, event | category | flops | bytes accessed | tf_op | source)
XLA Modules:
  0.0 86.4 jit_solution(10205197484834575060)
XLA Ops:
  0.6 0.0 copy-start
  0.6 0.7 add_reduce_fusion
  1.4 0.7 convert_bitcast_fusion.1
  2.1 0.7 fusion.1
  2.7 0.1 copy.21
  2.8 0.1 copy.20
  2.9 0.1 eq.15
  3.0 0.1 copy.19
  3.1 0.1 convert_reduce_fusion
  3.2 0.1 scatter.11
  3.4 0.1 scatter.14
  3.5 1.3 %convert_bitcast_fusion = bf16[16,128,128]{2,1,0:T(8,128)(2,1)S(1)} fusion(s32[1,1,16,128,128]{4,3,2,1,0:T(8,128)} %param.26), kind=kLoop, calls=%fused_computation.1 | loop fusion | flops 262144 | bytes 1572864 | tf_op jit(solution)/shard_map/convert_element_type | solution.py:192
  4.8 0.0 copy-done
  4.9 1.1 %pad_maximum_fusion.refs_0_ = bf16[16,264,128]{2,1,0:T(8,128)(2,1)} fusion(bf16[16,8,128]{2,1,0:T(8,128)(2,1)S(1)} %scatter.14, bf16[16,128,128]{2,1,0:T(8,128)(2,1)S(1)} %bitcast.16, bf16[16,128,128]{2,1,0:T(8,128)(2,1)S(1)} %convert_bitcast_fusion), kind=kLoop, calls=%fused_computation | loop fusion | flops 3244032 | bytes 2162688 | tf_op jit(solution)/shard_map/concatenate | solution.py:194
  5.9 36.5 %shard_map.138 = (bf16[16,264,128]{2,1,0:T(8,128)(2,1)}, f32[16,128,128]{2,1,0:T(8,128)}, f32[16,128,128]{2,1,0:T(8,128)}, bf16[16,128,128]{2,1,0:T(8,128)(2,1)}) custom-call(bf16[16,264,128]{2,1,0:T(8,128)(2,1)} %pad_maximum_fusion.refs_0_, bf16[1024,128]{1,0:T(8,128)(2,1)} %up_ref.1, bf16[1024,128]{1,0:T(8,128)(2,1)} %ui_ref.1, bf16[256,128]{1,0:T(8,128)(2,1)} %vp_ref.1, ...), custom_call_target="tpu_custom_call" | custom-call | tf_op jit(solution)/shard_map/pallas_call | solution.py:79
  42.4 0.8 slice_convert_fusion
  43.2 0.7 slice_reduce_fusion.valid_ref
  43.9 0.5 slice_reduce_fusion.1.count_ref
  44.5 0.9 %fusion.pos_ref = s32[16]{0:T(128)} fusion(f32[16,8,128]{2,1,0:T(8,128)S(1)} %slice_convert_fusion), kind=kLoop, calls=%fused_computation.12 | loop fusion | flops 16 | bytes 128 | tf_op jit(solution)/shard_map/convert_element_type | solution.py:209
  45.4 5.8 %shard_map.139 = (f32[16,2,64,128]{3,2,1,0:T(8,128)}, f32[16,2,16,128]{3,2,1,0:T(8,128)}) custom-call(s32[16]{0:T(128)} %fusion.pos_ref, f32[16]{0:T(128)} %slice_reduce_fusion.1.count_ref, f32[16]{0:T(128)} %slice_reduce_fusion.valid_ref, f32[16,128,128]{2,1,0:T(8,128)} %get-tuple-element.49.s_ref, f32[16,128,128]{2,1,0:T(8,128)} %get-tuple-element.50.m_ref, ...), custom_call_target="tpu_custom_call" | custom-call | tf_op jit(solution)/shard_map/pallas_call | solution.py:214
  51.2 32.6 %shard_map.140 = (f32[16,2,64,128]{3,2,1,0:T(8,128)}, f32[16,2,16,128]{3,2,1,0:T(8,128)}) custom-call(f32[16,2,64,128]{3,2,1,0:T(8,128)} %get-tuple-element.52.refs_0_, f32[16,2,16,128]{3,2,1,0:T(8,128)} %get-tuple-element.53.refs_1_), custom_call_target="tpu_custom_call" | custom-call | tf_op jit(solution)/shard_map/pallas_call | solution.py:79
  83.8 0.0 copy-start.1
  83.8 1.3 %reduce_sum.38 = f32[2,64,128]{2,1,0:T(8,128)S(1)} reduce(f32[16,2,64,128]{3,2,1,0:T(8,128)} %get-tuple-element.54, f32[]{:T(128)} %constant.96.clone.1), dimensions={0}, to_apply=%region_2.0 | reduce | flops 245760 | bytes 1114116 | tf_op jit(solution)/shard_map/reduce_sum | solution.py:233
  85.2 0.0 copy-done.1
  85.2 0.6 slice_bitcast_fusion.2
  85.8 0.6 slice_bitcast_fusion
  (2 shorter events, 0.0 us)
Async XLA Ops:
  0.6 4.2 %copy-start = (bf16[1,1,16,128,128]{4,3,2,1,0:T(8,128)(2,1)S(1)}, bf16[1,1,16,128,128]{4,3,2,1,0:T(8,128)(2,1)}, u32[]{:S(2)}) copy-start(bf16[1,1,16,128,128]{4,3,2,1,0:T(8,128)(2,1)} %param.27) | copy-start | bytes 1572868
  83.8 1.3 %copy-start.1 = (f32[16,2,16,128]{3,2,1,0:T(8,128)S(1)}, f32[16,2,16,128]{3,2,1,0:T(8,128)}, u32[]{:S(2)}) copy-start(f32[16,2,16,128]{3,2,1,0:T(8,128)} %get-tuple-element.55) | copy-start | bytes 786436

commit v6 on v5

--- a/solution.py
+++ b/solution.py
@@ -10,7 +10,6 @@
 MESH = pl.DeviceIdType.MESH
 
 loss_weight = 0.015625
-META_ROWS = 8
 
 
 def product(form, first, second):
@@ -90,28 +89,95 @@
     )(*arrays, *work_inputs)
 
 
+def reduce_kernel(axes, *refs):
+    count = len(axes)
+    x_refs, out_refs = refs[:count], refs[count : 2 * count]
+    land_refs = refs[2 * count : 3 * count]
+    send_sem, recv_sem, local_sem = refs[3 * count :]
+    barrier = pltpu.get_barrier_semaphore()
+    for axis in axes:
+        n = lax.axis_size(axis)
+        me = lax.axis_index(axis)
+        for k in range(1, n):
+            pl.semaphore_signal(barrier, inc=1, device_id={axis: lax.rem(me + k, n)}, device_id_type=MESH)
+    pl.semaphore_wait(barrier, sum(lax.axis_size(axis) - 1 for axis in axes))
+    copies = []
+    slot = 0
+    for which, axis in enumerate(axes):
+        n = lax.axis_size(axis)
+        me = lax.axis_index(axis)
+        x_ref, land = x_refs[which], land_refs[which]
+        local = pltpu.make_async_copy(x_ref.at[me], land.at[me], local_sem.at[which])
+        local.start()
+        copies.append(local)
+        for k in range(1, n):
+            peer = lax.rem(me + k, n)
+            copy = pltpu.make_async_remote_copy(
+                src_ref=x_ref.at[peer],
+                dst_ref=land.at[me],
+                send_sem=send_sem.at[slot],
+                recv_sem=recv_sem.at[slot],
+                device_id={axis: peer},
+                device_id_type=MESH,
+            )
+            copy.start()
+            copies.append(copy)
+            slot += 1
+    for copy in copies:
+        copy.wait()
+    for which in range(count):
+        land = land_refs[which]
+        total = land[0]
+        for source in range(1, land.shape[0]):
+            total = total + land[source]
+        out_refs[which][...] = total
+
+
+def reduce_exchange(pairs, collective):
+    axes = tuple(axis for _, axis in pairs)
+    arrays = [x for x, _ in pairs]
+    slots = sum(lax.axis_size(axis) - 1 for axis in axes)
+    return pl.pallas_call(
+        functools.partial(reduce_kernel, axes),
+        out_shape=[jax.ShapeDtypeStruct(x.shape[1:], x.dtype) for x in arrays],
+        in_specs=[pl.BlockSpec(memory_space=pl.ANY)] * len(arrays),
+        out_specs=[pl.BlockSpec(memory_space=pltpu.VMEM)] * len(arrays),
+        scratch_shapes=[pltpu.VMEM(x.shape, x.dtype) for x in arrays]
+        + [
+            pltpu.SemaphoreType.DMA((slots,)),
+            pltpu.SemaphoreType.DMA((slots,)),
+            pltpu.SemaphoreType.DMA((len(arrays),)),
+        ],
+        compiler_params=pltpu.CompilerParams(collective_id=collective, has_side_effects=True),
+    )(*arrays)
+
+
 def tile_kernel(
-    tile, user_blocks, item_blocks, n_tiles, obs_slots,
-    pos_ref, count_ref, valid_ref,
-    s_ref, m_ref, d_ref, got_ref, up_ref, ui_ref, vp_ref, vi_ref,
+    tile, user_blocks, item_blocks, obs_slots,
+    meta_ref,
+    s_ref, m_ref, d_ref, lab_ref, prop_ref, up_ref, ui_ref, vp_ref, vi_ref,
     user_out, item_out,
     g_acc, h_acc, user_acc, item_acc,
 ):
     n_blocks = user_blocks * item_blocks
+    origins = meta_ref.shape[0]
     for k in range(n_blocks):
-        g_acc[k] = count_ref[k] * d_ref[k].astype(jnp.float32)
+        count = meta_ref[0, k]
+        for origin in range(1, origins):
+            count = count + meta_ref[origin, k]
+        g_acc[k] = count.astype(jnp.float32) * d_ref[k].astype(jnp.float32)
         h_acc[k] = jnp.zeros((tile, tile), jnp.float32)
 
     def observed(t, carry):
-        pos = pos_ref[t]
-        valid = valid_ref[t]
+        origin = t // obs_slots
+        slot = t % obs_slots
+        pos = meta_ref[origin, n_blocks + slot]
+        valid = meta_ref[origin, n_blocks + obs_slots + slot].astype(jnp.float32)
         ologits = s_ref[pos]
         predicted = jax.nn.sigmoid(ologits)
         imputes = jax.nn.sigmoid(m_ref[pos])
-        origin = t // obs_slots
-        slot = t % obs_slots
-        labels = got_ref[origin, pl.ds(slot * tile, tile), :].astype(jnp.float32)
-        propens = got_ref[origin, pl.ds((obs_slots + slot) * tile, tile), :].astype(jnp.float32)
+        labels = lab_ref[origin, pl.ds(slot * tile, tile), :].astype(jnp.float32)
+        propens = prop_ref[origin, pl.ds(slot * tile, tile), :].astype(jnp.float32)
         seen = (labels > 0).astype(jnp.float32)
         clicks = (labels == 2).astype(jnp.float32)
         weight = valid * seen / propens
@@ -123,7 +189,7 @@
         h_acc[pos] += ohgrads.astype(jnp.float32)
         return carry
 
-    lax.fori_loop(0, n_tiles, observed, 0)
+    lax.fori_loop(0, origins * obs_slots, observed, 0)
 
     user_acc[...] = jnp.zeros(user_acc.shape, jnp.float32)
     item_acc[...] = jnp.zeros(item_acc.shape, jnp.float32)
@@ -179,22 +245,18 @@
     obs_slots = obs_user.shape[-1] // item_ways
 
     uno_pos = (uno_user * item_blocks + uno_item).reshape(item_ways, -1)
-    uno_counts = jnp.sum(
-        (uno_pos[:, :, None] == jnp.arange(n_blocks, dtype=jnp.int32)).astype(jnp.float32), axis=1
-    )
+    uno_counts = jnp.sum((uno_pos[:, :, None] == jnp.arange(n_blocks, dtype=jnp.int32)).astype(jnp.int32), axis=1)
     obs_pos = (obs_user * item_blocks + obs_item).reshape(item_ways, obs_slots)
     place = jnp.arange(obs_slots, dtype=jnp.int32)
-    valid = (place[None, :] < obs_count.reshape(item_ways, 1)).astype(jnp.float32)
-    meta = jnp.zeros((item_ways, META_ROWS, tile), jnp.float32)
-    meta = meta.at[:, 0, :n_blocks].set(uno_counts)
-    meta = meta.at[:, 1, :obs_slots].set(obs_pos.astype(jnp.float32))
-    meta = meta.at[:, 2, :obs_slots].set(valid)
+    valid = (place[None, :] < obs_count.reshape(item_ways, 1)).astype(jnp.int32)
+    meta = jnp.concatenate(
+        [uno_counts, obs_pos, valid, jnp.zeros((item_ways, tile - n_blocks - 2 * obs_slots), jnp.int32)], axis=1
+    )
     labels = obs_label.reshape(item_ways, obs_slots * tile, tile).astype(jnp.bfloat16)
     propens = obs_prop.reshape(item_ways, obs_slots * tile, tile)
-    package = jnp.concatenate([labels, propens, meta.astype(jnp.bfloat16)], axis=1)
     block_shape = (n_blocks, tile, tile)
-    got, logit_blocks, imputed_blocks, uno_grads = exchange(
-        [(package, "item")],
+    got_labels, got_props, got_meta, logit_blocks, imputed_blocks, uno_grads = exchange(
+        [(labels, "item"), (propens, "item"), (meta, "item")],
         0,
         functools.partial(dense_blocks, tile, item_blocks),
         (user_pred, user_imp, item_pred, item_imp),
@@ -204,20 +266,16 @@
             jax.ShapeDtypeStruct(block_shape, jnp.bfloat16),
         ),
     )
-    got_meta = got[:, 2 * obs_slots * tile :].astype(jnp.float32)
-    counts = jnp.sum(got_meta[:, 0, :n_blocks], axis=0)
-    tile_pos = got_meta[:, 1, :obs_slots].reshape(-1).astype(jnp.int32)
-    tile_valid = got_meta[:, 2, :obs_slots].reshape(-1)
 
     vmem = pl.BlockSpec(memory_space=pltpu.VMEM)
     smem = pl.BlockSpec(memory_space=pltpu.SMEM)
     user_chunks, item_chunks = pl.pallas_call(
-        functools.partial(tile_kernel, tile, user_blocks, item_blocks, item_ways * obs_slots, obs_slots),
+        functools.partial(tile_kernel, tile, user_blocks, item_blocks, obs_slots),
         out_shape=[
             jax.ShapeDtypeStruct((item_ways, 2, user_rows // item_ways, rank), jnp.float32),
             jax.ShapeDtypeStruct((user_ways, 2, shard_rows // user_ways, rank), jnp.float32),
         ],
-        in_specs=[smem] * 3 + [vmem] * 8,
+        in_specs=[smem] + [vmem] * 9,
         out_specs=[vmem, vmem],
         scratch_shapes=[
             pltpu.VMEM((n_blocks, tile, tile), jnp.float32),
@@ -226,12 +284,10 @@
             pltpu.VMEM((2, shard_rows, rank), jnp.float32),
         ],
     )(
-        tile_pos, counts, tile_valid,
-        logit_blocks, imputed_blocks, uno_grads, got, user_pred, user_imp, item_pred, item_imp,
-    )
-    user_got, item_got = exchange([(user_chunks, "item"), (item_chunks, "user")], 1)
-    user_share = jnp.sum(user_got, axis=0)
-    item_share = jnp.sum(item_got, axis=0)
+        got_meta,
+        logit_blocks, imputed_blocks, uno_grads, got_labels, got_props, user_pred, user_imp, item_pred, item_imp,
+    )
+    user_share, item_share = reduce_exchange([(user_chunks, "item"), (item_chunks, "user")], 1)
     return (user_share[0], user_share[1], item_share[0], item_share[1])
 
 

time: 86.7 us -> 85.8 us (0.990)
  other arithmetic: 8.12 us -> 2.91 us
  Pallas kernels: 75 us -> 77.6 us
  local copies, waits for them, and re-layouts: 2.63 us -> 4.38 us
    pallas_call x0 -> x1, Pallas kernels: none -> 34.3 us  [reduce_exchange(): pl.pallas_call(functools.partial(reduce_kernel, axes), out_shape=[jax.Sha...]
    pallas_call x2 -> x1, Pallas kernels: 69.1 us -> 37.4 us  [exchange(): pl.pallas_call(functools.partial(exchange_kernel, axes, len(arrays), len(...]
    convert_element_type x4 -> x1, other arithmetic: 3 us -> 0.01 us  [shards(): valid = (place[None, :] < obs_count.reshape(item_ways, 1)).astype(jnp.int32)]
    unnamed x4 -> x12, local copies, waits for them, and re-layouts: 0.01 us -> 1.96 us
    reduce_sum x3 -> x0, other arithmetic: 1.89 us -> none  [the longest x1 1.33 us: shards(): user_share = jnp.sum(user_got, axis=0)]
where the time goes in v6:
time: 85.8 us; the launch traced here: 85.5 us
  Pallas kernels  77.6 us (90%)
  local copies, waits for them, and re-layouts  4.38 us (5%)
  other arithmetic  2.91 us (3%)
    pallas_call x1, Pallas kernels, exchange(): pl.pallas_call(functools.partial(exchange_kernel, axes, len(arrays), len(...  37.4 us
    pallas_call x1, Pallas kernels, reduce_exchange(): pl.pallas_call(functools.partial(reduce_kernel, axes), out_shape=[jax.Sha...  34.3 us
    pallas_call x1, Pallas kernels, shards(): pl.pallas_call(functools.partial(tile_kernel, tile, user_blocks, item_blo...  5.86 us
    convert_element_type x1, other arithmetic, shards(): obs_label.reshape(item_ways, obs_slots * tile, tile).astype(jnp.bfloat16)  2.12 us
    squeeze x2, local copies, waits for them, and re-layouts, shards(): return (user_share[0], user_share[1], item_share[0], item_share[1])  2.01 us
    unnamed x12, local copies, waits for them, and re-layouts  1.96 us

profile of v6, /device:TPU:1, one launch (start us, length us, event | category | flops | bytes accessed | tf_op | source)
XLA Modules:
  0.0 85.5 jit_solution(1251358503051625058)
XLA Ops:
  0.6 0.0 copy-start.1
  0.6 0.0 copy-start.2
  0.7 0.6 copy-done.1
  1.3 0.0 copy-done.2
  1.3 0.0 copy-start.3
  1.3 0.0 copy-start.4
  1.3 0.6 copy-done.3
  2.0 0.0 copy-done.4
  2.0 0.0 copy-start.5
  2.0 0.6 copy-done.5
  2.6 0.1 pad.3.clone
  2.7 0.1 copy.21
  2.8 0.1 copy.20
  2.9 0.1 eq.15
  3.0 0.1 copy.19
  3.0 0.1 convert_reduce_fusion
  3.1 0.7 add_add_fusion.refs_2_
  3.8 2.1 %convert_bitcast_fusion.refs_0_ = bf16[16,128,128]{2,1,0:T(8,128)(2,1)} fusion(s32[1,1,16,128,128]{4,3,2,1,0:T(8,128)} %param.20), kind=kLoop, calls=%fused_computation | loop fusion | flops 262144 | bytes 1572864 | tf_op jit(solution)/shard_map/convert_element_type | solution.py:255
  5.9 37.4 %shard_map.138 = (bf16[16,128,128]{2,1,0:T(8,128)(2,1)}, bf16[16,128,128]{2,1,0:T(8,128)(2,1)}, s32[16,128]{1,0:T(8,128)}, f32[16,128,128]{2,1,0:T(8,128)}, f32[...) custom-call(bf16[16,128,128]{2,1,0:T(8,128)(2,1)} %convert_bitcast_fusion.refs_0_, bf16[16,128,128]{2,1,0:T(8,128)(2,1)} %bitcast.15, ...), custom_call_target="tpu_custom_call" | custom-call | tf_op jit(solution)/shard_map/pallas_call | solution.py:78
  43.4 5.9 %shard_map.139 = (f32[16,2,64,128]{3,2,1,0:T(8,128)}, f32[16,2,16,128]{3,2,1,0:T(8,128)}) custom-call(s32[16,128]{1,0:T(8,128)} %get-tuple-element.14.meta_ref, f32[16,128,128]{2,1,0:T(8,128)} %get-tuple-element.15.s_ref, f32[16,128,128]{2,1,0:T(8,128)} %get-tuple-element.16.m_ref, bf16[16,128,128]{2,1,0:T(8,128)(2,1)} %get-tuple-element.17.d_ref, ...), custom_call_target="tpu_custom_call" | custom-call | tf_op jit(solution)/shard_map/pallas_call | solution.py:272
  49.2 34.3 %shard_map.140 = (f32[2,64,128]{2,1,0:T(8,128)}, f32[2,16,128]{2,1,0:T(8,128)}) custom-call(f32[16,2,64,128]{3,2,1,0:T(8,128)} %get-tuple-element.20.refs_0_, f32[16,2,16,128]{3,2,1,0:T(8,128)} %get-tuple-element.21.refs_1_), custom_call_target="tpu_custom_call" | custom-call | tf_op jit(solution)/shard_map/pallas_call | solution.py:140
  83.5 0.0 copy-start
  83.5 1.4 %slice_bitcast_fusion = (f32[64,128]{1,0:T(8,128)}, f32[64,128]{1,0:T(8,128)}) fusion(f32[2,64,128]{2,1,0:T(8,128)} %get-tuple-element.22), kind=kLoop, calls=%fused_computation.1 | loop fusion | bytes 131072 | tf_op jit(solution)/shard_map/squeeze | solution.py:291
  84.9 0.0 copy-done
  84.9 0.6 slice_bitcast_fusion.2
  (4 shorter events, 0.0 us)
Async XLA Ops:
  0.6 0.7 copy-start.1
  0.6 0.7 copy-start.2
  1.3 0.7 copy-start.3
  1.3 0.7 copy-start.4
  2.0 0.7 copy-start.5
  83.5 1.4 %copy-start = (f32[2,16,128]{2,1,0:T(8,128)S(1)}, f32[2,16,128]{2,1,0:T(8,128)}, u32[]{:S(2)}) copy-start(f32[2,16,128]{2,1,0:T(8,128)} %get-tuple-element.23) | copy-start | bytes 49156

commit v7 on v6

--- a/solution.py
+++ b/solution.py
@@ -10,6 +10,7 @@
 MESH = pl.DeviceIdType.MESH
 
 loss_weight = 0.015625
+ITEM_RING = 8
 
 
 def product(form, first, second):
@@ -89,67 +90,124 @@
     )(*arrays, *work_inputs)
 
 
-def reduce_kernel(axes, *refs):
-    count = len(axes)
-    x_refs, out_refs = refs[:count], refs[count : 2 * count]
-    land_refs = refs[2 * count : 3 * count]
-    send_sem, recv_sem, local_sem = refs[3 * count :]
+def reduce_kernel(ring, *refs):
+    (user_x, item_x, user_pred_out, user_imp_out, item_pred_out, item_imp_out,
+     own, partner_land, stage, ring_land, item_land, send_sem, recv_sem, local_sem) = refs
+    item_n = lax.axis_size("item")
+    user_n = lax.axis_size("user")
+    me = lax.axis_index("item")
+    me_user = lax.axis_index("user")
+    layer = me // ring
+    spot = me % ring
+    layers = item_n // ring
     barrier = pltpu.get_barrier_semaphore()
-    for axis in axes:
-        n = lax.axis_size(axis)
-        me = lax.axis_index(axis)
-        for k in range(1, n):
-            pl.semaphore_signal(barrier, inc=1, device_id={axis: lax.rem(me + k, n)}, device_id_type=MESH)
-    pl.semaphore_wait(barrier, sum(lax.axis_size(axis) - 1 for axis in axes))
-    copies = []
-    slot = 0
-    for which, axis in enumerate(axes):
-        n = lax.axis_size(axis)
-        me = lax.axis_index(axis)
-        x_ref, land = x_refs[which], land_refs[which]
-        local = pltpu.make_async_copy(x_ref.at[me], land.at[me], local_sem.at[which])
-        local.start()
-        copies.append(local)
-        for k in range(1, n):
-            peer = lax.rem(me + k, n)
-            copy = pltpu.make_async_remote_copy(
-                src_ref=x_ref.at[peer],
-                dst_ref=land.at[me],
-                send_sem=send_sem.at[slot],
-                recv_sem=recv_sem.at[slot],
-                device_id={axis: peer},
-                device_id_type=MESH,
-            )
-            copy.start()
-            copies.append(copy)
-            slot += 1
-    for copy in copies:
+    for k in range(1, layers):
+        pl.semaphore_signal(barrier, inc=1, device_id={"item": lax.rem(me + k * ring, item_n)}, device_id_type=MESH)
+    for k in range(1, ring):
+        pl.semaphore_signal(
+            barrier, inc=1, device_id={"item": layer * ring + lax.rem(spot + k, ring)}, device_id_type=MESH
+        )
+    for k in range(1, user_n):
+        pl.semaphore_signal(barrier, inc=1, device_id={"user": lax.rem(me_user + k, user_n)}, device_id_type=MESH)
+    pl.semaphore_wait(barrier, (layers - 1) + (ring - 1) + (user_n - 1))
+
+    item_copies = []
+    local_item = pltpu.make_async_copy(item_x.at[me_user], item_land.at[me_user], local_sem.at[0])
+    local_item.start()
+    item_copies.append(local_item)
+    for k in range(1, user_n):
+        peer = lax.rem(me_user + k, user_n)
+        copy = pltpu.make_async_remote_copy(
+            src_ref=item_x.at[peer],
+            dst_ref=item_land.at[me_user],
+            send_sem=send_sem.at[k - 1],
+            recv_sem=recv_sem.at[k - 1],
+            device_id={"user": peer},
+            device_id_type=MESH,
+        )
+        copy.start()
+        item_copies.append(copy)
+    base = user_n - 1
+
+    local_own = pltpu.make_async_copy(user_x.at[pl.ds(layer * ring, ring)], own, local_sem.at[1])
+    local_own.start()
+    layer_copies = []
+    for k in range(1, layers):
+        other = lax.rem(layer + k, layers)
+        copy = pltpu.make_async_remote_copy(
+            src_ref=user_x.at[pl.ds(other * ring, ring)],
+            dst_ref=partner_land.at[k - 1],
+            send_sem=send_sem.at[base + k - 1],
+            recv_sem=recv_sem.at[base + k - 1],
+            device_id={"item": other * ring + spot},
+            device_id_type=MESH,
+        )
+        copy.start()
+        layer_copies.append(copy)
+    base += layers - 1
+    local_own.wait()
+    for copy in layer_copies:
         copy.wait()
-    for which in range(count):
-        land = land_refs[which]
-        total = land[0]
-        for source in range(1, land.shape[0]):
-            total = total + land[source]
-        out_refs[which][...] = total
-
-
-def reduce_exchange(pairs, collective):
-    axes = tuple(axis for _, axis in pairs)
-    arrays = [x for x, _ in pairs]
-    slots = sum(lax.axis_size(axis) - 1 for axis in axes)
+    total = own[...]
+    for k in range(layers - 1):
+        total = total + partner_land[k]
+    stage[...] = total
+
+    ring_copies = []
+    for k in range(1, ring):
+        peer = lax.rem(spot + k, ring)
+        copy = pltpu.make_async_remote_copy(
+            src_ref=stage.at[peer],
+            dst_ref=ring_land.at[spot],
+            send_sem=send_sem.at[base + k - 1],
+            recv_sem=recv_sem.at[base + k - 1],
+            device_id={"item": layer * ring + peer},
+            device_id_type=MESH,
+        )
+        copy.start()
+        ring_copies.append(copy)
+    for copy in ring_copies:
+        copy.wait()
+    user_total = stage[spot]
+    for k in range(1, ring):
+        user_total = user_total + ring_land[lax.rem(spot + k, ring)]
+    user_pred_out[...] = user_total[0]
+    user_imp_out[...] = user_total[1]
+
+    for copy in item_copies:
+        copy.wait()
+    item_total = item_land[0]
+    for source in range(1, user_n):
+        item_total = item_total + item_land[source]
+    item_pred_out[...] = item_total[0]
+    item_imp_out[...] = item_total[1]
+
+
+def reduce_exchange(user_x, item_x, ring):
+    item_n = lax.axis_size("item")
+    user_n = lax.axis_size("user")
+    layers = item_n // ring
+    slots = (user_n - 1) + (layers - 1) + (ring - 1)
+    layer_shape = (ring,) + user_x.shape[1:]
+    vmem = pl.BlockSpec(memory_space=pltpu.VMEM)
     return pl.pallas_call(
-        functools.partial(reduce_kernel, axes),
-        out_shape=[jax.ShapeDtypeStruct(x.shape[1:], x.dtype) for x in arrays],
-        in_specs=[pl.BlockSpec(memory_space=pl.ANY)] * len(arrays),
-        out_specs=[pl.BlockSpec(memory_space=pltpu.VMEM)] * len(arrays),
-        scratch_shapes=[pltpu.VMEM(x.shape, x.dtype) for x in arrays]
-        + [
+        functools.partial(reduce_kernel, ring),
+        out_shape=[jax.ShapeDtypeStruct(user_x.shape[2:], user_x.dtype)] * 2
+        + [jax.ShapeDtypeStruct(item_x.shape[2:], item_x.dtype)] * 2,
+        in_specs=[pl.BlockSpec(memory_space=pl.ANY)] * 2,
+        out_specs=[vmem] * 4,
+        scratch_shapes=[
+            pltpu.VMEM(layer_shape, user_x.dtype),
+            pltpu.VMEM((layers - 1,) + layer_shape, user_x.dtype),
+            pltpu.VMEM(layer_shape, user_x.dtype),
+            pltpu.VMEM(layer_shape, user_x.dtype),
+            pltpu.VMEM(item_x.shape, item_x.dtype),
             pltpu.SemaphoreType.DMA((slots,)),
             pltpu.SemaphoreType.DMA((slots,)),
-            pltpu.SemaphoreType.DMA((len(arrays),)),
+            pltpu.SemaphoreType.DMA((2,)),
         ],
-        compiler_params=pltpu.CompilerParams(collective_id=collective, has_side_effects=True),
-    )(*arrays)
+        compiler_params=pltpu.CompilerParams(collective_id=1, has_side_effects=True),
+    )(user_x, item_x)
 
 
 def tile_kernel(
@@ -287,8 +345,8 @@
         got_meta,
         logit_blocks, imputed_blocks, uno_grads, got_labels, got_props, user_pred, user_imp, item_pred, item_imp,
     )
-    user_share, item_share = reduce_exchange([(user_chunks, "item"), (item_chunks, "user")], 1)
-    return (user_share[0], user_share[1], item_share[0], item_share[1])
+    ring = ITEM_RING if item_ways % ITEM_RING == 0 else item_ways
+    return tuple(reduce_exchange(user_chunks, item_chunks, ring))
 
 
 def solution(mesh):

time: 85.8 us -> 90 us (1.049); the launches traced: 85.5 us -> 88.7 us
  Pallas kernels: 77.6 us -> 79.4 us
  local copies, waits for them, and re-layouts: 4.38 us -> 5.75 us
    unnamed x12 -> x20, local copies, waits for them, and re-layouts: 1.96 us -> 5.35 us
    squeeze x2 -> x0, local copies, waits for them, and re-layouts: 2.01 us -> none  [shards(): return (user_share[0], user_share[1], item_share[0], item_share[1])]
    pallas_call x1, Pallas kernels: 34.3 us -> 36.1 us  [reduce_exchange(): pl.pallas_call(functools.partial(reduce_kernel, ring), out_shape=[jax.Sha...]
where the time goes in v7:
time: 90 us; the launch traced here: 88.7 us
  Pallas kernels  79.4 us (88%)
  local copies, waits for them, and re-layouts  5.75 us (6%)
  other arithmetic  2.91 us (3%)
    pallas_call x1, Pallas kernels, exchange(): pl.pallas_call(functools.partial(exchange_kernel, axes, len(arrays), len(...  37.4 us
    pallas_call x1, Pallas kernels, reduce_exchange(): pl.pallas_call(functools.partial(reduce_kernel, ring), out_shape=[jax.Sha...  36.1 us
    pallas_call x1, Pallas kernels, shards(): pl.pallas_call(functools.partial(tile_kernel, tile, user_blocks, item_blo...  5.86 us
    unnamed x20, local copies, waits for them, and re-layouts  5.35 us
    convert_element_type x1, other arithmetic, shards(): obs_label.reshape(item_ways, obs_slots * tile, tile).astype(jnp.bfloat16)  2.12 us

profile of v7, /device:TPU:1, one launch (start us, length us, event | category | flops | bytes accessed | tf_op | source)
XLA Modules:
  0.0 88.7 jit_solution(972113203357891847)
XLA Ops:
  0.6 0.0 copy-start.3
  0.6 0.0 copy-start.4
  0.7 0.6 copy-done.3
  1.3 0.0 copy-done.4
  1.3 0.0 copy-start.5
  1.3 0.0 copy-start.6
  1.3 0.6 copy-done.5
  2.0 0.0 copy-done.6
  2.0 0.0 copy-start.7
  2.0 0.6 copy-done.7
  2.6 0.1 pad.3.clone
  2.7 0.1 copy.21
  2.8 0.1 copy.20
  2.9 0.1 eq.15
  3.0 0.1 copy.19
  3.0 0.1 convert_reduce_fusion
  3.1 0.7 add_add_fusion.refs_2_
  3.8 2.1 %convert_bitcast_fusion.refs_0_ = bf16[16,128,128]{2,1,0:T(8,128)(2,1)} fusion(s32[1,1,16,128,128]{4,3,2,1,0:T(8,128)} %param.20), kind=kLoop, calls=%fused_computation | loop fusion | flops 262144 | bytes 1572864 | tf_op jit(solution)/shard_map/convert_element_type | solution.py:313
  5.9 37.4 %shard_map.138 = (bf16[16,128,128]{2,1,0:T(8,128)(2,1)}, bf16[16,128,128]{2,1,0:T(8,128)(2,1)}, s32[16,128]{1,0:T(8,128)}, f32[16,128,128]{2,1,0:T(8,128)}, f32[...) custom-call(bf16[16,128,128]{2,1,0:T(8,128)(2,1)} %convert_bitcast_fusion.refs_0_, bf16[16,128,128]{2,1,0:T(8,128)(2,1)} %bitcast.7, ...), custom_call_target="tpu_custom_call" | custom-call | tf_op jit(solution)/shard_map/pallas_call | solution.py:79
  43.4 5.9 %shard_map.139 = (f32[16,2,64,128]{3,2,1,0:T(8,128)}, f32[16,2,16,128]{3,2,1,0:T(8,128)}) custom-call(s32[16,128]{1,0:T(8,128)} %get-tuple-element.12.meta_ref, f32[16,128,128]{2,1,0:T(8,128)} %get-tuple-element.13.s_ref, f32[16,128,128]{2,1,0:T(8,128)} %get-tuple-element.14.m_ref, bf16[16,128,128]{2,1,0:T(8,128)(2,1)} %get-tuple-element.15.d_ref, ...), custom_call_target="tpu_custom_call" | custom-call | tf_op jit(solution)/shard_map/pallas_call | solution.py:330
  49.2 36.1 %shard_map.140 = (f32[64,128]{1,0:T(8,128)}, f32[64,128]{1,0:T(8,128)}, f32[16,128]{1,0:T(8,128)}, f32[16,128]{1,0:T(8,128)}) custom-call(f32[16,2,64,128]{3,2,1,0:T(8,128)} %get-tuple-element.18.refs_0_, f32[16,2,16,128]{3,2,1,0:T(8,128)} %get-tuple-element.19.refs_1_), custom_call_target="tpu_custom_call" | custom-call | tf_op jit(solution)/shard_map/pallas_call | solution.py:193
  85.3 0.0 copy-start
  85.3 1.4 %copy.26 = f32[64,128]{1,0:T(8,128)} copy(f32[64,128]{1,0:T(8,128)} %get-tuple-element.24) | data formatting | bytes 65536
  86.7 0.0 copy-done
  86.7 0.0 copy-start.2
  86.7 0.6 copy.27
  87.3 0.1 copy-done.2
  87.4 0.0 copy-start.1
  87.4 0.6 copy.28
  88.0 0.1 copy-done.1
  88.1 0.6 copy.29
  (4 shorter events, 0.0 us)
Async XLA Ops:
  0.6 0.7 copy-start.3
  0.6 0.7 copy-start.4
  1.3 0.7 copy-start.5
  1.3 0.7 copy-start.6
  2.0 0.7 copy-start.7
  85.3 1.4 %copy-start = (f32[64,128]{1,0:T(8,128)S(1)}, f32[64,128]{1,0:T(8,128)}, u32[]{:S(2)}) copy-start(f32[64,128]{1,0:T(8,128)} %get-tuple-element.25) | copy-start | bytes 98308
  86.7 0.7 copy-start.2
  87.4 0.7 copy-start.1

commit v8 on v6

--- a/solution.py
+++ b/solution.py
@@ -155,11 +155,12 @@
 def tile_kernel(
     tile, user_blocks, item_blocks, obs_slots,
     meta_ref,
-    s_ref, m_ref, d_ref, lab_ref, prop_ref, up_ref, ui_ref, vp_ref, vi_ref,
+    lab_ref, prop_ref, up_ref, ui_ref, vp_ref, vi_ref,
     user_out, item_out,
-    g_acc, h_acc, user_acc, item_acc,
+    s_ref, m_ref, d_ref, g_acc, h_acc, user_acc, item_acc,
 ):
     n_blocks = user_blocks * item_blocks
+    dense_blocks(tile, item_blocks, up_ref, ui_ref, vp_ref, vi_ref, s_ref, m_ref, d_ref)
     origins = meta_ref.shape[0]
     for k in range(n_blocks):
         count = meta_ref[0, k]
@@ -254,18 +255,7 @@
     )
     labels = obs_label.reshape(item_ways, obs_slots * tile, tile).astype(jnp.bfloat16)
     propens = obs_prop.reshape(item_ways, obs_slots * tile, tile)
-    block_shape = (n_blocks, tile, tile)
-    got_labels, got_props, got_meta, logit_blocks, imputed_blocks, uno_grads = exchange(
-        [(labels, "item"), (propens, "item"), (meta, "item")],
-        0,
-        functools.partial(dense_blocks, tile, item_blocks),
-        (user_pred, user_imp, item_pred, item_imp),
-        (
-            jax.ShapeDtypeStruct(block_shape, jnp.float32),
-            jax.ShapeDtypeStruct(block_shape, jnp.float32),
-            jax.ShapeDtypeStruct(block_shape, jnp.bfloat16),
-        ),
-    )
+    got_labels, got_props, got_meta = exchange([(labels, "item"), (propens, "item"), (meta, "item")], 0)
 
     vmem = pl.BlockSpec(memory_space=pltpu.VMEM)
     smem = pl.BlockSpec(memory_space=pltpu.SMEM)
@@ -275,17 +265,19 @@
             jax.ShapeDtypeStruct((item_ways, 2, user_rows // item_ways, rank), jnp.float32),
             jax.ShapeDtypeStruct((user_ways, 2, shard_rows // user_ways, rank), jnp.float32),
         ],
-        in_specs=[smem] + [vmem] * 9,
+        in_specs=[smem] + [vmem] * 6,
         out_specs=[vmem, vmem],
         scratch_shapes=[
+            pltpu.VMEM((n_blocks, tile, tile), jnp.float32),
+            pltpu.VMEM((n_blocks, tile, tile), jnp.float32),
+            pltpu.VMEM((n_blocks, tile, tile), jnp.bfloat16),
             pltpu.VMEM((n_blocks, tile, tile), jnp.float32),
             pltpu.VMEM((n_blocks, tile, tile), jnp.float32),
             pltpu.VMEM((2, user_rows, rank), jnp.float32),
             pltpu.VMEM((2, shard_rows, rank), jnp.float32),
         ],
     )(
-        got_meta,
-        logit_blocks, imputed_blocks, uno_grads, got_labels, got_props, user_pred, user_imp, item_pred, item_imp,
+        got_meta, got_labels, got_props, user_pred, user_imp, item_pred, item_imp,
     )
     user_share, item_share = reduce_exchange([(user_chunks, "item"), (item_chunks, "user")], 1)
     return (user_share[0], user_share[1], item_share[0], item_share[1])

time: 85.8 us -> 85.5 us (level)
    pallas_call x1, Pallas kernels: 37.4 us -> 34.7 us  [exchange(): pl.pallas_call(functools.partial(exchange_kernel, axes, len(arrays), len(...]
    pallas_call x1, Pallas kernels: 5.86 us -> 8.07 us  [shards(): pl.pallas_call(functools.partial(tile_kernel, tile, user_blocks, item_blo...]
where the time goes in v8:
time: 85.5 us; the launch traced here: 85.2 us
  Pallas kernels  77.3 us (90%)
  local copies, waits for them, and re-layouts  4.38 us (5%)
  other arithmetic  2.91 us (3%)
    pallas_call x1, Pallas kernels, exchange(): pl.pallas_call(functools.partial(exchange_kernel, axes, len(arrays), len(...  34.7 us
    pallas_call x1, Pallas kernels, reduce_exchange(): pl.pallas_call(functools.partial(reduce_kernel, axes), out_shape=[jax.Sha...  34.5 us
    pallas_call x1, Pallas kernels, shards(): pl.pallas_call(functools.partial(tile_kernel, tile, user_blocks, item_blo...  8.07 us
    convert_element_type x1, other arithmetic, shards(): obs_label.reshape(item_ways, obs_slots * tile, tile).astype(jnp.bfloat16)  2.12 us
    squeeze x2, local copies, waits for them, and re-layouts, shards(): return (user_share[0], user_share[1], item_share[0], item_share[1])  2.01 us
    unnamed x12, local copies, waits for them, and re-layouts  1.96 us

profile of v8, /device:TPU:1, one launch (start us, length us, event | category | flops | bytes accessed | tf_op | source)
XLA Modules:
  0.0 85.2 jit_solution(16146146754462157204)
XLA Ops:
  0.6 0.0 copy-start.1
  0.6 0.0 copy-start.2
  0.7 0.6 copy-done.1
  1.3 0.0 copy-done.2
  1.3 0.0 copy-start.3
  1.3 0.0 copy-start.4
  1.3 0.6 copy-done.3
  2.0 0.0 copy-done.4
  2.0 0.0 copy-start.5
  2.0 0.6 copy-done.5
  2.6 0.1 pad.3.clone
  2.7 0.1 copy.21
  2.8 0.1 copy.20
  2.9 0.1 eq.15
  3.0 0.1 copy.19
  3.0 0.1 convert_reduce_fusion
  3.1 0.7 add_add_fusion.refs_2_
  3.8 2.1 %convert_bitcast_fusion.refs_0_ = bf16[16,128,128]{2,1,0:T(8,128)(2,1)} fusion(s32[1,1,16,128,128]{4,3,2,1,0:T(8,128)} %param.20), kind=kLoop, calls=%fused_computation | loop fusion | flops 262144 | bytes 1572864 | tf_op jit(solution)/shard_map/convert_element_type | solution.py:256
  5.9 34.7 %shard_map.138 = (bf16[16,128,128]{2,1,0:T(8,128)(2,1)}, bf16[16,128,128]{2,1,0:T(8,128)(2,1)}, s32[16,128]{1,0:T(8,128)}) custom-call(bf16[16,128,128]{2,1,0:T(8,128)(2,1)} %convert_bitcast_fusion.refs_0_, bf16[16,128,128]{2,1,0:T(8,128)(2,1)} %bitcast.15, s32[16,128]{1,0:T(8,128)} %add_add_fusion.refs_2_), custom_call_target="tpu_custom_call" | custom-call | tf_op jit(solution)/shard_map/pallas_call | solution.py:78
  40.6 8.1 %shard_map.139 = (f32[16,2,64,128]{3,2,1,0:T(8,128)}, f32[16,2,16,128]{3,2,1,0:T(8,128)}) custom-call(s32[16,128]{1,0:T(8,128)} %get-tuple-element.11.meta_ref, bf16[16,128,128]{2,1,0:T(8,128)(2,1)} %get-tuple-element.12.lab_ref, bf16[16,128,128]{2,1,0:T(8,128)(2,1)} %get-tuple-element.13.prop_ref, bf16[1024,128]{1,0:T(8,128)(2,1)} %up_ref.1, ...), custom_call_target="tpu_custom_call" | custom-call | tf_op jit(solution)/shard_map/pallas_call | solution.py:262
  48.7 34.5 %shard_map.140 = (f32[2,64,128]{2,1,0:T(8,128)}, f32[2,16,128]{2,1,0:T(8,128)}) custom-call(f32[16,2,64,128]{3,2,1,0:T(8,128)} %get-tuple-element.14.refs_0_, f32[16,2,16,128]{3,2,1,0:T(8,128)} %get-tuple-element.15.refs_1_), custom_call_target="tpu_custom_call" | custom-call | tf_op jit(solution)/shard_map/pallas_call | solution.py:140
  83.2 0.0 copy-start
  83.2 1.4 %slice_bitcast_fusion = (f32[64,128]{1,0:T(8,128)}, f32[64,128]{1,0:T(8,128)}) fusion(f32[2,64,128]{2,1,0:T(8,128)} %get-tuple-element.16), kind=kLoop, calls=%fused_computation.1 | loop fusion | bytes 131072 | tf_op jit(solution)/shard_map/squeeze | solution.py:283
  84.6 0.0 copy-done
  84.6 0.6 slice_bitcast_fusion.2
  (4 shorter events, 0.0 us)
Async XLA Ops:
  0.6 0.7 copy-start.1
  0.6 0.7 copy-start.2
  1.3 0.7 copy-start.3
  1.3 0.7 copy-start.4
  2.0 0.7 copy-start.5
  83.2 1.4 %copy-start = (f32[2,16,128]{2,1,0:T(8,128)S(1)}, f32[2,16,128]{2,1,0:T(8,128)}, u32[]{:S(2)}) copy-start(f32[2,16,128]{2,1,0:T(8,128)} %get-tuple-element.17) | copy-start | bytes 49156

commit v9 on v8

--- a/solution.py
+++ b/solution.py
@@ -14,21 +14,6 @@
 
 def product(form, first, second):
     return jnp.einsum(form, first, second, preferred_element_type=jnp.float32)
-
-
-def dense_blocks(tile, item_blocks, up_ref, ui_ref, vp_ref, vi_ref, s_ref, m_ref, d_ref):
-    def block(k, carry):
-        users = pl.ds(pl.multiple_of((k // item_blocks) * tile, tile), tile)
-        items = pl.ds(pl.multiple_of((k % item_blocks) * tile, tile), tile)
-        dims = (((1,), (1,)), ((), ()))
-        logits = lax.dot_general(up_ref[users, :], vp_ref[items, :], dims, preferred_element_type=jnp.float32)
-        imputed = lax.dot_general(ui_ref[users, :], vi_ref[items, :], dims, preferred_element_type=jnp.float32)
-        s_ref[k] = logits
-        m_ref[k] = imputed
-        d_ref[k] = ((jax.nn.sigmoid(logits) - jax.nn.sigmoid(imputed)) * loss_weight).astype(d_ref.dtype)
-        return carry
-
-    lax.fori_loop(0, s_ref.shape[0], block, 0)
 
 
 def exchange_kernel(axes, count, work_in, work, *refs):
@@ -157,17 +142,47 @@
     meta_ref,
     lab_ref, prop_ref, up_ref, ui_ref, vp_ref, vi_ref,
     user_out, item_out,
-    s_ref, m_ref, d_ref, g_acc, h_acc, user_acc, item_acc,
+    s_ref, m_ref, user_acc, item_acc,
 ):
     n_blocks = user_blocks * item_blocks
-    dense_blocks(tile, item_blocks, up_ref, ui_ref, vp_ref, vi_ref, s_ref, m_ref, d_ref)
     origins = meta_ref.shape[0]
-    for k in range(n_blocks):
+    forward = (((1,), (0,)), ((), ()))
+    backward = (((0,), (0,)), ((), ()))
+    outer = (((1,), (1,)), ((), ()))
+    user_acc[...] = jnp.zeros(user_acc.shape, jnp.float32)
+    item_acc[...] = jnp.zeros(item_acc.shape, jnp.float32)
+
+    def add_products(ub, ib, grads, hgrads, scale):
+        users = pl.ds(pl.multiple_of(ub * tile, tile), tile)
+        items = pl.ds(pl.multiple_of(ib * tile, tile), tile)
+        for model, g, u_ref, v_ref in ((0, grads, up_ref, vp_ref), (1, hgrads, ui_ref, vi_ref)):
+            if g is None:
+                continue
+            user_term = lax.dot_general(g, v_ref[items, :], forward, preferred_element_type=jnp.float32)
+            item_term = lax.dot_general(g, u_ref[users, :], backward, preferred_element_type=jnp.float32)
+            if scale is not None:
+                user_term = scale * user_term
+                item_term = scale * item_term
+            user_acc[model, users, :] += user_term
+            item_acc[model, items, :] += item_term
+
+    def unobserved(k, carry):
+        ub = k // item_blocks
+        ib = k % item_blocks
+        users = pl.ds(pl.multiple_of(ub * tile, tile), tile)
+        items = pl.ds(pl.multiple_of(ib * tile, tile), tile)
+        logits = lax.dot_general(up_ref[users, :], vp_ref[items, :], outer, preferred_element_type=jnp.float32)
+        imputed = lax.dot_general(ui_ref[users, :], vi_ref[items, :], outer, preferred_element_type=jnp.float32)
+        s_ref[k] = logits
+        m_ref[k] = imputed
+        grads = ((jax.nn.sigmoid(logits) - jax.nn.sigmoid(imputed)) * loss_weight).astype(jnp.bfloat16)
         count = meta_ref[0, k]
         for origin in range(1, origins):
             count = count + meta_ref[origin, k]
-        g_acc[k] = count.astype(jnp.float32) * d_ref[k].astype(jnp.float32)
-        h_acc[k] = jnp.zeros((tile, tile), jnp.float32)
+        add_products(ub, ib, grads, None, count.astype(jnp.float32))
+        return carry
+
+    lax.fori_loop(0, n_blocks, unobserved, 0)
 
     def observed(t, carry):
         origin = t // obs_slots
@@ -186,33 +201,11 @@
         ohgrads = (
             2.0 * weight * (imputes - clicks) * ologits * ologits * imputes * (1.0 - imputes) * loss_weight
         ).astype(jnp.bfloat16)
-        g_acc[pos] += ograds.astype(jnp.float32)
-        h_acc[pos] += ohgrads.astype(jnp.float32)
+        add_products(pos // item_blocks, pos % item_blocks, ograds, ohgrads, None)
         return carry
 
     lax.fori_loop(0, origins * obs_slots, observed, 0)
 
-    user_acc[...] = jnp.zeros(user_acc.shape, jnp.float32)
-    item_acc[...] = jnp.zeros(item_acc.shape, jnp.float32)
-    forward = (((1,), (0,)), ((), ()))
-    backward = (((0,), (0,)), ((), ()))
-    for ub in range(user_blocks):
-        users = pl.ds(ub * tile, tile)
-        for ib in range(item_blocks):
-            items = pl.ds(ib * tile, tile)
-            k = ub * item_blocks + ib
-            for model, acc, u_ref, v_ref in ((0, g_acc, up_ref, vp_ref), (1, h_acc, ui_ref, vi_ref)):
-                wide = acc[k]
-                hi = wide.astype(jnp.bfloat16)
-                lo = (wide - hi.astype(jnp.float32)).astype(jnp.bfloat16)
-                v = v_ref[items, :]
-                u = u_ref[users, :]
-                user_acc[model, users, :] += lax.dot_general(
-                    hi, v, forward, preferred_element_type=jnp.float32
-                ) + lax.dot_general(lo, v, forward, preferred_element_type=jnp.float32)
-                item_acc[model, items, :] += lax.dot_general(
-                    hi, u, backward, preferred_element_type=jnp.float32
-                ) + lax.dot_general(lo, u, backward, preferred_element_type=jnp.float32)
     user_rows = user_out.shape[2]
     for dest in range(user_out.shape[0]):
         user_out[dest] = user_acc[:, pl.ds(dest * user_rows, user_rows), :]
@@ -270,9 +263,6 @@
         scratch_shapes=[
             pltpu.VMEM((n_blocks, tile, tile), jnp.float32),
             pltpu.VMEM((n_blocks, tile, tile), jnp.float32),
-            pltpu.VMEM((n_blocks, tile, tile), jnp.bfloat16),
-            pltpu.VMEM((n_blocks, tile, tile), jnp.float32),
-            pltpu.VMEM((n_blocks, tile, tile), jnp.float32),
             pltpu.VMEM((2, user_rows, rank), jnp.float32),
             pltpu.VMEM((2, shard_rows, rank), jnp.float32),
         ],

time: 85.5 us -> 89.7 us (1.049)
  Pallas kernels: 77.3 us -> 81.4 us
    pallas_call x1, Pallas kernels: 8.07 us -> 12.3 us  [shards(): pl.pallas_call(functools.partial(tile_kernel, tile, user_blocks, item_blo...]
where the time goes in v9:
time: 89.7 us; the launch traced here: 89.4 us
  Pallas kernels  81.4 us (91%)
  local copies, waits for them, and re-layouts  4.38 us (5%)
  other arithmetic  2.91 us (3%)
    pallas_call x1, Pallas kernels, exchange(): pl.pallas_call(functools.partial(exchange_kernel, axes, len(arrays), len(...  34.7 us
    pallas_call x1, Pallas kernels, reduce_exchange(): pl.pallas_call(functools.partial(reduce_kernel, axes), out_shape=[jax.Sha...  34.5 us
    pallas_call x1, Pallas kernels, shards(): pl.pallas_call(functools.partial(tile_kernel, tile, user_blocks, item_blo...  12.3 us
    convert_element_type x1, other arithmetic, shards(): obs_label.reshape(item_ways, obs_slots * tile, tile).astype(jnp.bfloat16)  2.12 us
    squeeze x2, local copies, waits for them, and re-layouts, shards(): return (user_share[0], user_share[1], item_share[0], item_share[1])  2.01 us
    unnamed x12, local copies, waits for them, and re-layouts  1.96 us

profile of v9, /device:TPU:1, one launch (start us, length us, event | category | flops | bytes accessed | tf_op | source)
XLA Modules:
  0.0 89.4 jit_solution(9242407830371659685)
XLA Ops:
  0.6 0.0 copy-start.1
  0.6 0.0 copy-start.2
  0.7 0.6 copy-done.1
  1.3 0.0 copy-done.2
  1.3 0.0 copy-start.3
  1.3 0.0 copy-start.4
  1.3 0.6 copy-done.3
  2.0 0.0 copy-done.4
  2.0 0.0 copy-start.5
  2.0 0.6 copy-done.5
  2.6 0.1 pad.3.clone
  2.7 0.1 copy.21
  2.8 0.1 copy.20
  2.9 0.1 eq.15
  3.0 0.1 copy.19
  3.0 0.1 convert_reduce_fusion
  3.1 0.7 add_add_fusion.refs_2_
  3.8 2.1 %convert_bitcast_fusion.refs_0_ = bf16[16,128,128]{2,1,0:T(8,128)(2,1)} fusion(s32[1,1,16,128,128]{4,3,2,1,0:T(8,128)} %param.20), kind=kLoop, calls=%fused_computation | loop fusion | flops 262144 | bytes 1572864 | tf_op jit(solution)/shard_map/convert_element_type | solution.py:249
  5.9 34.7 %shard_map.138 = (bf16[16,128,128]{2,1,0:T(8,128)(2,1)}, bf16[16,128,128]{2,1,0:T(8,128)(2,1)}, s32[16,128]{1,0:T(8,128)}) custom-call(bf16[16,128,128]{2,1,0:T(8,128)(2,1)} %convert_bitcast_fusion.refs_0_, bf16[16,128,128]{2,1,0:T(8,128)(2,1)} %bitcast.15, s32[16,128]{1,0:T(8,128)} %add_add_fusion.refs_2_), custom_call_target="tpu_custom_call" | custom-call | tf_op jit(solution)/shard_map/pallas_call | solution.py:63
  40.6 12.3 %shard_map.139 = (f32[16,2,64,128]{3,2,1,0:T(8,128)}, f32[16,2,16,128]{3,2,1,0:T(8,128)}) custom-call(s32[16,128]{1,0:T(8,128)} %get-tuple-element.11.meta_ref, bf16[16,128,128]{2,1,0:T(8,128)(2,1)} %get-tuple-element.12.lab_ref, bf16[16,128,128]{2,1,0:T(8,128)(2,1)} %get-tuple-element.13.prop_ref, bf16[1024,128]{1,0:T(8,128)(2,1)} %up_ref.1, ...), custom_call_target="tpu_custom_call" | custom-call | tf_op jit(solution)/shard_map/pallas_call | solution.py:255
  52.9 34.5 %shard_map.140 = (f32[2,64,128]{2,1,0:T(8,128)}, f32[2,16,128]{2,1,0:T(8,128)}) custom-call(f32[16,2,64,128]{3,2,1,0:T(8,128)} %get-tuple-element.14.refs_0_, f32[16,2,16,128]{3,2,1,0:T(8,128)} %get-tuple-element.15.refs_1_), custom_call_target="tpu_custom_call" | custom-call | tf_op jit(solution)/shard_map/pallas_call | solution.py:125
  87.4 0.0 copy-start
  87.4 1.4 %slice_bitcast_fusion = (f32[64,128]{1,0:T(8,128)}, f32[64,128]{1,0:T(8,128)}) fusion(f32[2,64,128]{2,1,0:T(8,128)} %get-tuple-element.16), kind=kLoop, calls=%fused_computation.1 | loop fusion | bytes 131072 | tf_op jit(solution)/shard_map/squeeze | solution.py:273
  88.8 0.0 copy-done
  88.8 0.6 slice_bitcast_fusion.2
  (4 shorter events, 0.0 us)
Async XLA Ops:
  0.6 0.7 copy-start.1
  0.6 0.7 copy-start.2
  1.3 0.7 copy-start.3
  1.3 0.7 copy-start.4
  2.0 0.7 copy-start.5
  87.4 1.4 %copy-start = (f32[2,16,128]{2,1,0:T(8,128)S(1)}, f32[2,16,128]{2,1,0:T(8,128)}, u32[]{:S(2)}) copy-start(f32[2,16,128]{2,1,0:T(8,128)} %get-tuple-element.17) | copy-start | bytes 49156

commit v10 on v8

--- a/solution.py
+++ b/solution.py
@@ -31,7 +31,7 @@
     lax.fori_loop(0, s_ref.shape[0], block, 0)
 
 
-def exchange_kernel(axes, count, work_in, work, *refs):
+def exchange_kernel(axes, whole, count, work_in, work, *refs):
     x_refs, y_refs = refs[:count], refs[count + work_in : 2 * count + work_in]
     send_sem, recv_sem, local_sem = refs[-3:]
     work_refs = refs[count : count + work_in] + refs[2 * count + work_in : -3]
@@ -48,13 +48,13 @@
         n = lax.axis_size(axis)
         me = lax.axis_index(axis)
         x_ref, y_ref = x_refs[which], y_refs[which]
-        local = pltpu.make_async_copy(x_ref.at[me], y_ref.at[me], local_sem.at[which])
+        local = pltpu.make_async_copy(x_ref if whole[which] else x_ref.at[me], y_ref.at[me], local_sem.at[which])
         local.start()
         copies.append(local)
         for k in range(1, n):
             peer = lax.rem(me + k, n)
             copy = pltpu.make_async_remote_copy(
-                src_ref=x_ref.at[peer],
+                src_ref=x_ref if whole[which] else x_ref.at[peer],
                 dst_ref=y_ref.at[me],
                 send_sem=send_sem.at[slot],
                 recv_sem=recv_sem.at[slot],
@@ -70,14 +70,16 @@
         copy.wait()
 
 
-def exchange(pairs, collective, work=None, work_inputs=(), work_outputs=()):
+def exchange(pairs, collective, work=None, work_inputs=(), work_outputs=(), whole=None):
     axes = tuple(axis for _, axis in pairs)
     arrays = [x for x, _ in pairs]
+    whole = tuple(whole) if whole is not None else (False,) * len(arrays)
+    shapes = [(lax.axis_size(axis),) + x.shape if w else x.shape for (x, axis), w in zip(pairs, whole)]
     slots = sum(lax.axis_size(axis) - 1 for axis in axes)
     vmem = pl.BlockSpec(memory_space=pltpu.VMEM)
     return pl.pallas_call(
-        functools.partial(exchange_kernel, axes, len(arrays), len(work_inputs), work),
-        out_shape=[jax.ShapeDtypeStruct(x.shape, x.dtype) for x in arrays] + list(work_outputs),
+        functools.partial(exchange_kernel, axes, whole, len(arrays), len(work_inputs), work),
+        out_shape=[jax.ShapeDtypeStruct(shape, x.dtype) for shape, x in zip(shapes, arrays)] + list(work_outputs),
         in_specs=[pl.BlockSpec(memory_space=pl.ANY)] * len(arrays) + [vmem] * len(work_inputs),
         out_specs=[pl.BlockSpec(memory_space=pl.ANY)] * len(arrays) + [vmem] * len(work_outputs),
         scratch_shapes=[
@@ -154,26 +156,42 @@
 
 def tile_kernel(
     tile, user_blocks, item_blocks, obs_slots,
-    meta_ref,
+    uu_ref, ui_idx_ref, ou_ref, oi_ref, oc_ref,
     lab_ref, prop_ref, up_ref, ui_ref, vp_ref, vi_ref,
     user_out, item_out,
+    count_ref, pos_ref, valid_ref,
     s_ref, m_ref, d_ref, g_acc, h_acc, user_acc, item_acc,
 ):
     n_blocks = user_blocks * item_blocks
+    origins = uu_ref.shape[0]
+    shard = lax.axis_index("item")
+    uno_slots = uu_ref.shape[1] // origins
+    for k in range(n_blocks):
+        count_ref[k] = 0
+
+    def tally(t, carry):
+        origin = t // uno_slots
+        slot = shard * uno_slots + t % uno_slots
+        k = uu_ref[origin, slot] * item_blocks + ui_idx_ref[origin, slot]
+        count_ref[k] = count_ref[k] + 1
+        return carry
+
+    lax.fori_loop(0, origins * uno_slots, tally, 0)
+    for t in range(origins * obs_slots):
+        origin, place = t // obs_slots, t % obs_slots
+        slot = shard * obs_slots + place
+        pos_ref[t] = ou_ref[origin, slot] * item_blocks + oi_ref[origin, slot]
+        valid_ref[t] = jnp.where(place < oc_ref[origin, shard], 1.0, 0.0).astype(jnp.float32)
     dense_blocks(tile, item_blocks, up_ref, ui_ref, vp_ref, vi_ref, s_ref, m_ref, d_ref)
-    origins = meta_ref.shape[0]
     for k in range(n_blocks):
-        count = meta_ref[0, k]
-        for origin in range(1, origins):
-            count = count + meta_ref[origin, k]
-        g_acc[k] = count.astype(jnp.float32) * d_ref[k].astype(jnp.float32)
+        g_acc[k] = count_ref[k].astype(jnp.float32) * d_ref[k].astype(jnp.float32)
         h_acc[k] = jnp.zeros((tile, tile), jnp.float32)
 
     def observed(t, carry):
         origin = t // obs_slots
         slot = t % obs_slots
-        pos = meta_ref[origin, n_blocks + slot]
-        valid = meta_ref[origin, n_blocks + obs_slots + slot].astype(jnp.float32)
+        pos = pos_ref[t]
+        valid = valid_ref[t]
         ologits = s_ref[pos]
         predicted = jax.nn.sigmoid(ologits)
         imputes = jax.nn.sigmoid(m_ref[pos])
@@ -245,18 +263,14 @@
     n_blocks = user_blocks * item_blocks
     obs_slots = obs_user.shape[-1] // item_ways
 
-    uno_pos = (uno_user * item_blocks + uno_item).reshape(item_ways, -1)
-    uno_counts = jnp.sum((uno_pos[:, :, None] == jnp.arange(n_blocks, dtype=jnp.int32)).astype(jnp.int32), axis=1)
-    obs_pos = (obs_user * item_blocks + obs_item).reshape(item_ways, obs_slots)
-    place = jnp.arange(obs_slots, dtype=jnp.int32)
-    valid = (place[None, :] < obs_count.reshape(item_ways, 1)).astype(jnp.int32)
-    meta = jnp.concatenate(
-        [uno_counts, obs_pos, valid, jnp.zeros((item_ways, tile - n_blocks - 2 * obs_slots), jnp.int32)], axis=1
-    )
     labels = obs_label.reshape(item_ways, obs_slots * tile, tile).astype(jnp.bfloat16)
     propens = obs_prop.reshape(item_ways, obs_slots * tile, tile)
-    got_labels, got_props, got_meta = exchange([(labels, "item"), (propens, "item"), (meta, "item")], 0)
-
+    indices = [x.reshape(x.shape[-1]) for x in (uno_user, uno_item, obs_user, obs_item, obs_count)]
+    got_labels, got_props, *got_indices = exchange(
+        [(labels, "item"), (propens, "item")] + [(x, "item") for x in indices],
+        0,
+        whole=[False, False] + [True] * len(indices),
+    )
     vmem = pl.BlockSpec(memory_space=pltpu.VMEM)
     smem = pl.BlockSpec(memory_space=pltpu.SMEM)
     user_chunks, item_chunks = pl.pallas_call(
@@ -265,9 +279,12 @@
             jax.ShapeDtypeStruct((item_ways, 2, user_rows // item_ways, rank), jnp.float32),
             jax.ShapeDtypeStruct((user_ways, 2, shard_rows // user_ways, rank), jnp.float32),
         ],
-        in_specs=[smem] + [vmem] * 6,
+        in_specs=[smem] * 5 + [vmem] * 6,
         out_specs=[vmem, vmem],
         scratch_shapes=[
+            pltpu.SMEM((n_blocks,), jnp.int32),
+            pltpu.SMEM((item_ways * obs_slots,), jnp.int32),
+            pltpu.SMEM((item_ways * obs_slots,), jnp.float32),
             pltpu.VMEM((n_blocks, tile, tile), jnp.float32),
             pltpu.VMEM((n_blocks, tile, tile), jnp.float32),
             pltpu.VMEM((n_blocks, tile, tile), jnp.bfloat16),
@@ -277,7 +294,7 @@
             pltpu.VMEM((2, shard_rows, rank), jnp.float32),
         ],
     )(
-        got_meta, got_labels, got_props, user_pred, user_imp, item_pred, item_imp,
+        *got_indices, got_labels, got_props, user_pred, user_imp, item_pred, item_imp,
     )
     user_share, item_share = reduce_exchange([(user_chunks, "item"), (item_chunks, "user")], 1)
     return (user_share[0], user_share[1], item_share[0], item_share[1])

time: 85.5 us -> 86.1 us (level)
  Pallas kernels: 77.3 us -> 81 us
  local copies, waits for them, and re-layouts: 4.38 us -> 2.02 us
    pallas_call x1, Pallas kernels: 34.7 us -> 36.9 us  [exchange(): pl.pallas_call(functools.partial(exchange_kernel, axes, whole, len(arrays...]
    unnamed x12 -> x2, local copies, waits for them, and re-layouts: 1.96 us -> 0.01 us
    pallas_call x1, Pallas kernels: 8.07 us -> 9.22 us  [shards(): pl.pallas_call(functools.partial(tile_kernel, tile, user_blocks, item_blo...]
where the time goes in v10:
time: 86.1 us; the launch traced here: 85.8 us
  Pallas kernels  81 us (94%)
  other arithmetic  2.12 us (2%)
  local copies, waits for them, and re-layouts  2.02 us (2%)
    pallas_call x1, Pallas kernels, exchange(): pl.pallas_call(functools.partial(exchange_kernel, axes, whole, len(arrays...  36.9 us
    pallas_call x1, Pallas kernels, reduce_exchange(): pl.pallas_call(functools.partial(reduce_kernel, axes), out_shape=[jax.Sha...  34.9 us
    pallas_call x1, Pallas kernels, shards(): pl.pallas_call(functools.partial(tile_kernel, tile, user_blocks, item_blo...  9.22 us
    convert_element_type x1, other arithmetic, shards(): obs_label.reshape(item_ways, obs_slots * tile, tile).astype(jnp.bfloat16)  2.12 us
    squeeze x2, local copies, waits for them, and re-layouts, shards(): return (user_share[0], user_share[1], item_share[0], item_share[1])  2.01 us

profile of v10, /device:TPU:1, one launch (start us, length us, event | category | flops | bytes accessed | tf_op | source)
XLA Modules:
  0.0 85.8 jit_solution(2697463285287318683)
XLA Ops:
  0.6 2.1 %convert_bitcast_fusion.refs_0_ = bf16[16,128,128]{2,1,0:T(8,128)(2,1)} fusion(s32[1,1,16,128,128]{4,3,2,1,0:T(8,128)} %param.20), kind=kLoop, calls=%fused_computation | loop fusion | flops 262144 | bytes 1572864 | tf_op jit(solution)/shard_map/convert_element_type | solution.py:266
  2.8 36.9 %shard_map.138 = (bf16[16,128,128]{2,1,0:T(8,128)(2,1)}, bf16[16,128,128]{2,1,0:T(8,128)(2,1)}, s32[16,64]{1,0:T(8,128)}, s32[16,64]{1,0:T(8,128)}, s32[16,16]{1...) custom-call(bf16[16,128,128]{2,1,0:T(8,128)(2,1)} %convert_bitcast_fusion.refs_0_, bf16[16,128,128]{2,1,0:T(8,128)(2,1)} %bitcast.16, ...), custom_call_target="tpu_custom_call" | custom-call | tf_op jit(solution)/shard_map/pallas_call | solution.py:80
  39.6 9.2 %shard_map.139 = (f32[16,2,64,128]{3,2,1,0:T(8,128)}, f32[16,2,16,128]{3,2,1,0:T(8,128)}) custom-call(s32[16,64]{1,0:T(8,128)} %get-tuple-element.15.uu_ref, s32[16,64]{1,0:T(8,128)} %get-tuple-element.16.ui_idx_ref, s32[16,16]{1,0:T(8,128)} %get-tuple-element.17.ou_ref, s32[16,16]{1,0:T(8,128)} %get-tuple-element.18.oi_ref, ...), custom_call_target="tpu_custom_call" | custom-call | tf_op jit(solution)/shard_map/pallas_call | solution.py:276
  48.9 34.9 %shard_map.140 = (f32[2,64,128]{2,1,0:T(8,128)}, f32[2,16,128]{2,1,0:T(8,128)}) custom-call(f32[16,2,64,128]{3,2,1,0:T(8,128)} %get-tuple-element.22.refs_0_, f32[16,2,16,128]{3,2,1,0:T(8,128)} %get-tuple-element.23.refs_1_), custom_call_target="tpu_custom_call" | custom-call | tf_op jit(solution)/shard_map/pallas_call | solution.py:142
  83.8 0.0 copy-start
  83.8 1.4 %slice_bitcast_fusion = (f32[64,128]{1,0:T(8,128)}, f32[64,128]{1,0:T(8,128)}) fusion(f32[2,64,128]{2,1,0:T(8,128)} %get-tuple-element.24), kind=kLoop, calls=%fused_computation.1 | loop fusion | bytes 131072 | tf_op jit(solution)/shard_map/squeeze | solution.py:300
  85.2 0.0 copy-done
  85.2 0.6 slice_bitcast_fusion.2
Async XLA Ops:
  83.8 1.4 %copy-start = (f32[2,16,128]{2,1,0:T(8,128)S(1)}, f32[2,16,128]{2,1,0:T(8,128)}, u32[]{:S(2)}) copy-start(f32[2,16,128]{2,1,0:T(8,128)} %get-tuple-element.25) | copy-start | bytes 49156

commit v11 on v10

--- a/solution.py
+++ b/solution.py
@@ -14,21 +14,6 @@
 
 def product(form, first, second):
     return jnp.einsum(form, first, second, preferred_element_type=jnp.float32)
-
-
-def dense_blocks(tile, item_blocks, up_ref, ui_ref, vp_ref, vi_ref, s_ref, m_ref, d_ref):
-    def block(k, carry):
-        users = pl.ds(pl.multiple_of((k // item_blocks) * tile, tile), tile)
-        items = pl.ds(pl.multiple_of((k % item_blocks) * tile, tile), tile)
-        dims = (((1,), (1,)), ((), ()))
-        logits = lax.dot_general(up_ref[users, :], vp_ref[items, :], dims, preferred_element_type=jnp.float32)
-        imputed = lax.dot_general(ui_ref[users, :], vi_ref[items, :], dims, preferred_element_type=jnp.float32)
-        s_ref[k] = logits
-        m_ref[k] = imputed
-        d_ref[k] = ((jax.nn.sigmoid(logits) - jax.nn.sigmoid(imputed)) * loss_weight).astype(d_ref.dtype)
-        return carry
-
-    lax.fori_loop(0, s_ref.shape[0], block, 0)
 
 
 def exchange_kernel(axes, whole, count, work_in, work, *refs):
@@ -154,61 +139,174 @@
     )(*arrays)
 
 
+def observed_grads(valid, ologits, imputed, labels, propens):
+    predicted = jax.nn.sigmoid(ologits)
+    imputes = jax.nn.sigmoid(imputed)
+    seen = (labels > 0).astype(jnp.float32)
+    clicks = (labels == 2).astype(jnp.float32)
+    weight = valid * seen / propens
+    ograds = ((valid * (predicted - imputes) + weight * (imputes - clicks)) * loss_weight).astype(jnp.bfloat16)
+    ohgrads = (
+        2.0 * weight * (imputes - clicks) * ologits * ologits * imputes * (1.0 - imputes) * loss_weight
+    ).astype(jnp.bfloat16)
+    return ograds, ohgrads
+
+
+def gather_kernel(
+    tile, item_blocks, obs_slots,
+    lab_x, prop_x, uu_x, ui_x, ou_x, oi_x, oc_x, up_ref, uimp_ref, vp_ref, vi_ref,
+    d_out, g_out, h_out, count_out, pos_out,
+    lab_land, prop_land, uu_land, ui_land, ou_land, oi_land, oc_land, s_ref, m_ref,
+    send_sem, recv_sem, local_sem,
+):
+    n = lax.axis_size("item")
+    me = lax.axis_index("item")
+    barrier = pltpu.get_barrier_semaphore()
+    for k in range(1, n):
+        pl.semaphore_signal(barrier, inc=1, device_id={"item": lax.rem(me + k, n)}, device_id_type=MESH)
+    pl.semaphore_wait(barrier, n - 1)
+
+    index_pairs = ((uu_x, uu_land), (ui_x, ui_land), (ou_x, ou_land), (oi_x, oi_land), (oc_x, oc_land))
+    tile_pairs = ((lab_x, lab_land), (prop_x, prop_land))
+
+    def send(which, src, dst, k):
+        copy = pltpu.make_async_remote_copy(
+            src_ref=src,
+            dst_ref=dst,
+            send_sem=send_sem.at[which, k - 1],
+            recv_sem=recv_sem.at[which, k - 1],
+            device_id={"item": lax.rem(me + k, n)},
+            device_id_type=MESH,
+        )
+        copy.start()
+        return copy
+
+    index_copies = []
+    for which, (x, land) in enumerate(index_pairs):
+        local = pltpu.make_async_copy(x, land.at[me], local_sem.at[which])
+        local.start()
+        index_copies.append(local)
+        for k in range(1, n):
+            index_copies.append(send(which, x, land.at[me], k))
+    tile_local = []
+    tile_copies = [[] for _ in range(n)]
+    for which, (x, land) in enumerate(tile_pairs):
+        slot = len(index_pairs) + which
+        local = pltpu.make_async_copy(x.at[me], land.at[me], local_sem.at[slot])
+        local.start()
+        tile_local.append(local)
+        for k in range(1, n):
+            tile_copies[k].append(send(slot, x.at[lax.rem(me + k, n)], land.at[me], k))
+
+    dims = (((1,), (1,)), ((), ()))
+
+    def block(k, carry):
+        users = pl.ds(pl.multiple_of((k // item_blocks) * tile, tile), tile)
+        items = pl.ds(pl.multiple_of((k % item_blocks) * tile, tile), tile)
+        logits = lax.dot_general(up_ref[users, :], vp_ref[items, :], dims, preferred_element_type=jnp.float32)
+        imputed = lax.dot_general(uimp_ref[users, :], vi_ref[items, :], dims, preferred_element_type=jnp.float32)
+        s_ref[k] = logits
+        m_ref[k] = imputed
+        d_out[k] = ((jax.nn.sigmoid(logits) - jax.nn.sigmoid(imputed)) * loss_weight).astype(d_out.dtype)
+        return carry
+
+    lax.fori_loop(0, s_ref.shape[0], block, 0)
+
+    for copy in index_copies:
+        copy.wait()
+    uno_slots = uu_land.shape[1] // n
+
+    def tally(t, carry):
+        origin = t // uno_slots
+        slot = me * uno_slots + t % uno_slots
+        count_out[t] = uu_land[origin, slot] * item_blocks + ui_land[origin, slot]
+        return carry
+
+    lax.fori_loop(0, n * uno_slots, tally, 0)
+
+    def origin_tiles(origin):
+        for place in range(obs_slots):
+            slot = me * obs_slots + place
+            t = origin * obs_slots + place
+            pos = ou_land[origin, slot] * item_blocks + oi_land[origin, slot]
+            pos_out[t] = pos
+            valid = jnp.where(place < oc_land[origin, me], 1.0, 0.0).astype(jnp.float32)
+            labels = lab_land[origin, pl.ds(place * tile, tile), :].astype(jnp.float32)
+            propens = prop_land[origin, pl.ds(place * tile, tile), :].astype(jnp.float32)
+            ograds, ohgrads = observed_grads(valid, s_ref[pos], m_ref[pos], labels, propens)
+            g_out[t] = ograds
+            h_out[t] = ohgrads
+
+    for copy in tile_local:
+        copy.wait()
+    origin_tiles(me)
+    for k in range(1, n):
+        for copy in tile_copies[k]:
+            copy.wait()
+        origin_tiles(lax.rem(me + n - k, n))
+
+
+def exchange_tiles(labels, propens, indices, factors, tile, item_blocks, obs_slots):
+    n = lax.axis_size("item")
+    n_blocks = (factors[0].shape[0] // tile) * item_blocks
+    n_tiles = n * obs_slots
+    vmem = pl.BlockSpec(memory_space=pltpu.VMEM)
+    smem = pl.BlockSpec(memory_space=pltpu.SMEM)
+    anyspace = pl.BlockSpec(memory_space=pl.ANY)
+    return pl.pallas_call(
+        functools.partial(gather_kernel, tile, item_blocks, obs_slots),
+        out_shape=[
+            jax.ShapeDtypeStruct((n_blocks, tile, tile), jnp.bfloat16),
+            jax.ShapeDtypeStruct((n_tiles, tile, tile), jnp.bfloat16),
+            jax.ShapeDtypeStruct((n_tiles, tile, tile), jnp.bfloat16),
+            jax.ShapeDtypeStruct((indices[0].shape[0],), jnp.int32),
+            jax.ShapeDtypeStruct((n_tiles,), jnp.int32),
+        ],
+        in_specs=[anyspace] * 7 + [vmem] * 4,
+        out_specs=[vmem] * 3 + [smem] * 2,
+        scratch_shapes=[
+            pltpu.VMEM((n,) + labels.shape[1:], labels.dtype),
+            pltpu.VMEM((n,) + propens.shape[1:], propens.dtype),
+        ]
+        + [pltpu.SMEM((n,) + x.shape, x.dtype) for x in indices]
+        + [
+            pltpu.VMEM((n_blocks, tile, tile), jnp.float32),
+            pltpu.VMEM((n_blocks, tile, tile), jnp.float32),
+            pltpu.SemaphoreType.DMA((7, n - 1)),
+            pltpu.SemaphoreType.DMA((7, n - 1)),
+            pltpu.SemaphoreType.DMA((7,)),
+        ],
+        compiler_params=pltpu.CompilerParams(collective_id=0, has_side_effects=True),
+    )(labels, propens, *indices, *factors)
+
+
 def tile_kernel(
-    tile, user_blocks, item_blocks, obs_slots,
-    uu_ref, ui_idx_ref, ou_ref, oi_ref, oc_ref,
-    lab_ref, prop_ref, up_ref, ui_ref, vp_ref, vi_ref,
+    tile, user_blocks, item_blocks,
+    slot_ref, pos_ref, d_ref, gt_ref, ht_ref, up_ref, ui_ref, vp_ref, vi_ref,
     user_out, item_out,
-    count_ref, pos_ref, valid_ref,
-    s_ref, m_ref, d_ref, g_acc, h_acc, user_acc, item_acc,
+    count_ref, g_acc, h_acc, user_acc, item_acc,
 ):
     n_blocks = user_blocks * item_blocks
-    origins = uu_ref.shape[0]
-    shard = lax.axis_index("item")
-    uno_slots = uu_ref.shape[1] // origins
     for k in range(n_blocks):
         count_ref[k] = 0
 
     def tally(t, carry):
-        origin = t // uno_slots
-        slot = shard * uno_slots + t % uno_slots
-        k = uu_ref[origin, slot] * item_blocks + ui_idx_ref[origin, slot]
+        k = slot_ref[t]
         count_ref[k] = count_ref[k] + 1
         return carry
 
-    lax.fori_loop(0, origins * uno_slots, tally, 0)
-    for t in range(origins * obs_slots):
-        origin, place = t // obs_slots, t % obs_slots
-        slot = shard * obs_slots + place
-        pos_ref[t] = ou_ref[origin, slot] * item_blocks + oi_ref[origin, slot]
-        valid_ref[t] = jnp.where(place < oc_ref[origin, shard], 1.0, 0.0).astype(jnp.float32)
-    dense_blocks(tile, item_blocks, up_ref, ui_ref, vp_ref, vi_ref, s_ref, m_ref, d_ref)
+    lax.fori_loop(0, slot_ref.shape[0], tally, 0)
     for k in range(n_blocks):
         g_acc[k] = count_ref[k].astype(jnp.float32) * d_ref[k].astype(jnp.float32)
         h_acc[k] = jnp.zeros((tile, tile), jnp.float32)
 
     def observed(t, carry):
-        origin = t // obs_slots
-        slot = t % obs_slots
         pos = pos_ref[t]
-        valid = valid_ref[t]
-        ologits = s_ref[pos]
-        predicted = jax.nn.sigmoid(ologits)
-        imputes = jax.nn.sigmoid(m_ref[pos])
-        labels = lab_ref[origin, pl.ds(slot * tile, tile), :].astype(jnp.float32)
-        propens = prop_ref[origin, pl.ds(slot * tile, tile), :].astype(jnp.float32)
-        seen = (labels > 0).astype(jnp.float32)
-        clicks = (labels == 2).astype(jnp.float32)
-        weight = valid * seen / propens
-        ograds = ((valid * (predicted - imputes) + weight * (imputes - clicks)) * loss_weight).astype(jnp.bfloat16)
-        ohgrads = (
-            2.0 * weight * (imputes - clicks) * ologits * ologits * imputes * (1.0 - imputes) * loss_weight
-        ).astype(jnp.bfloat16)
-        g_acc[pos] += ograds.astype(jnp.float32)
-        h_acc[pos] += ohgrads.astype(jnp.float32)
+        g_acc[pos] += gt_ref[t].astype(jnp.float32)
+        h_acc[pos] += ht_ref[t].astype(jnp.float32)
         return carry
 
-    lax.fori_loop(0, origins * obs_slots, observed, 0)
+    lax.fori_loop(0, gt_ref.shape[0], observed, 0)
 
     user_acc[...] = jnp.zeros(user_acc.shape, jnp.float32)
     item_acc[...] = jnp.zeros(item_acc.shape, jnp.float32)
@@ -266,36 +364,27 @@
     labels = obs_label.reshape(item_ways, obs_slots * tile, tile).astype(jnp.bfloat16)
     propens = obs_prop.reshape(item_ways, obs_slots * tile, tile)
     indices = [x.reshape(x.shape[-1]) for x in (uno_user, uno_item, obs_user, obs_item, obs_count)]
-    got_labels, got_props, *got_indices = exchange(
-        [(labels, "item"), (propens, "item")] + [(x, "item") for x in indices],
-        0,
-        whole=[False, False] + [True] * len(indices),
+    uno_grads, obs_grads, obs_hgrads, counts, tile_pos = exchange_tiles(
+        labels, propens, indices, (user_pred, user_imp, item_pred, item_imp), tile, item_blocks, obs_slots
     )
     vmem = pl.BlockSpec(memory_space=pltpu.VMEM)
     smem = pl.BlockSpec(memory_space=pltpu.SMEM)
     user_chunks, item_chunks = pl.pallas_call(
-        functools.partial(tile_kernel, tile, user_blocks, item_blocks, obs_slots),
+        functools.partial(tile_kernel, tile, user_blocks, item_blocks),
         out_shape=[
             jax.ShapeDtypeStruct((item_ways, 2, user_rows // item_ways, rank), jnp.float32),
             jax.ShapeDtypeStruct((user_ways, 2, shard_rows // user_ways, rank), jnp.float32),
         ],
-        in_specs=[smem] * 5 + [vmem] * 6,
+        in_specs=[smem] * 2 + [vmem] * 7,
         out_specs=[vmem, vmem],
         scratch_shapes=[
             pltpu.SMEM((n_blocks,), jnp.int32),
-            pltpu.SMEM((item_ways * obs_slots,), jnp.int32),
-            pltpu.SMEM((item_ways * obs_slots,), jnp.float32),
-            pltpu.VMEM((n_blocks, tile, tile), jnp.float32),
-            pltpu.VMEM((n_blocks, tile, tile), jnp.float32),
-            pltpu.VMEM((n_blocks, tile, tile), jnp.bfloat16),
             pltpu.VMEM((n_blocks, tile, tile), jnp.float32),
             pltpu.VMEM((n_blocks, tile, tile), jnp.float32),
             pltpu.VMEM((2, user_rows, rank), jnp.float32),
             pltpu.VMEM((2, shard_rows, rank), jnp.float32),
         ],
-    )(
-        *got_indices, got_labels, got_props, user_pred, user_imp, item_pred, item_imp,
-    )
+    )(counts, tile_pos, uno_grads, obs_grads, obs_hgrads, user_pred, user_imp, item_pred, item_imp)
     user_share, item_share = reduce_exchange([(user_chunks, "item"), (item_chunks, "user")], 1)
     return (user_share[0], user_share[1], item_share[0], item_share[1])
 

time: 86.1 us -> 82.7 us (0.961)
  Pallas kernels: 81 us -> 77.6 us
    pallas_call x1, Pallas kernels: 9.22 us -> 4.69 us  [shards(): pl.pallas_call(functools.partial(tile_kernel, tile, user_blocks, item_blo...]
    pallas_call x1, Pallas kernels: 36.9 us -> 38 us  [exchange_tiles(): pl.pallas_call(functools.partial(gather_kernel, tile, item_blocks, obs_sl...]
where the time goes in v11:
time: 82.7 us; the launch traced here: 82.4 us
  Pallas kernels  77.6 us (94%)
  other arithmetic  2.12 us (3%)
  local copies, waits for them, and re-layouts  2.02 us (2%)
    pallas_call x1, Pallas kernels, exchange_tiles(): pl.pallas_call(functools.partial(gather_kernel, tile, item_blocks, obs_sl...  38 us
    pallas_call x1, Pallas kernels, reduce_exchange(): pl.pallas_call(functools.partial(reduce_kernel, axes), out_shape=[jax.Sha...  35 us
    pallas_call x1, Pallas kernels, shards(): pl.pallas_call(functools.partial(tile_kernel, tile, user_blocks, item_blo...  4.69 us
    convert_element_type x1, other arithmetic, shards(): obs_label.reshape(item_ways, obs_slots * tile, tile).astype(jnp.bfloat16)  2.12 us
    squeeze x2, local copies, waits for them, and re-layouts, shards(): return (user_share[0], user_share[1], item_share[0], item_share[1])  2.01 us

profile of v11, /device:TPU:1, one launch (start us, length us, event | category | flops | bytes accessed | tf_op | source)
XLA Modules:
  0.0 82.4 jit_solution(16606883219586508421)
XLA Ops:
  0.6 2.1 %convert_bitcast_fusion.lab_x = bf16[16,128,128]{2,1,0:T(8,128)(2,1)} fusion(s32[1,1,16,128,128]{4,3,2,1,0:T(8,128)} %param.20), kind=kLoop, calls=%fused_computation | loop fusion | flops 262144 | bytes 1572864 | tf_op jit(solution)/shard_map/convert_element_type | solution.py:364
  2.8 38.0 %shard_map.138 = (bf16[16,128,128]{2,1,0:T(8,128)(2,1)}, bf16[16,128,128]{2,1,0:T(8,128)(2,1)}, bf16[16,128,128]{2,1,0:T(8,128)(2,1)}, s32[64]{0:T(128)}, s32[16]{0:T(128)}) custom-call(bf16[16,128,128]{2,1,0:T(8,128)(2,1)} %convert_bitcast_fusion.lab_x, bf16[16,128,128]{2,1,0:T(8,128)(2,1)} %bitcast.16, s32[64]{0:T(128)} %bitcast.17, s32[64]{0:T(128)} %bitcast.18, ...), custom_call_target="tpu_custom_call" | custom-call | tf_op jit(solution)/shard_map/pallas_call | solution.py:256
  40.7 4.7 %shard_map.139 = (f32[16,2,64,128]{3,2,1,0:T(8,128)}, f32[16,2,16,128]{3,2,1,0:T(8,128)}) custom-call(s32[64]{0:T(128)} %get-tuple-element.13.slot_ref, s32[16]{0:T(128)} %get-tuple-element.14.pos_ref, bf16[16,128,128]{2,1,0:T(8,128)(2,1)} %get-tuple-element.15.d_ref, bf16[16,128,128]{2,1,0:T(8,128)(2,1)} %get-tuple-element.16.gt_ref, ...), custom_call_target="tpu_custom_call" | custom-call | tf_op jit(solution)/shard_map/pallas_call | solution.py:372
  45.4 35.0 %shard_map.140 = (f32[2,64,128]{2,1,0:T(8,128)}, f32[2,16,128]{2,1,0:T(8,128)}) custom-call(f32[16,2,64,128]{3,2,1,0:T(8,128)} %get-tuple-element.18.refs_0_, f32[16,2,16,128]{3,2,1,0:T(8,128)} %get-tuple-element.19.refs_1_), custom_call_target="tpu_custom_call" | custom-call | tf_op jit(solution)/shard_map/pallas_call | solution.py:127
  80.4 0.0 copy-start
  80.4 1.4 %slice_bitcast_fusion = (f32[64,128]{1,0:T(8,128)}, f32[64,128]{1,0:T(8,128)}) fusion(f32[2,64,128]{2,1,0:T(8,128)} %get-tuple-element.20), kind=kLoop, calls=%fused_computation.1 | loop fusion | bytes 131072 | tf_op jit(solution)/shard_map/squeeze | solution.py:389
  81.8 0.0 copy-done
  81.8 0.6 slice_bitcast_fusion.2
Async XLA Ops:
  80.4 1.4 %copy-start = (f32[2,16,128]{2,1,0:T(8,128)S(1)}, f32[2,16,128]{2,1,0:T(8,128)}, u32[]{:S(2)}) copy-start(f32[2,16,128]{2,1,0:T(8,128)} %get-tuple-element.21) | copy-start | bytes 49156

commit v12 on v11

--- a/solution.py
+++ b/solution.py
@@ -337,6 +337,21 @@
         item_out[dest] = item_acc[:, pl.ds(dest * item_rows, item_rows), :]
 
 
+def convert_kernel(x_ref, y_ref):
+    y_ref[...] = x_ref[...].astype(y_ref.dtype)
+
+
+def to_bfloat16(x):
+    block = (1,) + x.shape[1:]
+    return pl.pallas_call(
+        convert_kernel,
+        grid=(x.shape[0],),
+        out_shape=jax.ShapeDtypeStruct(x.shape, jnp.bfloat16),
+        in_specs=[pl.BlockSpec(block, lambda i: (i, 0, 0))],
+        out_specs=pl.BlockSpec(block, lambda i: (i, 0, 0)),
+    )(x)
+
+
 def shards(
     user_pred,
     user_imp,
@@ -361,7 +376,7 @@
     n_blocks = user_blocks * item_blocks
     obs_slots = obs_user.shape[-1] // item_ways
 
-    labels = obs_label.reshape(item_ways, obs_slots * tile, tile).astype(jnp.bfloat16)
+    labels = to_bfloat16(obs_label.reshape(item_ways, obs_slots * tile, tile))
     propens = obs_prop.reshape(item_ways, obs_slots * tile, tile)
     indices = [x.reshape(x.shape[-1]) for x in (uno_user, uno_item, obs_user, obs_item, obs_count)]
     uno_grads, obs_grads, obs_hgrads, counts, tile_pos = exchange_tiles(

time: 82.7 us -> 89.8 us (1.086)
  Pallas kernels: 77.6 us -> 86.3 us
  other arithmetic: 2.12 us -> 0 us
    pallas_call x0 -> x1, Pallas kernels: none -> 8.71 us  [to_bfloat16(): pl.pallas_call(convert_kernel, grid=(x.shape[0],), out_shape=jax.ShapeDty...]
    convert_element_type x1 -> x0, other arithmetic: 2.12 us -> none  [shards(): obs_label.reshape(item_ways, obs_slots * tile, tile).astype(jnp.bfloat16)]
where the time goes in v12:
time: 89.8 us; the launch traced here: 89 us
  Pallas kernels  86.3 us (96%)
  local copies, waits for them, and re-layouts  2.02 us (2%)
    pallas_call x1, Pallas kernels, exchange_tiles(): pl.pallas_call(functools.partial(gather_kernel, tile, item_blocks, obs_sl...  38 us
    pallas_call x1, Pallas kernels, reduce_exchange(): pl.pallas_call(functools.partial(reduce_kernel, axes), out_shape=[jax.Sha...  35 us
    pallas_call x1, Pallas kernels, to_bfloat16(): pl.pallas_call(convert_kernel, grid=(x.shape[0],), out_shape=jax.ShapeDty...  8.71 us
    pallas_call x1, Pallas kernels, shards(): pl.pallas_call(functools.partial(tile_kernel, tile, user_blocks, item_blo...  4.69 us
    squeeze x2, local copies, waits for them, and re-layouts, shards(): return (user_share[0], user_share[1], item_share[0], item_share[1])  2.01 us

profile of v12, /device:TPU:1, one launch (start us, length us, event | category | flops | bytes accessed | tf_op | source)
XLA Modules:
  0.0 89.0 jit_solution(1323219137476616135)
XLA Ops:
  0.6 8.7 %shard_map.138.lab_x = bf16[16,128,128]{2,1,0:T(8,128)(2,1)} custom-call(s32[16,128,128]{2,1,0:T(8,128)} %bitcast.15), custom_call_target="tpu_custom_call" | custom-call | tf_op jit(solution)/shard_map/pallas_call | solution.py:346
  9.3 38.0 %shard_map.139 = (bf16[16,128,128]{2,1,0:T(8,128)(2,1)}, bf16[16,128,128]{2,1,0:T(8,128)(2,1)}, bf16[16,128,128]{2,1,0:T(8,128)(2,1)}, s32[64]{0:T(128)}, s32[16]{0:T(128)}) custom-call(bf16[16,128,128]{2,1,0:T(8,128)(2,1)} %shard_map.138.lab_x, bf16[16,128,128]{2,1,0:T(8,128)(2,1)} %bitcast.16, s32[64]{0:T(128)} %bitcast.17, s32[64]{0:T(128)} %bitcast.18, ...), custom_call_target="tpu_custom_call" | custom-call | tf_op jit(solution)/shard_map/pallas_call | solution.py:256
  47.3 4.7 %shard_map.140 = (f32[16,2,64,128]{3,2,1,0:T(8,128)}, f32[16,2,16,128]{3,2,1,0:T(8,128)}) custom-call(s32[64]{0:T(128)} %get-tuple-element.13.slot_ref, s32[16]{0:T(128)} %get-tuple-element.14.pos_ref, bf16[16,128,128]{2,1,0:T(8,128)(2,1)} %get-tuple-element.15.d_ref, bf16[16,128,128]{2,1,0:T(8,128)(2,1)} %get-tuple-element.16.gt_ref, ...), custom_call_target="tpu_custom_call" | custom-call | tf_op jit(solution)/shard_map/pallas_call | solution.py:387
  52.0 35.0 %shard_map.141 = (f32[2,64,128]{2,1,0:T(8,128)}, f32[2,16,128]{2,1,0:T(8,128)}) custom-call(f32[16,2,64,128]{3,2,1,0:T(8,128)} %get-tuple-element.18.refs_0_, f32[16,2,16,128]{3,2,1,0:T(8,128)} %get-tuple-element.19.refs_1_), custom_call_target="tpu_custom_call" | custom-call | tf_op jit(solution)/shard_map/pallas_call | solution.py:127
  87.0 0.0 copy-start
  87.0 1.4 %slice_bitcast_fusion = (f32[64,128]{1,0:T(8,128)}, f32[64,128]{1,0:T(8,128)}) fusion(f32[2,64,128]{2,1,0:T(8,128)} %get-tuple-element.20), kind=kLoop, calls=%fused_computation | loop fusion | bytes 131072 | tf_op jit(solution)/shard_map/squeeze | solution.py:404
  88.4 0.0 copy-done
  88.4 0.6 slice_bitcast_fusion.2
Async XLA Ops:
  87.0 1.4 %copy-start = (f32[2,16,128]{2,1,0:T(8,128)S(1)}, f32[2,16,128]{2,1,0:T(8,128)}, u32[]{:S(2)}) copy-start(f32[2,16,128]{2,1,0:T(8,128)} %get-tuple-element.21) | copy-start | bytes 49156

commit v13 on v11

--- a/solution.py
+++ b/solution.py
@@ -88,7 +88,7 @@
         for k in range(1, n):
             pl.semaphore_signal(barrier, inc=1, device_id={axis: lax.rem(me + k, n)}, device_id_type=MESH)
     pl.semaphore_wait(barrier, sum(lax.axis_size(axis) - 1 for axis in axes))
-    copies = []
+    copies = [[] for _ in axes]
     slot = 0
     for which, axis in enumerate(axes):
         n = lax.axis_size(axis)
@@ -96,7 +96,7 @@
         x_ref, land = x_refs[which], land_refs[which]
         local = pltpu.make_async_copy(x_ref.at[me], land.at[me], local_sem.at[which])
         local.start()
-        copies.append(local)
+        copies[which].append(local)
         for k in range(1, n):
             peer = lax.rem(me + k, n)
             copy = pltpu.make_async_remote_copy(
@@ -108,15 +108,17 @@
                 device_id_type=MESH,
             )
             copy.start()
-            copies.append(copy)
+            copies[which].append(copy)
             slot += 1
-    for copy in copies:
-        copy.wait()
-    for which in range(count):
+    for which, axis in enumerate(axes):
+        n = lax.axis_size(axis)
+        me = lax.axis_index(axis)
         land = land_refs[which]
-        total = land[0]
-        for source in range(1, land.shape[0]):
-            total = total + land[source]
+        copies[which][0].wait()
+        total = land[me]
+        for k in range(1, n):
+            copies[which][k].wait()
+            total = total + land[lax.rem(me + n - k, n)]
         out_refs[which][...] = total
 
 

time: 82.7 us -> 82.7 us (level)
  no operation moved by 1% of the time
where the time goes in v13:
time: 82.7 us; the launch traced here: 82.4 us
  Pallas kernels  77.6 us (94%)
  other arithmetic  2.12 us (3%)
  local copies, waits for them, and re-layouts  2.02 us (2%)
    pallas_call x1, Pallas kernels, exchange_tiles(): pl.pallas_call(functools.partial(gather_kernel, tile, item_blocks, obs_sl...  38 us
    pallas_call x1, Pallas kernels, reduce_exchange(): pl.pallas_call(functools.partial(reduce_kernel, axes), out_shape=[jax.Sha...  35 us
    pallas_call x1, Pallas kernels, shards(): pl.pallas_call(functools.partial(tile_kernel, tile, user_blocks, item_blo...  4.69 us
    convert_element_type x1, other arithmetic, shards(): obs_label.reshape(item_ways, obs_slots * tile, tile).astype(jnp.bfloat16)  2.12 us
    squeeze x2, local copies, waits for them, and re-layouts, shards(): return (user_share[0], user_share[1], item_share[0], item_share[1])  2.01 us

profile of v13, /device:TPU:1, one launch (start us, length us, event | category | flops | bytes accessed | tf_op | source)
XLA Modules:
  0.0 82.4 jit_solution(16308119776085843608)
XLA Ops:
  0.6 2.1 %convert_bitcast_fusion.lab_x = bf16[16,128,128]{2,1,0:T(8,128)(2,1)} fusion(s32[1,1,16,128,128]{4,3,2,1,0:T(8,128)} %param.20), kind=kLoop, calls=%fused_computation | loop fusion | flops 262144 | bytes 1572864 | tf_op jit(solution)/shard_map/convert_element_type | solution.py:366
  2.8 38.0 %shard_map.138 = (bf16[16,128,128]{2,1,0:T(8,128)(2,1)}, bf16[16,128,128]{2,1,0:T(8,128)(2,1)}, bf16[16,128,128]{2,1,0:T(8,128)(2,1)}, s32[64]{0:T(128)}, s32[16]{0:T(128)}) custom-call(bf16[16,128,128]{2,1,0:T(8,128)(2,1)} %convert_bitcast_fusion.lab_x, bf16[16,128,128]{2,1,0:T(8,128)(2,1)} %bitcast.16, s32[64]{0:T(128)} %bitcast.17, s32[64]{0:T(128)} %bitcast.18, ...), custom_call_target="tpu_custom_call" | custom-call | tf_op jit(solution)/shard_map/pallas_call | solution.py:258
  40.7 4.7 %shard_map.139 = (f32[16,2,64,128]{3,2,1,0:T(8,128)}, f32[16,2,16,128]{3,2,1,0:T(8,128)}) custom-call(s32[64]{0:T(128)} %get-tuple-element.13.slot_ref, s32[16]{0:T(128)} %get-tuple-element.14.pos_ref, bf16[16,128,128]{2,1,0:T(8,128)(2,1)} %get-tuple-element.15.d_ref, bf16[16,128,128]{2,1,0:T(8,128)(2,1)} %get-tuple-element.16.gt_ref, ...), custom_call_target="tpu_custom_call" | custom-call | tf_op jit(solution)/shard_map/pallas_call | solution.py:374
  45.4 35.0 %shard_map.140 = (f32[2,64,128]{2,1,0:T(8,128)}, f32[2,16,128]{2,1,0:T(8,128)}) custom-call(f32[16,2,64,128]{3,2,1,0:T(8,128)} %get-tuple-element.18.refs_0_, f32[16,2,16,128]{3,2,1,0:T(8,128)} %get-tuple-element.19.refs_1_), custom_call_target="tpu_custom_call" | custom-call | tf_op jit(solution)/shard_map/pallas_call | solution.py:129
  80.4 0.0 copy-start
  80.4 1.4 %slice_bitcast_fusion = (f32[64,128]{1,0:T(8,128)}, f32[64,128]{1,0:T(8,128)}) fusion(f32[2,64,128]{2,1,0:T(8,128)} %get-tuple-element.20), kind=kLoop, calls=%fused_computation.1 | loop fusion | bytes 131072 | tf_op jit(solution)/shard_map/squeeze | solution.py:391
  81.8 0.0 copy-done
  81.8 0.6 slice_bitcast_fusion.2
Async XLA Ops:
  80.4 1.4 %copy-start = (f32[2,16,128]{2,1,0:T(8,128)S(1)}, f32[2,16,128]{2,1,0:T(8,128)}, u32[]{:S(2)}) copy-start(f32[2,16,128]{2,1,0:T(8,128)} %get-tuple-element.21) | copy-start | bytes 49156

commit v14 on v11

--- a/solution.py
+++ b/solution.py
@@ -155,8 +155,8 @@
 def gather_kernel(
     tile, item_blocks, obs_slots,
     lab_x, prop_x, uu_x, ui_x, ou_x, oi_x, oc_x, up_ref, uimp_ref, vp_ref, vi_ref,
-    d_out, g_out, h_out, count_out, pos_out,
-    lab_land, prop_land, uu_land, ui_land, ou_land, oi_land, oc_land, s_ref, m_ref,
+    user_out, item_out,
+    lab_land, prop_land, uu_land, ui_land, ou_land, oi_land, oc_land, s_ref, m_ref, d_ref, user_acc, item_acc,
     send_sem, recv_sem, local_sem,
 ):
     n = lax.axis_size("item")
@@ -201,41 +201,70 @@
     dims = (((1,), (1,)), ((), ()))
 
     def block(k, carry):
-        users = pl.ds(pl.multiple_of((k // item_blocks) * tile, tile), tile)
-        items = pl.ds(pl.multiple_of((k % item_blocks) * tile, tile), tile)
-        logits = lax.dot_general(up_ref[users, :], vp_ref[items, :], dims, preferred_element_type=jnp.float32)
-        imputed = lax.dot_general(uimp_ref[users, :], vi_ref[items, :], dims, preferred_element_type=jnp.float32)
+        ub = k // item_blocks
+        ib = k % item_blocks
+        logits = lax.dot_general(up_ref[ub], vp_ref[ib], dims, preferred_element_type=jnp.float32)
+        imputed = lax.dot_general(uimp_ref[ub], vi_ref[ib], dims, preferred_element_type=jnp.float32)
         s_ref[k] = logits
         m_ref[k] = imputed
-        d_out[k] = ((jax.nn.sigmoid(logits) - jax.nn.sigmoid(imputed)) * loss_weight).astype(d_out.dtype)
+        d_ref[k] = ((jax.nn.sigmoid(logits) - jax.nn.sigmoid(imputed)) * loss_weight).astype(d_ref.dtype)
         return carry
 
     lax.fori_loop(0, s_ref.shape[0], block, 0)
+    user_acc[...] = jnp.zeros(user_acc.shape, jnp.float32)
+    item_acc[...] = jnp.zeros(item_acc.shape, jnp.float32)
+    forward = (((1,), (0,)), ((), ()))
+    backward = (((0,), (0,)), ((), ()))
+    user_blocks = user_acc.shape[1] // tile
 
     for copy in index_copies:
         copy.wait()
     uno_slots = uu_land.shape[1] // n
-
-    def tally(t, carry):
+    slots = []
+    for t in range(n * uno_slots):
         origin = t // uno_slots
         slot = me * uno_slots + t % uno_slots
-        count_out[t] = uu_land[origin, slot] * item_blocks + ui_land[origin, slot]
-        return carry
-
-    lax.fori_loop(0, n * uno_slots, tally, 0)
+        slots.append(uu_land[origin, slot] * item_blocks + ui_land[origin, slot])
+    for k in range(s_ref.shape[0]):
+        count = jnp.where(slots[0] == k, 1.0, 0.0)
+        for t in range(1, len(slots)):
+            count = count + jnp.where(slots[t] == k, 1.0, 0.0)
+        users = pl.ds((k // item_blocks) * tile, tile)
+        items = pl.ds((k % item_blocks) * tile, tile)
+        grads = d_ref[k]
+        user_acc[0, users, :] += count * lax.dot_general(
+            grads, vp_ref[k % item_blocks], forward, preferred_element_type=jnp.float32
+        )
+        item_acc[0, items, :] += count * lax.dot_general(
+            grads, up_ref[k // item_blocks], backward, preferred_element_type=jnp.float32
+        )
 
     def origin_tiles(origin):
         for place in range(obs_slots):
             slot = me * obs_slots + place
-            t = origin * obs_slots + place
-            pos = ou_land[origin, slot] * item_blocks + oi_land[origin, slot]
-            pos_out[t] = pos
+            ub = ou_land[origin, slot]
+            ib = oi_land[origin, slot]
+            pos = ub * item_blocks + ib
             valid = jnp.where(place < oc_land[origin, me], 1.0, 0.0).astype(jnp.float32)
             labels = lab_land[origin, pl.ds(place * tile, tile), :].astype(jnp.float32)
             propens = prop_land[origin, pl.ds(place * tile, tile), :].astype(jnp.float32)
             ograds, ohgrads = observed_grads(valid, s_ref[pos], m_ref[pos], labels, propens)
-            g_out[t] = ograds
-            h_out[t] = ohgrads
+            terms = []
+            for g, u_ref, v_ref in ((ograds, up_ref, vp_ref), (ohgrads, uimp_ref, vi_ref)):
+                terms.append(
+                    (
+                        lax.dot_general(g, v_ref[ib], forward, preferred_element_type=jnp.float32),
+                        lax.dot_general(g, u_ref[ub], backward, preferred_element_type=jnp.float32),
+                    )
+                )
+            for b in range(user_blocks):
+                hit = jnp.where(ub == b, 1.0, 0.0)
+                for model in range(2):
+                    user_acc[model, pl.ds(b * tile, tile), :] += hit * terms[model][0]
+            for c in range(item_blocks):
+                hit = jnp.where(ib == c, 1.0, 0.0)
+                for model in range(2):
+                    item_acc[model, pl.ds(c * tile, tile), :] += hit * terms[model][1]
 
     for copy in tile_local:
         copy.wait()
@@ -244,11 +273,20 @@
         for copy in tile_copies[k]:
             copy.wait()
         origin_tiles(lax.rem(me + n - k, n))
-
-
-def exchange_tiles(labels, propens, indices, factors, tile, item_blocks, obs_slots):
+    user_rows = user_out.shape[2]
+    for dest in range(user_out.shape[0]):
+        user_out[dest] = user_acc[:, pl.ds(dest * user_rows, user_rows), :]
+    item_rows = item_out.shape[2]
+    for dest in range(item_out.shape[0]):
+        item_out[dest] = item_acc[:, pl.ds(dest * item_rows, item_rows), :]
+
+
+def exchange_tiles(labels, propens, indices, factors, tile, item_blocks, obs_slots, user_ways):
     n = lax.axis_size("item")
-    n_blocks = (factors[0].shape[0] // tile) * item_blocks
+    user_rows, rank = factors[0].shape
+    shard_rows = factors[2].shape[0]
+    factors = [x.reshape(x.shape[0] // tile, tile, rank) for x in factors]
+    n_blocks = factors[0].shape[0] * item_blocks
     n_tiles = n * obs_slots
     vmem = pl.BlockSpec(memory_space=pltpu.VMEM)
     smem = pl.BlockSpec(memory_space=pltpu.SMEM)
@@ -256,14 +294,11 @@
     return pl.pallas_call(
         functools.partial(gather_kernel, tile, item_blocks, obs_slots),
         out_shape=[
-            jax.ShapeDtypeStruct((n_blocks, tile, tile), jnp.bfloat16),
-            jax.ShapeDtypeStruct((n_tiles, tile, tile), jnp.bfloat16),
-            jax.ShapeDtypeStruct((n_tiles, tile, tile), jnp.bfloat16),
-            jax.ShapeDtypeStruct((indices[0].shape[0],), jnp.int32),
-            jax.ShapeDtypeStruct((n_tiles,), jnp.int32),
+            jax.ShapeDtypeStruct((n, 2, user_rows // n, rank), jnp.float32),
+            jax.ShapeDtypeStruct((user_ways, 2, shard_rows // user_ways, rank), jnp.float32),
         ],
         in_specs=[anyspace] * 7 + [vmem] * 4,
-        out_specs=[vmem] * 3 + [smem] * 2,
+        out_specs=[vmem] * 2,
         scratch_shapes=[
             pltpu.VMEM((n,) + labels.shape[1:], labels.dtype),
             pltpu.VMEM((n,) + propens.shape[1:], propens.dtype),
@@ -272,6 +307,9 @@
         + [
             pltpu.VMEM((n_blocks, tile, tile), jnp.float32),
             pltpu.VMEM((n_blocks, tile, tile), jnp.float32),
+            pltpu.VMEM((n_blocks, tile, tile), jnp.bfloat16),
+            pltpu.VMEM((2, user_rows, rank), jnp.float32),
+            pltpu.VMEM((2, shard_rows, rank), jnp.float32),
             pltpu.SemaphoreType.DMA((7, n - 1)),
             pltpu.SemaphoreType.DMA((7, n - 1)),
             pltpu.SemaphoreType.DMA((7,)),
@@ -364,27 +402,9 @@
     labels = obs_label.reshape(item_ways, obs_slots * tile, tile).astype(jnp.bfloat16)
     propens = obs_prop.reshape(item_ways, obs_slots * tile, tile)
     indices = [x.reshape(x.shape[-1]) for x in (uno_user, uno_item, obs_user, obs_item, obs_count)]
-    uno_grads, obs_grads, obs_hgrads, counts, tile_pos = exchange_tiles(
-        labels, propens, indices, (user_pred, user_imp, item_pred, item_imp), tile, item_blocks, obs_slots
+    user_chunks, item_chunks = exchange_tiles(
+        labels, propens, indices, (user_pred, user_imp, item_pred, item_imp), tile, item_blocks, obs_slots, user_ways
     )
-    vmem = pl.BlockSpec(memory_space=pltpu.VMEM)
-    smem = pl.BlockSpec(memory_space=pltpu.SMEM)
-    user_chunks, item_chunks = pl.pallas_call(
-        functools.partial(tile_kernel, tile, user_blocks, item_blocks),
-        out_shape=[
-            jax.ShapeDtypeStruct((item_ways, 2, user_rows // item_ways, rank), jnp.float32),
-            jax.ShapeDtypeStruct((user_ways, 2, shard_rows // user_ways, rank), jnp.float32),
-        ],
-        in_specs=[smem] * 2 + [vmem] * 7,
-        out_specs=[vmem, vmem],
-        scratch_shapes=[
-            pltpu.SMEM((n_blocks,), jnp.int32),
-            pltpu.VMEM((n_blocks, tile, tile), jnp.float32),
-            pltpu.VMEM((n_blocks, tile, tile), jnp.float32),
-            pltpu.VMEM((2, user_rows, rank), jnp.float32),
-            pltpu.VMEM((2, shard_rows, rank), jnp.float32),
-        ],
-    )(counts, tile_pos, uno_grads, obs_grads, obs_hgrads, user_pred, user_imp, item_pred, item_imp)
     user_share, item_share = reduce_exchange([(user_chunks, "item"), (item_chunks, "user")], 1)
     return (user_share[0], user_share[1], item_share[0], item_share[1])
 

time: 82.7 us -> 79.5 us (0.961)
  Pallas kernels: 77.6 us -> 74.4 us
    pallas_call x1 -> x0, Pallas kernels: 4.69 us -> none  [shards(): pl.pallas_call(functools.partial(tile_kernel, tile, user_blocks, item_blo...]
    pallas_call x1, Pallas kernels: 35 us -> 36.2 us  [reduce_exchange(): pl.pallas_call(functools.partial(reduce_kernel, axes), out_shape=[jax.Sha...]
where the time goes in v14:
time: 79.5 us; the launch traced here: 79.2 us
  Pallas kernels  74.4 us (94%)
  other arithmetic  2.15 us (3%)
  local copies, waits for them, and re-layouts  2.02 us (3%)
    pallas_call x1, Pallas kernels, exchange_tiles(): pl.pallas_call(functools.partial(gather_kernel, tile, item_blocks, obs_sl...  38.2 us
    pallas_call x1, Pallas kernels, reduce_exchange(): pl.pallas_call(functools.partial(reduce_kernel, axes), out_shape=[jax.Sha...  36.2 us
    convert_element_type x1, other arithmetic, shards(): obs_label.reshape(item_ways, obs_slots * tile, tile).astype(jnp.bfloat16)  2.15 us
    squeeze x2, local copies, waits for them, and re-layouts, shards(): return (user_share[0], user_share[1], item_share[0], item_share[1])  2.01 us

profile of v14, /device:TPU:1, one launch (start us, length us, event | category | flops | bytes accessed | tf_op | source)
XLA Modules:
  0.0 79.2 jit_solution(3467385705955055709)
XLA Ops:
  0.6 2.1 %convert_bitcast_fusion.lab_x = bf16[16,128,128]{2,1,0:T(8,128)(2,1)} fusion(s32[1,1,16,128,128]{4,3,2,1,0:T(8,128)} %param.20), kind=kLoop, calls=%fused_computation | loop fusion | flops 262144 | bytes 1572864 | tf_op jit(solution)/shard_map/convert_element_type | solution.py:402
  2.8 38.2 %shard_map.138 = (f32[16,2,64,128]{3,2,1,0:T(8,128)}, f32[16,2,16,128]{3,2,1,0:T(8,128)}) custom-call(bf16[16,128,128]{2,1,0:T(8,128)(2,1)} %convert_bitcast_fusion.lab_x, bf16[16,128,128]{2,1,0:T(8,128)(2,1)} %bitcast.20, s32[64]{0:T(128)} %bitcast.25, s32[64]{0:T(128)} %bitcast.26, s32[16]{0:T(128)} %bitcast.27, s32[16]{0:T(128)} %bitcast.28, s32[16]{0:T(128)} %bitcast.29, ...), custom_call_target="tpu_custom_call" | custom-call | tf_op jit(solution)/shard_map/pallas_call | solution.py:294
  41.0 36.2 %shard_map.139 = (f32[2,64,128]{2,1,0:T(8,128)}, f32[2,16,128]{2,1,0:T(8,128)}) custom-call(f32[16,2,64,128]{3,2,1,0:T(8,128)} %get-tuple-element.8.refs_0_, f32[16,2,16,128]{3,2,1,0:T(8,128)} %get-tuple-element.9.refs_1_), custom_call_target="tpu_custom_call" | custom-call | tf_op jit(solution)/shard_map/pallas_call | solution.py:127
  77.2 0.0 copy-start
  77.2 1.4 %slice_bitcast_fusion = (f32[64,128]{1,0:T(8,128)}, f32[64,128]{1,0:T(8,128)}) fusion(f32[2,64,128]{2,1,0:T(8,128)} %get-tuple-element.10), kind=kLoop, calls=%fused_computation.1 | loop fusion | bytes 131072 | tf_op jit(solution)/shard_map/squeeze | solution.py:409
  78.6 0.0 copy-done
  78.6 0.6 slice_bitcast_fusion.2
Async XLA Ops:
  77.2 1.4 %copy-start = (f32[2,16,128]{2,1,0:T(8,128)S(1)}, f32[2,16,128]{2,1,0:T(8,128)}, u32[]{:S(2)}) copy-start(f32[2,16,128]{2,1,0:T(8,128)} %get-tuple-element.11) | copy-start | bytes 49156

commit v15 on v14

--- a/solution.py
+++ b/solution.py
@@ -155,16 +155,20 @@
 def gather_kernel(
     tile, item_blocks, obs_slots,
     lab_x, prop_x, uu_x, ui_x, ou_x, oi_x, oc_x, up_ref, uimp_ref, vp_ref, vi_ref,
-    user_out, item_out,
+    user_pred_out, user_imp_out, item_pred_out, item_imp_out,
     lab_land, prop_land, uu_land, ui_land, ou_land, oi_land, oc_land, s_ref, m_ref, d_ref, user_acc, item_acc,
-    send_sem, recv_sem, local_sem,
+    user_land, item_land, send_sem, recv_sem, local_sem, sum_send, sum_recv, sum_local,
 ):
     n = lax.axis_size("item")
     me = lax.axis_index("item")
     barrier = pltpu.get_barrier_semaphore()
+    user_n = lax.axis_size("user")
+    me_user = lax.axis_index("user")
     for k in range(1, n):
         pl.semaphore_signal(barrier, inc=1, device_id={"item": lax.rem(me + k, n)}, device_id_type=MESH)
-    pl.semaphore_wait(barrier, n - 1)
+    for k in range(1, user_n):
+        pl.semaphore_signal(barrier, inc=1, device_id={"user": lax.rem(me_user + k, user_n)}, device_id_type=MESH)
+    pl.semaphore_wait(barrier, (n - 1) + (user_n - 1))
 
     index_pairs = ((uu_x, uu_land), (ui_x, ui_land), (ou_x, ou_land), (oi_x, oi_land), (oc_x, oc_land))
     tile_pairs = ((lab_x, lab_land), (prop_x, prop_land))
@@ -273,12 +277,36 @@
         for copy in tile_copies[k]:
             copy.wait()
         origin_tiles(lax.rem(me + n - k, n))
-    user_rows = user_out.shape[2]
-    for dest in range(user_out.shape[0]):
-        user_out[dest] = user_acc[:, pl.ds(dest * user_rows, user_rows), :]
-    item_rows = item_out.shape[2]
-    for dest in range(item_out.shape[0]):
-        item_out[dest] = item_acc[:, pl.ds(dest * item_rows, item_rows), :]
+    sums = []
+    for which, (acc, land, axis, me_at, size) in enumerate(
+        ((user_acc, user_land, "item", me, n), (item_acc, item_land, "user", me_user, user_n))
+    ):
+        rows = land.shape[2]
+        local = pltpu.make_async_copy(acc.at[:, pl.ds(me_at * rows, rows), :], land.at[me_at], sum_local.at[which])
+        local.start()
+        copies = [local]
+        for k in range(1, size):
+            peer = lax.rem(me_at + k, size)
+            copy = pltpu.make_async_remote_copy(
+                src_ref=acc.at[:, pl.ds(peer * rows, rows), :],
+                dst_ref=land.at[me_at],
+                send_sem=sum_send.at[which, k - 1],
+                recv_sem=sum_recv.at[which, k - 1],
+                device_id={axis: peer},
+                device_id_type=MESH,
+            )
+            copy.start()
+            copies.append(copy)
+        sums.append(copies)
+    for copies in sums:
+        for copy in copies:
+            copy.wait()
+    for land, outs in ((user_land, (user_pred_out, user_imp_out)), (item_land, (item_pred_out, item_imp_out))):
+        total = land[0]
+        for source in range(1, land.shape[0]):
+            total = total + land[source]
+        outs[0][...] = total[0]
+        outs[1][...] = total[1]
 
 
 def exchange_tiles(labels, propens, indices, factors, tile, item_blocks, obs_slots, user_ways):
@@ -293,12 +321,10 @@
     anyspace = pl.BlockSpec(memory_space=pl.ANY)
     return pl.pallas_call(
         functools.partial(gather_kernel, tile, item_blocks, obs_slots),
-        out_shape=[
-            jax.ShapeDtypeStruct((n, 2, user_rows // n, rank), jnp.float32),
-            jax.ShapeDtypeStruct((user_ways, 2, shard_rows // user_ways, rank), jnp.float32),
-        ],
+        out_shape=[jax.ShapeDtypeStruct((user_rows // n, rank), jnp.float32)] * 2
+        + [jax.ShapeDtypeStruct((shard_rows // user_ways, rank), jnp.float32)] * 2,
         in_specs=[anyspace] * 7 + [vmem] * 4,
-        out_specs=[vmem] * 2,
+        out_specs=[vmem] * 4,
         scratch_shapes=[
             pltpu.VMEM((n,) + labels.shape[1:], labels.dtype),
             pltpu.VMEM((n,) + propens.shape[1:], propens.dtype),
@@ -310,9 +336,14 @@
             pltpu.VMEM((n_blocks, tile, tile), jnp.bfloat16),
             pltpu.VMEM((2, user_rows, rank), jnp.float32),
             pltpu.VMEM((2, shard_rows, rank), jnp.float32),
+            pltpu.VMEM((n, 2, user_rows // n, rank), jnp.float32),
+            pltpu.VMEM((user_ways, 2, shard_rows // user_ways, rank), jnp.float32),
             pltpu.SemaphoreType.DMA((7, n - 1)),
             pltpu.SemaphoreType.DMA((7, n - 1)),
             pltpu.SemaphoreType.DMA((7,)),
+            pltpu.SemaphoreType.DMA((2, max(n, user_ways) - 1)),
+            pltpu.SemaphoreType.DMA((2, max(n, user_ways) - 1)),
+            pltpu.SemaphoreType.DMA((2,)),
         ],
         compiler_params=pltpu.CompilerParams(collective_id=0, has_side_effects=True),
     )(labels, propens, *indices, *factors)
@@ -402,11 +433,12 @@
     labels = obs_label.reshape(item_ways, obs_slots * tile, tile).astype(jnp.bfloat16)
     propens = obs_prop.reshape(item_ways, obs_slots * tile, tile)
     indices = [x.reshape(x.shape[-1]) for x in (uno_user, uno_item, obs_user, obs_item, obs_count)]
-    user_chunks, item_chunks = exchange_tiles(
-        labels, propens, indices, (user_pred, user_imp, item_pred, item_imp), tile, item_blocks, obs_slots, user_ways
+    return tuple(
+        exchange_tiles(
+            labels, propens, indices, (user_pred, user_imp, item_pred, item_imp), tile, item_blocks, obs_slots,
+            user_ways,
+        )
     )
-    user_share, item_share = reduce_exchange([(user_chunks, "item"), (item_chunks, "user")], 1)
-    return (user_share[0], user_share[1], item_share[0], item_share[1])
 
 
 def solution(mesh):

time: 79.5 us -> 71.7 us (0.902)
  Pallas kernels: 74.4 us -> 65.3 us
  local copies, waits for them, and re-layouts: 2.02 us -> 3.39 us
    pallas_call x1 -> x0, Pallas kernels: 36.2 us -> none  [reduce_exchange(): pl.pallas_call(functools.partial(reduce_kernel, axes), out_shape=[jax.Sha...]
    pallas_call x1, Pallas kernels: 38.2 us -> 65.3 us  [exchange_tiles(): pl.pallas_call(functools.partial(gather_kernel, tile, item_blocks, obs_sl...]
    unnamed x2 -> x10, local copies, waits for them, and re-layouts: 0.01 us -> 3.39 us
    squeeze x2 -> x0, local copies, waits for them, and re-layouts: 2.01 us -> none  [shards(): return (user_share[0], user_share[1], item_share[0], item_share[1])]
where the time goes in v15:
time: 71.7 us; the launch traced here: 71.4 us
  Pallas kernels  65.3 us (91%)
  local copies, waits for them, and re-layouts  3.39 us (5%)
  other arithmetic  2.13 us (3%)
    pallas_call x1, Pallas kernels, exchange_tiles(): pl.pallas_call(functools.partial(gather_kernel, tile, item_blocks, obs_sl...  65.3 us
    unnamed x10, local copies, waits for them, and re-layouts  3.39 us
    convert_element_type x1, other arithmetic, shards(): obs_label.reshape(item_ways, obs_slots * tile, tile).astype(jnp.bfloat16)  2.13 us

profile of v15, /device:TPU:1, one launch (start us, length us, event | category | flops | bytes accessed | tf_op | source)
XLA Modules:
  0.0 71.4 jit_solution(8891352201146163941)
XLA Ops:
  0.6 2.1 %convert_bitcast_fusion.lab_x = bf16[16,128,128]{2,1,0:T(8,128)(2,1)} fusion(s32[1,1,16,128,128]{4,3,2,1,0:T(8,128)} %param.20), kind=kLoop, calls=%fused_computation | loop fusion | flops 262144 | bytes 1572864 | tf_op jit(solution)/shard_map/convert_element_type | solution.py:433
  2.8 65.3 %shard_map.138 = (f32[64,128]{1,0:T(8,128)}, f32[64,128]{1,0:T(8,128)}, f32[16,128]{1,0:T(8,128)}, f32[16,128]{1,0:T(8,128)}) custom-call(bf16[16,128,128]{2,1,0:T(8,128)(2,1)} %convert_bitcast_fusion.lab_x, bf16[16,128,128]{2,1,0:T(8,128)(2,1)} %bitcast.12, s32[64]{0:T(128)} %bitcast.17, s32[64]{0:T(128)} %bitcast.18, s32[16]{0:T(128)} %bitcast.19, ...), custom_call_target="tpu_custom_call" | custom-call | tf_op jit(solution)/shard_map/pallas_call | solution.py:322
  68.0 0.0 copy-start
  68.0 1.4 %copy.19 = f32[64,128]{1,0:T(8,128)} copy(f32[64,128]{1,0:T(8,128)} %get-tuple-element.8) | data formatting | bytes 65536
  69.4 0.0 copy-done
  69.4 0.0 copy-start.2
  69.4 0.6 copy.20
  70.0 0.1 copy-done.2
  70.1 0.0 copy-start.1
  70.1 0.6 copy.21
  70.7 0.1 copy-done.1
  70.8 0.6 copy.22
Async XLA Ops:
  68.0 1.4 %copy-start = (f32[64,128]{1,0:T(8,128)S(1)}, f32[64,128]{1,0:T(8,128)}, u32[]{:S(2)}) copy-start(f32[64,128]{1,0:T(8,128)} %get-tuple-element.9) | copy-start | bytes 98308
  69.4 0.7 copy-start.2
  70.1 0.7 copy-start.1

commit v16 on v15

--- a/solution.py
+++ b/solution.py
@@ -155,7 +155,7 @@
 def gather_kernel(
     tile, item_blocks, obs_slots,
     lab_x, prop_x, uu_x, ui_x, ou_x, oi_x, oc_x, up_ref, uimp_ref, vp_ref, vi_ref,
-    user_pred_out, user_imp_out, item_pred_out, item_imp_out,
+    user_out, item_out,
     lab_land, prop_land, uu_land, ui_land, ou_land, oi_land, oc_land, s_ref, m_ref, d_ref, user_acc, item_acc,
     user_land, item_land, send_sem, recv_sem, local_sem, sum_send, sum_recv, sum_local,
 ):
@@ -301,12 +301,11 @@
     for copies in sums:
         for copy in copies:
             copy.wait()
-    for land, outs in ((user_land, (user_pred_out, user_imp_out)), (item_land, (item_pred_out, item_imp_out))):
+    for land, out in ((user_land, user_out), (item_land, item_out)):
         total = land[0]
         for source in range(1, land.shape[0]):
             total = total + land[source]
-        outs[0][...] = total[0]
-        outs[1][...] = total[1]
+        out[...] = total
 
 
 def exchange_tiles(labels, propens, indices, factors, tile, item_blocks, obs_slots, user_ways):
@@ -321,10 +320,12 @@
     anyspace = pl.BlockSpec(memory_space=pl.ANY)
     return pl.pallas_call(
         functools.partial(gather_kernel, tile, item_blocks, obs_slots),
-        out_shape=[jax.ShapeDtypeStruct((user_rows // n, rank), jnp.float32)] * 2
-        + [jax.ShapeDtypeStruct((shard_rows // user_ways, rank), jnp.float32)] * 2,
+        out_shape=[
+            jax.ShapeDtypeStruct((2, user_rows // n, rank), jnp.float32),
+            jax.ShapeDtypeStruct((2, shard_rows // user_ways, rank), jnp.float32),
+        ],
         in_specs=[anyspace] * 7 + [vmem] * 4,
-        out_specs=[vmem] * 4,
+        out_specs=[vmem] * 2,
         scratch_shapes=[
             pltpu.VMEM((n,) + labels.shape[1:], labels.dtype),
             pltpu.VMEM((n,) + propens.shape[1:], propens.dtype),
@@ -433,12 +434,10 @@
     labels = obs_label.reshape(item_ways, obs_slots * tile, tile).astype(jnp.bfloat16)
     propens = obs_prop.reshape(item_ways, obs_slots * tile, tile)
     indices = [x.reshape(x.shape[-1]) for x in (uno_user, uno_item, obs_user, obs_item, obs_count)]
-    return tuple(
-        exchange_tiles(
-            labels, propens, indices, (user_pred, user_imp, item_pred, item_imp), tile, item_blocks, obs_slots,
-            user_ways,
-        )
+    user_share, item_share = exchange_tiles(
+        labels, propens, indices, (user_pred, user_imp, item_pred, item_imp), tile, item_blocks, obs_slots, user_ways
     )
+    return (user_share[0], user_share[1], item_share[0], item_share[1])
 
 
 def solution(mesh):

time: 71.7 us -> 70.3 us (0.980)
  local copies, waits for them, and re-layouts: 3.39 us -> 2.02 us
    unnamed x10 -> x2, local copies, waits for them, and re-layouts: 3.39 us -> 0.01 us
    squeeze x0 -> x2, local copies, waits for them, and re-layouts: none -> 2.01 us  [shards(): return (user_share[0], user_share[1], item_share[0], item_share[1])]
where the time goes in v16:
time: 70.3 us; the launch traced here: 70.1 us
  Pallas kernels  65.3 us (93%)
  other arithmetic  2.13 us (3%)
  local copies, waits for them, and re-layouts  2.02 us (3%)
    pallas_call x1, Pallas kernels, exchange_tiles(): pl.pallas_call(functools.partial(gather_kernel, tile, item_blocks, obs_sl...  65.3 us
    convert_element_type x1, other arithmetic, shards(): obs_label.reshape(item_ways, obs_slots * tile, tile).astype(jnp.bfloat16)  2.13 us
    squeeze x2, local copies, waits for them, and re-layouts, shards(): return (user_share[0], user_share[1], item_share[0], item_share[1])  2.01 us

profile of v16, /device:TPU:1, one launch (start us, length us, event | category | flops | bytes accessed | tf_op | source)
XLA Modules:
  0.0 70.1 jit_solution(18444075322034262923)
XLA Ops:
  0.6 2.1 %convert_bitcast_fusion.lab_x = bf16[16,128,128]{2,1,0:T(8,128)(2,1)} fusion(s32[1,1,16,128,128]{4,3,2,1,0:T(8,128)} %param.20), kind=kLoop, calls=%fused_computation | loop fusion | flops 262144 | bytes 1572864 | tf_op jit(solution)/shard_map/convert_element_type | solution.py:434
  2.8 65.3 %shard_map.138 = (f32[2,64,128]{2,1,0:T(8,128)}, f32[2,16,128]{2,1,0:T(8,128)}) custom-call(bf16[16,128,128]{2,1,0:T(8,128)(2,1)} %convert_bitcast_fusion.lab_x, bf16[16,128,128]{2,1,0:T(8,128)(2,1)} %bitcast.20, s32[64]{0:T(128)} %bitcast.25, s32[64]{0:T(128)} %bitcast.26, s32[16]{0:T(128)} %bitcast.27, s32[16]{0:T(128)} %bitcast.28, s32[16]{0:T(128)} %bitcast.29, ...), custom_call_target="tpu_custom_call" | custom-call | tf_op jit(solution)/shard_map/pallas_call | solution.py:321
  68.0 0.0 copy-start
  68.1 1.4 %slice_bitcast_fusion = (f32[64,128]{1,0:T(8,128)}, f32[64,128]{1,0:T(8,128)}) fusion(f32[2,64,128]{2,1,0:T(8,128)} %get-tuple-element.6), kind=kLoop, calls=%fused_computation.1 | loop fusion | bytes 131072 | tf_op jit(solution)/shard_map/squeeze | solution.py:440
  69.5 0.0 copy-done
  69.5 0.6 slice_bitcast_fusion.2
Async XLA Ops:
  68.0 1.4 %copy-start = (f32[2,16,128]{2,1,0:T(8,128)S(1)}, f32[2,16,128]{2,1,0:T(8,128)}, u32[]{:S(2)}) copy-start(f32[2,16,128]{2,1,0:T(8,128)} %get-tuple-element.7) | copy-start | bytes 49156

commit v17 on v16

--- a/solution.py
+++ b/solution.py
@@ -157,7 +157,7 @@
     lab_x, prop_x, uu_x, ui_x, ou_x, oi_x, oc_x, up_ref, uimp_ref, vp_ref, vi_ref,
     user_out, item_out,
     lab_land, prop_land, uu_land, ui_land, ou_land, oi_land, oc_land, s_ref, m_ref, d_ref, user_acc, item_acc,
-    user_land, item_land, send_sem, recv_sem, local_sem, sum_send, sum_recv, sum_local,
+    user_land, item_land, lab_wide, lab_narrow, send_sem, recv_sem, local_sem, sum_send, sum_recv, sum_local,
 ):
     n = lax.axis_size("item")
     me = lax.axis_index("item")
@@ -194,13 +194,22 @@
             index_copies.append(send(which, x, land.at[me], k))
     tile_local = []
     tile_copies = [[] for _ in range(n)]
-    for which, (x, land) in enumerate(tile_pairs):
+    staging = pltpu.make_async_copy(lab_x, lab_wide, local_sem.at[len(index_pairs) + len(tile_pairs)])
+    staging.start()
+
+    def send_tiles(which, x, land):
         slot = len(index_pairs) + which
         local = pltpu.make_async_copy(x.at[me], land.at[me], local_sem.at[slot])
         local.start()
         tile_local.append(local)
         for k in range(1, n):
             tile_copies[k].append(send(slot, x.at[lax.rem(me + k, n)], land.at[me], k))
+
+    send_tiles(1, prop_x, prop_land)
+    staging.wait()
+    for row in range(lab_wide.shape[0]):
+        lab_narrow[row] = lab_wide[row].astype(lab_narrow.dtype)
+    send_tiles(0, lab_narrow, lab_land)
 
     dims = (((1,), (1,)), ((), ()))
 
@@ -327,7 +336,7 @@
         in_specs=[anyspace] * 7 + [vmem] * 4,
         out_specs=[vmem] * 2,
         scratch_shapes=[
-            pltpu.VMEM((n,) + labels.shape[1:], labels.dtype),
+            pltpu.VMEM((n,) + labels.shape[1:], jnp.bfloat16),
             pltpu.VMEM((n,) + propens.shape[1:], propens.dtype),
         ]
         + [pltpu.SMEM((n,) + x.shape, x.dtype) for x in indices]
@@ -339,9 +348,11 @@
             pltpu.VMEM((2, shard_rows, rank), jnp.float32),
             pltpu.VMEM((n, 2, user_rows // n, rank), jnp.float32),
             pltpu.VMEM((user_ways, 2, shard_rows // user_ways, rank), jnp.float32),
+            pltpu.VMEM(labels.shape, labels.dtype),
+            pltpu.VMEM(labels.shape, jnp.bfloat16),
             pltpu.SemaphoreType.DMA((7, n - 1)),
             pltpu.SemaphoreType.DMA((7, n - 1)),
-            pltpu.SemaphoreType.DMA((7,)),
+            pltpu.SemaphoreType.DMA((8,)),
             pltpu.SemaphoreType.DMA((2, max(n, user_ways) - 1)),
             pltpu.SemaphoreType.DMA((2, max(n, user_ways) - 1)),
             pltpu.SemaphoreType.DMA((2,)),
@@ -431,7 +442,7 @@
     n_blocks = user_blocks * item_blocks
     obs_slots = obs_user.shape[-1] // item_ways
 
-    labels = obs_label.reshape(item_ways, obs_slots * tile, tile).astype(jnp.bfloat16)
+    labels = obs_label.reshape(item_ways, obs_slots * tile, tile)
     propens = obs_prop.reshape(item_ways, obs_slots * tile, tile)
     indices = [x.reshape(x.shape[-1]) for x in (uno_user, uno_item, obs_user, obs_item, obs_count)]
     user_share, item_share = exchange_tiles(

time: 70.3 us -> 68.3 us (0.972)
  other arithmetic: 2.13 us -> 0 us
    convert_element_type x1 -> x0, other arithmetic: 2.13 us -> none  [shards(): obs_label.reshape(item_ways, obs_slots * tile, tile).astype(jnp.bfloat16)]
where the time goes in v17:
time: 68.3 us; the launch traced here: 68.1 us
  Pallas kernels  65.4 us (96%)
  local copies, waits for them, and re-layouts  2.02 us (3%)
    pallas_call x1, Pallas kernels, exchange_tiles(): pl.pallas_call(functools.partial(gather_kernel, tile, item_blocks, obs_sl...  65.4 us
    squeeze x2, local copies, waits for them, and re-layouts, shards(): return (user_share[0], user_share[1], item_share[0], item_share[1])  2.01 us

profile of v17, /device:TPU:1, one launch (start us, length us, event | category | flops | bytes accessed | tf_op | source)
XLA Modules:
  0.0 68.1 jit_solution(3832636837275975951)
XLA Ops:
  0.6 65.4 %shard_map.138 = (f32[2,64,128]{2,1,0:T(8,128)}, f32[2,16,128]{2,1,0:T(8,128)}) custom-call(s32[16,128,128]{2,1,0:T(8,128)} %bitcast.19, bf16[16,128,128]{2,1,0:T(8,128)(2,1)} %bitcast.20, s32[64]{0:T(128)} %bitcast.25, s32[64]{0:T(128)} %bitcast.26, s32[16]{0:T(128)} %bitcast.27, s32[16]{0:T(128)} %bitcast.28, s32[16]{0:T(128)} %bitcast.29, ...), custom_call_target="tpu_custom_call" | custom-call | tf_op jit(solution)/shard_map/pallas_call | solution.py:330
  66.1 0.0 copy-start
  66.1 1.4 %slice_bitcast_fusion = (f32[64,128]{1,0:T(8,128)}, f32[64,128]{1,0:T(8,128)}) fusion(f32[2,64,128]{2,1,0:T(8,128)} %get-tuple-element.6), kind=kLoop, calls=%fused_computation | loop fusion | bytes 131072 | tf_op jit(solution)/shard_map/squeeze | solution.py:451
  67.5 0.0 copy-done
  67.5 0.6 slice_bitcast_fusion.2
Async XLA Ops:
  66.1 1.4 %copy-start = (f32[2,16,128]{2,1,0:T(8,128)S(1)}, f32[2,16,128]{2,1,0:T(8,128)}, u32[]{:S(2)}) copy-start(f32[2,16,128]{2,1,0:T(8,128)} %get-tuple-element.7) | copy-start | bytes 49156

commit v18 on v17

--- a/solution.py
+++ b/solution.py
@@ -155,7 +155,7 @@
 def gather_kernel(
     tile, item_blocks, obs_slots,
     lab_x, prop_x, uu_x, ui_x, ou_x, oi_x, oc_x, up_ref, uimp_ref, vp_ref, vi_ref,
-    user_out, item_out,
+    shares,
     lab_land, prop_land, uu_land, ui_land, ou_land, oi_land, oc_land, s_ref, m_ref, d_ref, user_acc, item_acc,
     user_land, item_land, lab_wide, lab_narrow, send_sem, recv_sem, local_sem, sum_send, sum_recv, sum_local,
 ):
@@ -310,11 +310,13 @@
     for copies in sums:
         for copy in copies:
             copy.wait()
-    for land, out in ((user_land, user_out), (item_land, item_out)):
+    rows = 0
+    for land in (user_land, item_land):
         total = land[0]
         for source in range(1, land.shape[0]):
             total = total + land[source]
-        out[...] = total
+        shares[:, pl.ds(rows, land.shape[2]), :] = total
+        rows += land.shape[2]
 
 
 def exchange_tiles(labels, propens, indices, factors, tile, item_blocks, obs_slots, user_ways):
@@ -329,12 +331,9 @@
     anyspace = pl.BlockSpec(memory_space=pl.ANY)
     return pl.pallas_call(
         functools.partial(gather_kernel, tile, item_blocks, obs_slots),
-        out_shape=[
-            jax.ShapeDtypeStruct((2, user_rows // n, rank), jnp.float32),
-            jax.ShapeDtypeStruct((2, shard_rows // user_ways, rank), jnp.float32),
-        ],
+        out_shape=jax.ShapeDtypeStruct((2, user_rows // n + shard_rows // user_ways, rank), jnp.float32),
         in_specs=[anyspace] * 7 + [vmem] * 4,
-        out_specs=[vmem] * 2,
+        out_specs=vmem,
         scratch_shapes=[
             pltpu.VMEM((n,) + labels.shape[1:], jnp.bfloat16),
             pltpu.VMEM((n,) + propens.shape[1:], propens.dtype),
@@ -445,10 +444,11 @@
     labels = obs_label.reshape(item_ways, obs_slots * tile, tile)
     propens = obs_prop.reshape(item_ways, obs_slots * tile, tile)
     indices = [x.reshape(x.shape[-1]) for x in (uno_user, uno_item, obs_user, obs_item, obs_count)]
-    user_share, item_share = exchange_tiles(
+    shares = exchange_tiles(
         labels, propens, indices, (user_pred, user_imp, item_pred, item_imp), tile, item_blocks, obs_slots, user_ways
     )
-    return (user_share[0], user_share[1], item_share[0], item_share[1])
+    user_part = user_rows // item_ways
+    return (shares[0, :user_part], shares[1, :user_part], shares[0, user_part:], shares[1, user_part:])
 
 
 def solution(mesh):

time: 68.3 us -> 69 us (1.010)
  local copies, waits for them, and re-layouts: 2.02 us -> 2.72 us
    squeeze x2, local copies, waits for them, and re-layouts: 2.01 us -> 2.72 us  [the longest x1 1.4 us: shards(): shares[1, :user_part]]
where the time goes in v18:
time: 69 us; the launch traced here: 68.8 us
  Pallas kernels  65.4 us (95%)
  local copies, waits for them, and re-layouts  2.72 us (4%)
    pallas_call x1, Pallas kernels, exchange_tiles(): pl.pallas_call(functools.partial(gather_kernel, tile, item_blocks, obs_sl...  65.4 us
    squeeze x1, local copies, waits for them, and re-layouts, shards(): shares[1, :user_part]  1.4 us

profile of v18, /device:TPU:1, one launch (start us, length us, event | category | flops | bytes accessed | tf_op | source)
XLA Modules:
  0.0 68.8 jit_solution(17614704245025239427)
XLA Ops:
  0.6 65.4 %shard_map.138 = f32[2,80,128]{2,1,0:T(8,128)} custom-call(s32[16,128,128]{2,1,0:T(8,128)} %bitcast.19, bf16[16,128,128]{2,1,0:T(8,128)(2,1)} %bitcast.20, s32[64]{0:T(128)} %bitcast.25, s32[64]{0:T(128)} %bitcast.26, s32[16]{0:T(128)} %bitcast.27, s32[16]{0:T(128)} %bitcast.28, s32[16]{0:T(128)} %bitcast.29, bf16[8,128,128]{2,1,0:T(8,128)(2,1)} %bitcast.21, ...), custom_call_target="tpu_custom_call" | custom-call | tf_op jit(solution)/shard_map/pallas_call | solution.py:332
  66.1 1.4 %slice_bitcast_fusion = (f32[64,128]{1,0:T(8,128)}, f32[64,128]{1,0:T(8,128)}) fusion(f32[2,80,128]{2,1,0:T(8,128)} %shard_map.138), kind=kLoop, calls=%fused_computation | loop fusion | bytes 131072 | tf_op jit(solution)/shard_map/squeeze | solution.py:451
  67.5 1.3 %slice_bitcast_fusion.2 = (f32[16,128]{1,0:T(8,128)}, f32[16,128]{1,0:T(8,128)}) fusion(f32[2,80,128]{2,1,0:T(8,128)} %shard_map.138), kind=kLoop, calls=%fused_computation.2 | loop fusion | bytes 32768 | tf_op jit(solution)/shard_map/squeeze | solution.py:451

commit v19 on v17

--- a/solution.py
+++ b/solution.py
@@ -185,6 +185,20 @@
         copy.start()
         return copy
 
+    tile_local = []
+    tile_copies = [[] for _ in range(n)]
+    staging = pltpu.make_async_copy(lab_x, lab_wide, local_sem.at[len(index_pairs) + len(tile_pairs)])
+    staging.start()
+
+    def send_tiles(which, x, land):
+        slot = len(index_pairs) + which
+        local = pltpu.make_async_copy(x.at[me], land.at[me], local_sem.at[slot])
+        local.start()
+        tile_local.append(local)
+        for k in range(1, n):
+            tile_copies[k].append(send(slot, x.at[lax.rem(me + k, n)], land.at[me], k))
+
+    send_tiles(1, prop_x, prop_land)
     index_copies = []
     for which, (x, land) in enumerate(index_pairs):
         local = pltpu.make_async_copy(x, land.at[me], local_sem.at[which])
@@ -192,20 +206,6 @@
         index_copies.append(local)
         for k in range(1, n):
             index_copies.append(send(which, x, land.at[me], k))
-    tile_local = []
-    tile_copies = [[] for _ in range(n)]
-    staging = pltpu.make_async_copy(lab_x, lab_wide, local_sem.at[len(index_pairs) + len(tile_pairs)])
-    staging.start()
-
-    def send_tiles(which, x, land):
-        slot = len(index_pairs) + which
-        local = pltpu.make_async_copy(x.at[me], land.at[me], local_sem.at[slot])
-        local.start()
-        tile_local.append(local)
-        for k in range(1, n):
-            tile_copies[k].append(send(slot, x.at[lax.rem(me + k, n)], land.at[me], k))
-
-    send_tiles(1, prop_x, prop_land)
     staging.wait()
     for row in range(lab_wide.shape[0]):
         lab_narrow[row] = lab_wide[row].astype(lab_narrow.dtype)

time: 68.3 us -> 68 us (level)
  no operation moved by 1% of the time
where the time goes in v19:
time: 68 us; the launch traced here: 67.6 us
  Pallas kernels  65 us (96%)
  local copies, waits for them, and re-layouts  2.02 us (3%)
    pallas_call x1, Pallas kernels, exchange_tiles(): pl.pallas_call(functools.partial(gather_kernel, tile, item_blocks, obs_sl...  65 us
    squeeze x2, local copies, waits for them, and re-layouts, shards(): return (user_share[0], user_share[1], item_share[0], item_share[1])  2.01 us

profile of v19, /device:TPU:1, one launch (start us, length us, event | category | flops | bytes accessed | tf_op | source)
XLA Modules:
  0.0 67.6 jit_solution(14911312995749444819)
XLA Ops:
  0.6 65.0 %shard_map.138 = (f32[2,64,128]{2,1,0:T(8,128)}, f32[2,16,128]{2,1,0:T(8,128)}) custom-call(s32[16,128,128]{2,1,0:T(8,128)} %bitcast.19, bf16[16,128,128]{2,1,0:T(8,128)(2,1)} %bitcast.20, s32[64]{0:T(128)} %bitcast.25, s32[64]{0:T(128)} %bitcast.26, s32[16]{0:T(128)} %bitcast.27, s32[16]{0:T(128)} %bitcast.28, s32[16]{0:T(128)} %bitcast.29, ...), custom_call_target="tpu_custom_call" | custom-call | tf_op jit(solution)/shard_map/pallas_call | solution.py:330
  65.6 0.0 copy-start
  65.6 1.4 %slice_bitcast_fusion = (f32[64,128]{1,0:T(8,128)}, f32[64,128]{1,0:T(8,128)}) fusion(f32[2,64,128]{2,1,0:T(8,128)} %get-tuple-element.6), kind=kLoop, calls=%fused_computation | loop fusion | bytes 131072 | tf_op jit(solution)/shard_map/squeeze | solution.py:451
  67.0 0.0 copy-done
  67.0 0.6 slice_bitcast_fusion.2
Async XLA Ops:
  65.6 1.4 %copy-start = (f32[2,16,128]{2,1,0:T(8,128)S(1)}, f32[2,16,128]{2,1,0:T(8,128)}, u32[]{:S(2)}) copy-start(f32[2,16,128]{2,1,0:T(8,128)} %get-tuple-element.7) | copy-start | bytes 49156

commit v20 on v19

--- a/solution.py
+++ b/solution.py
@@ -282,7 +282,9 @@
     for copy in tile_local:
         copy.wait()
     origin_tiles(me)
-    for k in range(1, n):
+    order = [k for pair in zip(range(1, n), range(n - 1, 0, -1)) for k in pair]
+    order = list(dict.fromkeys(order))
+    for k in order:
         for copy in tile_copies[k]:
             copy.wait()
         origin_tiles(lax.rem(me + n - k, n))

time: 68 us -> 70.3 us (1.034)
  the two profiles are of different devices: /device:TPU:1 before, /device:TPU:0 now
where the time goes in v20:
time: 70.3 us; the launch traced here: 70.1 us
  Pallas kernels  67.4 us (96%)
  local copies, waits for them, and re-layouts  2.02 us (3%)
    pallas_call x1, Pallas kernels, exchange_tiles(): pl.pallas_call(functools.partial(gather_kernel, tile, item_blocks, obs_sl...  67.4 us
    squeeze x2, local copies, waits for them, and re-layouts, shards(): return (user_share[0], user_share[1], item_share[0], item_share[1])  2.01 us

profile of v20, /device:TPU:0, one launch (start us, length us, event | category | flops | bytes accessed | tf_op | source)
XLA Modules:
  0.0 70.1 jit_solution(11424924253323008318)
XLA Ops:
  0.6 67.4 %shard_map.138 = (f32[2,64,128]{2,1,0:T(8,128)}, f32[2,16,128]{2,1,0:T(8,128)}) custom-call(s32[16,128,128]{2,1,0:T(8,128)} %bitcast.19, bf16[16,128,128]{2,1,0:T(8,128)(2,1)} %bitcast.20, s32[64]{0:T(128)} %bitcast.25, s32[64]{0:T(128)} %bitcast.26, s32[16]{0:T(128)} %bitcast.27, s32[16]{0:T(128)} %bitcast.28, s32[16]{0:T(128)} %bitcast.29, ...), custom_call_target="tpu_custom_call" | custom-call | tf_op jit(solution)/shard_map/pallas_call | solution.py:332
  68.1 0.0 copy-start
  68.1 1.4 %slice_bitcast_fusion = (f32[64,128]{1,0:T(8,128)}, f32[64,128]{1,0:T(8,128)}) fusion(f32[2,64,128]{2,1,0:T(8,128)} %get-tuple-element.6), kind=kLoop, calls=%fused_computation | loop fusion | bytes 131072 | tf_op jit(solution)/shard_map/squeeze | solution.py:453
  69.5 0.0 copy-done
  69.5 0.6 slice_bitcast_fusion.2
Async XLA Ops:
  68.1 1.4 %copy-start = (f32[2,16,128]{2,1,0:T(8,128)S(1)}, f32[2,16,128]{2,1,0:T(8,128)}, u32[]{:S(2)}) copy-start(f32[2,16,128]{2,1,0:T(8,128)} %get-tuple-element.7) | copy-start | bytes 49156
